TPU v7x, 256 devices: a whole 4x4x8 slice. The times are simulated.
256 devices in a mesh: blk: 4 (over x_hi, core), rows: 64 (over x_lo, y, z).
Axes of the slice: x: 4 (x_hi: 2, x_lo: 2; x = x_hi * 2 + x_lo), y: 4, z: 8, core: 2. Of those that a mesh axis runs over, the one named last changes fastest.
Arguments:
- fock_band: bfloat16 [65536, 2176], P('rows'), may hold values from -0.125 to 0.125
- fock_slot_mask: int32 [512, 17], P('rows'), may hold values from 0 to 1, as said below
- orbital_slab: bfloat16 [65536, 2048], P('rows', 'blk'), may hold values from -16 to 16
- orbital_mask: int32 [512, 16], P('rows', 'blk'), may hold values 0 or 1
- result_mask: int32 [512, 16], P('rows', 'blk'), may hold values 0 or 1
Outputs:
- product_slab: bfloat16 [65536, 2048], P('rows', 'blk')
- projected: float32 [2048, 2048], P('rows', 'blk')
Inputs may be any that keep to these rules, and one draw needn't show every extreme that they name: `fock_slot_mask`: 1 marks a present block slot.
All inputs are finite; a program needn't handle non-finite values. No bound on the sum of `orbital_mask` or of `result_mask` on one device may be relied on, other than what follows from the above.
Results may differ from a plain program's by a relative error of at most 0.0029.
Values may be sent and summed in bfloat16 or wider, within the bound.
No kernel may reach another device: no remote copies, remote signals or barrier semaphores. Data moves between devices by JAX's collectives and lax.ppermute only.
A program may use at most 64 MiB of HBM per device.

v0:
```python
import math

import jax
import jax.numpy as jnp
from jax import lax
from jax.sharding import PartitionSpec as P


def with_halo(block, sides, width):
    for axis, dim in sides:
        count = lax.axis_size(axis)
        forward = [(i, i + 1) for i in range(count - 1)]
        forward.append((count - 1, 0))
        backward = [(target, source) for source, target in forward]
        low = lax.ppermute(
            lax.slice_in_dim(block, block.shape[dim] - width, None, axis=dim), axis, forward
        )
        high = lax.ppermute(lax.slice_in_dim(block, 0, width, axis=dim), axis, backward)
        block = jnp.concatenate([low, block, high], axis=dim)
    return block


def on_device(fock_band, fock_slot_mask, orbital_slab, orbital_mask, result_mask):
    local_blocks = fock_slot_mask.shape[0]
    band_extent = fock_slot_mask.shape[1]
    radius = (band_extent - 1) // 2
    block_size = fock_band.shape[0] // local_blocks
    columns = orbital_slab.shape[1]
    col_blocks = orbital_mask.shape[1]
    fock_block_list = fock_band.reshape(
        local_blocks, block_size, band_extent, block_size
    ) * fock_slot_mask[:, None, :, None].astype(jnp.bfloat16)
    slab_rows = (
        orbital_slab.reshape(local_blocks, block_size, col_blocks, block_size)
        * orbital_mask[:, None, :, None].astype(jnp.bfloat16)
    ).reshape(local_blocks * block_size, columns)
    extended = with_halo(slab_rows, (("rows", 0),), radius * block_size)
    extended = extended.reshape(local_blocks + 2 * radius, block_size, columns)

    def add_offset(band_shift, summed_total):
        band_window = lax.dynamic_slice_in_dim(extended, band_shift, local_blocks, 0)
        fock_block_piece = lax.dynamic_index_in_dim(fock_block_list, band_shift, 2, keepdims=False)
        return summed_total + jnp.einsum(
            "wnq,wqg->wng", fock_block_piece, band_window, preferred_element_type=jnp.float32
        )

    summed_total = lax.fori_loop(
        0, band_extent, add_offset, jnp.zeros((local_blocks, block_size, columns), jnp.float32)
    )
    product_slab = (
        (
            summed_total.reshape(local_blocks, block_size, col_blocks, block_size)
            * result_mask[:, None, :, None].astype(jnp.float32)
        )
        .reshape(local_blocks * block_size, columns)
        .astype(jnp.bfloat16)
    )
    groups = lax.axis_size("rows")
    factor = 1.0 / math.sqrt(local_blocks * block_size * groups)
    gathered = lax.all_gather(slab_rows, "blk", axis=1, tiled=True)
    projected = lax.psum_scatter(
        jnp.einsum("rc,rd->cd", gathered, product_slab, preferred_element_type=jnp.float32)
        * factor,
        "rows",
        scatter_dimension=0,
        tiled=True,
    )
    return (product_slab, projected)


def solution(mesh):
    placed = (
        P("rows", None),
        P("rows", None),
        P("rows", "blk"),
        P("rows", "blk"),
        P("rows", "blk"),
    )
    return jax.shard_map(
        on_device,
        mesh=mesh,
        in_specs=placed,
        out_specs=(P("rows", "blk"), P("rows", "blk")),
        check_vma=False,
    )
```

profile of v0, /device:TPU:4, one launch (start us, length us, event | category | flops | bytes accessed | tf_op | source)
XLA Modules:
  0.0 434.9 jit_solution(14791575717867508314)
XLA Ops:
  8.3 1.4 bitcast_multiply_fusion.1
  9.7 2.0 collective-permute-start
  11.7 7.1 %collective-permute-start.1 = (bf16[1024,512]{1,0:T(8,128)(2,1)S(1)}, bf16[1024,512]{1,0:T(8,128)(2,1)}, u32[]{:S(2)}, u32[]{:S(2)}) collective-permute-start(bf16[1024,512]{1,0:T(8,128)(2,1)S(1)} %bitcast_multiply_fusion.1), channel_id=1, source_target_pairs={{1,0},{2,1},{3,2},{4,3},{5,4},{6,5},{7,6},{8,7},{9,8},{10,9},{11,1... | collective-permute-start | bytes 3145736 | tf_op jit(solution)/shard_map/ppermute | solution.py:18
  18.9 6.5 %copy.10 = bf16[1024,2176]{0,1:T(8,128)(2,1)} copy(bf16[1024,2176]{1,0:T(8,128)(2,1)} %param.7) | data formatting | bytes 8912896 | tf_op args[0]
  25.4 5.8 %copy.16 = bf16[272,8,8,128]{3,2,1,0:T(8,128)(2,1)} copy(bf16[272,8,8,128]{3,1,2,0:T(8,128)(2,1)} %bitcast.27) | data formatting | bytes 8912896
  31.4 4.7 %broadcast_multiply_fusion = bf16[8,128,17,128]{1,0,3,2:T(8,128)(2,1)} fusion(bf16[8,128,17,128]{1,0,3,2:T(8,128)(2,1)} %bitcast.26, bf16[8,17]{0,1:T(8,128)(2,1)S(1)} %copy.11), kind=kLoop, calls=%fused_computation.7 | loop fusion | flops 2228224 | bytes 8913168 | tf_op jit(solution)/shard_map/mul | solution.py:30
  36.2 5.9 %collective-permute-done = bf16[1024,512]{1,0:T(8,128)(2,1)} collective-permute-done((bf16[1024,512]{1,0:T(8,128)(2,1)S(1)}, bf16[1024,512]{1,0:T(8,128)(2,1)}, u32[]{:S(2)}, u32[]{:S(2)}) %collective-permute-start) | collective-permute-done | bytes 1048608 | tf_op jit(solution)/shard_map/ppermute | solution.py:15
  42.1 3.0 pad_maximum_fusion
  45.1 54.9 %while.14 = (s32[]{:T(128)}, f32[8,128,512]{2,1,0:T(8,128)S(1)}, bf16[8,128,17,128]{1,0,3,2:T(8,128)(2,1)}, bf16[24,128,512]{2,1,0:T(8,128)(2,1)}, s32[]{:T(128)}, /*index=5*/s32[]{:T(128)}) while((s32[]{:T(128)}, f32[8,128,512]{2,1,0:T(8,128)S(1)}, bf16[8,128,17,128]{1,0,3,2:T(8,128)(2,1)}, bf16[24,128,512]{2,1,0:T(8,128)(2,1)}, ...), condition=%wide.region_1.2_spmd.clone, body=%wide.region_0.1_spmd.clone.sunk | while | flops 135266304 | bytes 6554195 | solution.py:47
  46.3 2.0 select_add_fusion.2
  48.3 1.0 constant_dynamic-slice_fusion.2
  49.5 2.0 select_add_fusion.2
  51.5 1.0 constant_dynamic-slice_fusion.2
  52.7 2.0 select_add_fusion.2
  54.8 1.0 constant_dynamic-slice_fusion.2
  56.0 2.0 select_add_fusion.2
  58.0 1.0 constant_dynamic-slice_fusion.2
  59.2 2.0 select_add_fusion.2
  62.4 2.0 select_add_fusion.2
  65.7 2.0 select_add_fusion.2
  68.9 2.0 select_add_fusion.2
  72.1 2.0 select_add_fusion.2
  75.3 2.0 select_add_fusion.2
  78.6 2.0 select_add_fusion.2
  81.8 2.0 select_add_fusion.2
  85.0 2.0 select_add_fusion.2
  88.3 2.0 select_add_fusion.2
  91.5 2.0 select_add_fusion.2
  94.7 2.0 select_add_fusion.2
  98.0 2.0 select_add_fusion.2
  100.9 6.9 %convolution_multiply_fusion = f32[2048,512]{1,0:T(8,128)} fusion(bf16[1024,2048]{1,0:T(8,128)(2,1)} %all-gather.2.cloned.1.call-done, bf16[1024,512]{1,0:T(8,128)(2,1)S(1)} %fusion.3), kind=kOutput, calls=%fused_computation.5 | convolution fusion | flops 2148532224 | bytes 9437184 | tf_op jit(solution)/shard_map/rc,rd->cd/dot_general | solution.py:62
  107.8 320.3 %reduce-scatter.2.cloned.1.call-done = f32[32,512]{1,0:T(8,128)} async-done(((f32[2048,512]{1,0:T(8,128)}), f32[32,512]{1,0:T(8,128)}) %reduce-scatter.2.cloned.1.call-update) | async-done | bytes 65552 | tf_op jit(solution)/shard_map/reduce_scatter | solution.py:61
  (56 shorter events, 18.8 us)
Async XLA Ops:
  7.2 93.7 %all-gather.2.cloned.1.call-start = ((), (), s32[]{:S(2)}) async-start(), calls=%async_computation.1 | async-start | bytes 5242880 | tf_op jit(solution)/shard_map/all_gather | solution.py:60
  9.7 9.1 %copy-start = (bf16[1024,512]{1,0:T(8,128)(2,1)}, bf16[1024,512]{1,0:T(8,128)(2,1)S(1)}, u32[]{:S(2)}) copy-start(bf16[1024,512]{1,0:T(8,128)(2,1)S(1)} %bitcast_multiply_fusion.1) | copy-start | bytes 3145732
  9.7 32.4 %collective-permute-start = (bf16[1024,512]{1,0:T(8,128)(2,1)S(1)}, bf16[1024,512]{1,0:T(8,128)(2,1)}, u32[]{:S(2)}, u32[]{:S(2)}) collective-permute-start(bf16[1024,512]{1,0:T(8,128)(2,1)S(1)} %bitcast_multiply_fusion.1), channel_id=1, source_target_pairs={{0,1},{1,2},{2,3},{3,4},{4,5},{5,6},{6,7},{7,8},{8,9},{9,10},{10,1... | collective-permute-start | bytes 3145736 | tf_op jit(solution)/shard_map/ppermute | solution.py:15
  11.7 30.4 %collective-permute-start.1 = (bf16[1024,512]{1,0:T(8,128)(2,1)S(1)}, bf16[1024,512]{1,0:T(8,128)(2,1)}, u32[]{:S(2)}, u32[]{:S(2)}) collective-permute-start(bf16[1024,512]{1,0:T(8,128)(2,1)S(1)} %bitcast_multiply_fusion.1), channel_id=1, source_target_pairs={{1,0},{2,1},{3,2},{4,3},{5,4},{6,5},{7,6},{8,7},{9,8},{10,9},{11,1... | collective-permute-start | bytes 3145736 | tf_op jit(solution)/shard_map/ppermute | solution.py:18
  18.9 409.2 %reduce-scatter.2.cloned.1.call-start = ((), (), s32[]{:S(2)}) async-start(), calls=%async_computation.2 | async-start | bytes 4259840 | tf_op jit(solution)/shard_map/reduce_scatter | solution.py:61
  25.4 5.8 %copy-start.3 = (s32[8,17]{1,0:T(8,128)S(1)}, s32[8,17]{1,0:T(8,128)}, u32[]{:S(2)}) copy-start(s32[8,17]{1,0:T(8,128)} %param.8) | copy-start | bytes 1636
  25.4 5.9 %copy-start.4 = (s32[8,4]{0,1:T(4,128)S(1)}, s32[8,4]{0,1:T(4,128)}, u32[]{:S(2)}) copy-start(s32[8,4]{0,1:T(4,128)} %param.11) | copy-start | bytes 388
  31.4 10.7 %copy-start.1 = (bf16[1024,512]{1,0:T(8,128)(2,1)S(1)}, bf16[1024,512]{1,0:T(8,128)(2,1)}, u32[]{:S(2)}) copy-start(bf16[1024,512]{1,0:T(8,128)(2,1)} %copy-done) | copy-start | bytes 3145732
  100.8 6.9 %copy-start.2 = (bf16[1024,512]{1,0:T(8,128)(2,1)}, bf16[1024,512]{1,0:T(8,128)(2,1)S(1)}, u32[]{:S(2)}) copy-start(bf16[1024,512]{1,0:T(8,128)(2,1)S(1)} %fusion.3) | copy-start | bytes 3145732
Sparse Core Ops, SparseCore 0:
  19.0 35.5 all-gather.1
  107.9 320.1 reduce-scatter.1
where the time goes:
time: 436 us; the launch traced here: 435 us
  waiting for transfers between devices  326 us (75%)
  matrix products  40.8 us (9%)
  local copies, waits for them, and re-layouts  33.7 us (8%)
  between operations  14.1 us (3%)
  other arithmetic  10.3 us (2%)
  starting transfers between devices  9.19 us (2%)
    reduce_scatter x1, waiting for transfers between devices, on_device(): lax.psum_scatter(jnp.einsum('rc,rd->cd', gathered, product_slab, preferre...  320 us
    dot_general x17, matrix products, add_offset(): jnp.einsum('wnq,wqg->wng', fock_block_piece, band_window, preferred_eleme...  33.9 us
    dynamic_slice x34, local copies, waits for them, and re-layouts, add_offset(): lax.dynamic_index_in_dim(fock_block_list, band_shift, 2, keepdims=False)  20.4 us
    unnamed x12, local copies, waits for them, and re-layouts  12.3 us
  transfers between devices with their start and end apart: 4, of which 2 were waited for; matrix products, arithmetic and copies ran while one was open for 17% of the time, Pallas kernels for 0%

commit v1 on v0

v1 whole, which is shorter than its diff:
```python
import functools
import math

import jax
import jax.numpy as jnp
from jax import lax
from jax.experimental import pallas as pl
from jax.experimental.pallas import tpu as pltpu
from jax.sharding import Mesh, PartitionSpec as P

F32, BF16 = jnp.float32, jnp.bfloat16
ROWS = ("xl", "y", "z")
BLK = ("xh", "core")
VMEM = pl.BlockSpec(memory_space=pltpu.VMEM)
SMEM = pl.BlockSpec(memory_space=pltpu.SMEM)
MIB = 1 << 20


def call(body, outs, ins, scratch=(), limit=24 * MIB, flops=0, moved=0):
    return pl.pallas_call(
        body,
        out_shape=outs,
        in_specs=ins,
        out_specs=jax.tree.map(lambda _: VMEM, outs),
        scratch_shapes=list(scratch),
        compiler_params=pltpu.CompilerParams(vmem_limit_bytes=limit),
        cost_estimate=pl.CostEstimate(flops=flops, bytes_accessed=moved, transcendentals=0),
    )


def mask_kernel(size, mask_ref, slab_ref, out_ref):
    blocks, panels = mask_ref.shape
    for i in range(blocks):
        for j in range(panels):
            at = (pl.ds(i * size, size), pl.ds(j * size, size))
            tile = slab_ref[at]
            out_ref[at] = jnp.where(mask_ref[i, j] != 0, tile, jnp.zeros_like(tile))


def product_kernel(size, fmask_ref, rmask_ref, fock_ref, low_ref, mid_ref, high_ref, out_ref, outt_ref, held):
    blocks, slots = fmask_ref.shape
    panels = rmask_ref.shape[1]
    for i in range(blocks):
        rows = pl.ds(i * size, size)
        for o in range(slots):
            tile = fock_ref[rows, pl.ds(o * size, size)]
            held[i % 2, :, pl.ds(o * size, size)] = jnp.where(
                fmask_ref[i, o] != 0, tile, jnp.zeros_like(tile)
            )
        first, last = (blocks - i) * size, (2 * blocks - i) * size
        fock = held.at[i % 2]
        total = jnp.dot(fock[:, first:last], mid_ref[...], preferred_element_type=F32)
        total += jnp.dot(fock[:, :first], low_ref[i * size :, :], preferred_element_type=F32)
        total += jnp.dot(
            fock[:, last:], high_ref[: (i + 1) * size, :], preferred_element_type=F32
        )
        for j in range(panels):
            cols = slice(j * size, (j + 1) * size)
            tile = total[:, cols]
            tile = jnp.where(rmask_ref[i, j] != 0, tile, jnp.zeros_like(tile)).astype(BF16)
            out_ref[rows, cols] = tile
            outt_ref[cols, rows] = tile.T


def project_kernel(panel_ref, prodt_ref, own_ref, core_ref, far_ref, both_ref, out_ref):
    half = out_ref.shape[2]
    for q, ref in enumerate((own_ref, core_ref, far_ref, both_ref)):
        terms = jnp.dot(prodt_ref[...], ref[...], preferred_element_type=F32).astype(BF16)
        where = (panel_ref[0] ^ q) * 2
        out_ref[where] = terms[:, :half]
        out_ref[where + 1] = terms[:, half:]


def first_sum_kernel(in_ref, out_ref):
    total = in_ref[0].astype(F32)
    for s in range(1, in_ref.shape[0]):
        total += in_ref[s].astype(F32)
    out_ref[...] = total.T.astype(BF16)


def last_sum_kernel(factor, in_ref, out_ref):
    total = in_ref[0].astype(F32)
    for s in range(1, in_ref.shape[0]):
        total += in_ref[s].astype(F32)
    out_ref[...] = total * factor


def ring(count, step):
    return [(i, (i + step) % count) for i in range(count)]


def on_device(fock_band, fock_slot_mask, orbital_slab, orbital_mask, result_mask):
    blocks, slots = fock_slot_mask.shape
    rows, columns = orbital_slab.shape
    size = rows // blocks
    like = functools.partial(jax.ShapeDtypeStruct)
    slab = call(functools.partial(mask_kernel, size), like((rows, columns), BF16), [SMEM, VMEM])(
        orbital_mask, orbital_slab
    )
    groups = lax.axis_size(ROWS)
    low = lax.ppermute(slab, ROWS, ring(groups, 1))
    high = lax.ppermute(slab, ROWS, ring(groups, groups - 1))
    far = lax.ppermute(slab, "xh", ring(2, 1))
    near = lax.ppermute(slab, "core", ring(2, 1))
    both = lax.ppermute(far, "core", ring(2, 1))
    product, flipped = call(
        functools.partial(product_kernel, size),
        (like((rows, columns), BF16), like((columns, rows), BF16)),
        [SMEM, SMEM, VMEM, VMEM, VMEM, VMEM],
        [pltpu.VMEM((2, size, slots * size), BF16)],
        flops=2 * rows * slots * size * columns,
        moved=2 * rows * (slots * size + 5 * columns),
    )(fock_slot_mask, result_mask, fock_band, low, slab, high)
    panel = (lax.axis_index("xh") * 2 + lax.axis_index("core")).reshape(1)
    outer = lax.axis_size("xl") * lax.axis_size("y")
    inner = lax.axis_size("z")
    chunk = columns * 4 // outer
    terms = call(
        project_kernel,
        like((outer, columns, chunk), BF16),
        [SMEM, VMEM, VMEM, VMEM, VMEM, VMEM],
        flops=8 * rows * columns * columns,
        moved=2 * 9 * rows * columns,
    )(panel, flipped, slab, near, far, both)
    terms = lax.all_to_all(terms, ("xl", "y"), 0, 0, tiled=True)
    part = call(first_sum_kernel, like((chunk, columns), BF16), [VMEM])(terms)
    part = part.reshape(inner, chunk // inner, columns)
    part = lax.all_to_all(part, "z", 0, 0, tiled=True)
    factor = 1.0 / math.sqrt(rows * groups)
    projected = call(
        functools.partial(last_sum_kernel, factor),
        like((chunk // inner, columns), F32),
        [VMEM],
    )(part)
    return (product, projected)


def solution(mesh):
    split = Mesh(mesh.devices.reshape(2, 2, 2, 4, 8), BLK + ROWS)
    placed = (P(ROWS, None), P(ROWS, None), P(ROWS, BLK), P(ROWS, BLK), P(ROWS, BLK))
    return jax.shard_map(
        on_device,
        mesh=split,
        in_specs=placed,
        out_specs=(P(ROWS, BLK), P(ROWS, BLK)),
        check_vma=False,
    )
```

time: 436 us -> 114 us (0.26)
  the two profiles are of different devices: /device:TPU:4 before, /device:TPU:10 now
where the time goes in v1:
time: 114 us; the launch traced here: 113 us
  blocking collectives  65.8 us (58%)
  waiting for transfers between devices  22.9 us (20%)
  Pallas kernels  11.4 us (10%)
  starting transfers between devices  7.96 us (7%)
  local copies, waits for them, and re-layouts  4.34 us (4%)
    all_to_all x1, blocking collectives, on_device(): terms = lax.all_to_all(terms, ('xl', 'y'), 0, 0, tiled=True)  49.1 us
    ppermute x1, waiting for transfers between devices, on_device(): far = lax.ppermute(slab, 'xh', ring(2, 1))  18.5 us
    all_to_all x1, blocking collectives, on_device(): part = lax.all_to_all(part, 'z', 0, 0, tiled=True)  16.7 us
    pallas_call x1, Pallas kernels, on_device(): call(functools.partial(product_kernel, size), (like((rows, columns), BF16...  5.95 us
    ppermute x1, waiting for transfers between devices, on_device(): low = lax.ppermute(slab, ROWS, ring(groups, 1))  4.36 us
    unnamed x10, local copies, waits for them, and re-layouts  4.34 us
    ppermute x1, starting transfers between devices, on_device(): high = lax.ppermute(slab, ROWS, ring(groups, groups - 1))  3.83 us
    pallas_call x1, Pallas kernels, on_device(): call(project_kernel, like((outer, columns, chunk), BF16), [SMEM, VMEM, VM...  3.58 us
  transfers between devices with their start and end apart: 5, of which 2 were waited for; matrix products, arithmetic and copies ran while one was open for 0% of the time, Pallas kernels for 5%

profile of v1, /device:TPU:10, one launch (start us, length us, event | category | flops | bytes accessed | tf_op | source)
XLA Modules:
  0.0 113.1 jit_solution(18172013686219748669)
XLA Ops:
  0.6 0.0 copy-start.3
  0.6 0.0 copy-start.2
  0.7 0.8 copy.7.mask_ref
  1.4 0.0 copy-start
  1.4 1.2 %copy-done = bf16[1024,512]{1,0:T(8,128)(2,1)S(1)} copy-done((bf16[1024,512]{1,0:T(8,128)(2,1)S(1)}, bf16[1024,512]{1,0:T(8,128)(2,1)}, u32[]{:S(2)}) %copy-start) | copy-done | bytes 1048600
  2.6 0.8 shard_map.68.mid_ref.own_ref
  3.5 2.2 %collective-permute-start.3 = (bf16[1024,512]{1,0:T(8,128)(2,1)S(1)}, bf16[1024,512]{1,0:T(8,128)(2,1)S(1)}, u32[]{:S(2)}, u32[]{:S(2)}) collective-permute-start(bf16[1024,512]{1,0:T(8,128)(2,1)S(1)} %shard_map.68.mid_ref.own_ref), channel_id=1, source_target_pairs={{0,128},{128,0},{1,129},{129,1},{2,130},{130,2},{3,131},{131,3},{4... | collective-permute-start | bytes 3145736 | tf_op jit(solution)/shard_map/ppermute | solution.py:103
  5.7 1.9 %collective-permute-start = (bf16[1024,512]{1,0:T(8,128)(2,1)S(1)}, bf16[1024,512]{1,0:T(8,128)(2,1)}, u32[]{:S(2)}, u32[]{:S(2)}) collective-permute-start(bf16[1024,512]{1,0:T(8,128)(2,1)S(1)} %shard_map.68.mid_ref.own_ref), channel_id=1, source_target_pairs={{0,1},{1,2},{2,3},{3,4},{4,5},{5,6},{6,7},{7,8},{8,9},{9,10},{10,1... | collective-permute-start | bytes 3145736 | tf_op jit(solution)/shard_map/ppermute | solution.py:101
  7.6 3.8 %collective-permute-start.1 = (bf16[1024,512]{1,0:T(8,128)(2,1)S(1)}, bf16[1024,512]{1,0:T(8,128)(2,1)}, u32[]{:S(2)}, u32[]{:S(2)}) collective-permute-start(bf16[1024,512]{1,0:T(8,128)(2,1)S(1)} %shard_map.68.mid_ref.own_ref), channel_id=1, source_target_pairs={{0,63},{1,0},{2,1},{3,2},{4,3},{5,4},{6,5},{7,6},{8,7},{9,8},{10,9... | collective-permute-start | bytes 3145736 | tf_op jit(solution)/shard_map/ppermute | solution.py:102
  11.4 0.0 collective-permute-start.2
  11.5 18.5 %collective-permute-done.3.far_ref = bf16[1024,512]{1,0:T(8,128)(2,1)S(1)} collective-permute-done((bf16[1024,512]{1,0:T(8,128)(2,1)S(1)}, bf16[1024,512]{1,0:T(8,128)(2,1)S(1)}, u32[]{:S(2)}, u32[]{:S(2)}) %collective-permute-start.3) | collective-permute-done | bytes 1048608 | tf_op jit(solution)/shard_map/ppermute | solution.py:103
  30.0 0.0 collective-permute-start.4
  30.0 0.0 copy-done.3
  30.0 0.1 copy.8.rmask_ref
  30.1 4.4 %collective-permute-done.low_ref = bf16[1024,512]{1,0:T(8,128)(2,1)} collective-permute-done((bf16[1024,512]{1,0:T(8,128)(2,1)S(1)}, bf16[1024,512]{1,0:T(8,128)(2,1)}, u32[]{:S(2)}, u32[]{:S(2)}) %collective-permute-start) | collective-permute-done | bytes 1048608 | tf_op jit(solution)/shard_map/ppermute | solution.py:101
  34.4 0.0 collective-permute-done.1.high_ref
  34.4 0.0 copy-done.2
  34.4 0.0 copy-start.1
  34.4 2.3 %copy-done.1 = bf16[1024,2176]{1,0:T(8,128)(2,1)S(1)} copy-done((bf16[1024,2176]{1,0:T(8,128)(2,1)S(1)}, bf16[1024,2176]{1,0:T(8,128)(2,1)}, u32[]{:S(2)}) %copy-start.1) | copy-done | bytes 4456472
  36.7 5.9 %shard_map.69 = (bf16[1024,512]{1,0:T(8,128)(2,1)}, bf16[512,1024]{1,0:T(8,128)(2,1)S(1)}) custom-call(s32[8,17]{1,0:T(8,128)S(1)} %copy-done.2, s32[8,4]{1,0:T(8,128)S(1)} %copy.8.rmask_ref, bf16[1024,2176]{1,0:T(8,128)(2,1)S(1)} %copy-done.1, bf16[1024,512]{1,0:T(8,128)(2,1)} %collective-permute-done.low_ref, ...), custom_call_target="tpu_custom_call" | custom-call | flops 2281701376 | bytes 9699328 | tf_op jit(solution)/shard_map/pallas_call | solution.py:106
  42.6 0.0 collective-permute-done.2.core_ref
  42.6 0.0 collective-permute-done.4.both_ref
  42.7 3.6 %shard_map.70 = bf16[8,512,256]{2,1,0:T(8,128)(2,1)S(1)} custom-call(s32[1]{0:T(128)} %bitcast.panel_ref, bf16[512,1024]{1,0:T(8,128)(2,1)S(1)} %get-tuple-element.5.prodt_ref, bf16[1024,512]{1,0:T(8,128)(2,1)S(1)} %shard_map.68.mid_ref.own_ref, bf16[1024,512]{1,0:T(8,128)(2,1)S(1)} %collective-permute-done.2.core_ref, ...), custom_call_target="tpu_custom_call" | custom-call | flops 2147483648 | bytes 9437184 | tf_op jit(solution)/shard_map/pallas_call | solution.py:118
  46.2 49.1 %all_to_all.10.in_ref = bf16[8,512,256]{2,1,0:T(8,128)(2,1)S(1)} all-to-all(bf16[8,512,256]{2,1,0:T(8,128)(2,1)S(1)} %shard_map.70), channel_id=1, replica_groups=mesh['xh'=2,'core'=2,'xl'=2,'y'=4,'z'=8] {'xl','y'}, dimensions={0} | all-to-all | bytes 4194304 | tf_op jit(solution)/shard_map/all_to_all | solution.py:125
  95.3 0.3 shard_map.71
  95.7 16.7 %all_to_all.11.in_ref = bf16[8,32,512]{2,1,0:T(8,128)(2,1)S(1)} all-to-all(bf16[8,32,512]{2,1,0:T(8,128)(2,1)S(1)} %bitcast.2), channel_id=1, replica_groups=mesh['xh'=2,'core'=2,'xl'=2,'y'=4,'z'=8] {'z'}, dimensions={0} | all-to-all | bytes 524288 | tf_op jit(solution)/shard_map/all_to_all | solution.py:128
  112.4 0.7 shard_map.72
Async XLA Ops:
  0.6 29.4 %copy-start.3 = (s32[8,4]{0,1:T(4,128)S(1)}, s32[8,4]{0,1:T(4,128)}, u32[]{:S(2)}) copy-start(s32[8,4]{0,1:T(4,128)} %param.9) | copy-start | bytes 388
  0.6 33.8 %copy-start.2 = (s32[8,17]{1,0:T(8,128)S(1)}, s32[8,17]{1,0:T(8,128)}, u32[]{:S(2)}) copy-start(s32[8,17]{1,0:T(8,128)} %fmask_ref.1) | copy-start | bytes 1636
  1.4 1.2 %copy-start = (bf16[1024,512]{1,0:T(8,128)(2,1)S(1)}, bf16[1024,512]{1,0:T(8,128)(2,1)}, u32[]{:S(2)}) copy-start(bf16[1024,512]{1,0:T(8,128)(2,1)} %slab_ref.1) | copy-start | bytes 3145732
  3.5 26.5 %collective-permute-start.3 = (bf16[1024,512]{1,0:T(8,128)(2,1)S(1)}, bf16[1024,512]{1,0:T(8,128)(2,1)S(1)}, u32[]{:S(2)}, u32[]{:S(2)}) collective-permute-start(bf16[1024,512]{1,0:T(8,128)(2,1)S(1)} %shard_map.68.mid_ref.own_ref), channel_id=1, source_target_pairs={{0,128},{128,0},{1,129},{129,1},{2,130},{130,2},{3,131},{131,3},{4... | collective-permute-start | bytes 3145736 | tf_op jit(solution)/shard_map/ppermute | solution.py:103
  5.7 28.7 %collective-permute-start = (bf16[1024,512]{1,0:T(8,128)(2,1)S(1)}, bf16[1024,512]{1,0:T(8,128)(2,1)}, u32[]{:S(2)}, u32[]{:S(2)}) collective-permute-start(bf16[1024,512]{1,0:T(8,128)(2,1)S(1)} %shard_map.68.mid_ref.own_ref), channel_id=1, source_target_pairs={{0,1},{1,2},{2,3},{3,4},{4,5},{5,6},{6,7},{7,8},{8,9},{9,10},{10,1... | collective-permute-start | bytes 3145736 | tf_op jit(solution)/shard_map/ppermute | solution.py:101
  7.6 26.8 %collective-permute-start.1 = (bf16[1024,512]{1,0:T(8,128)(2,1)S(1)}, bf16[1024,512]{1,0:T(8,128)(2,1)}, u32[]{:S(2)}, u32[]{:S(2)}) collective-permute-start(bf16[1024,512]{1,0:T(8,128)(2,1)S(1)} %shard_map.68.mid_ref.own_ref), channel_id=1, source_target_pairs={{0,63},{1,0},{2,1},{3,2},{4,3},{5,4},{6,5},{7,6},{8,7},{9,8},{10,9... | collective-permute-start | bytes 3145736 | tf_op jit(solution)/shard_map/ppermute | solution.py:102
  11.4 31.2 %collective-permute-start.2 = (bf16[1024,512]{1,0:T(8,128)(2,1)S(1)}, bf16[1024,512]{1,0:T(8,128)(2,1)S(1)}, u32[]{:S(2)}, u32[]{:S(2)}) collective-permute-start(bf16[1024,512]{1,0:T(8,128)(2,1)S(1)} %shard_map.68.mid_ref.own_ref), channel_id=1, source_target_pairs={{0,64},{64,0},{1,65},{65,1},{2,66},{66,2},{3,67},{67,3},{4,68},{68... | collective-permute-start | bytes 3145736 | tf_op jit(solution)/shard_map/ppermute | solution.py:104
  30.0 12.7 %collective-permute-start.4 = (bf16[1024,512]{1,0:T(8,128)(2,1)S(1)}, bf16[1024,512]{1,0:T(8,128)(2,1)}, u32[]{:S(2)}, u32[]{:S(2)}) collective-permute-start(bf16[1024,512]{1,0:T(8,128)(2,1)S(1)} %collective-permute-done.3.far_ref), channel_id=1, source_target_pairs={{0,64},{64,0},{1,65},{65,1},{2,66},{66,2},{3,67},{67,3},{4,68},{68... | collective-permute-start | bytes 3145736 | tf_op jit(solution)/shard_map/ppermute | solution.py:105
  34.4 2.3 %copy-start.1 = (bf16[1024,2176]{1,0:T(8,128)(2,1)S(1)}, bf16[1024,2176]{1,0:T(8,128)(2,1)}, u32[]{:S(2)}) copy-start(bf16[1024,2176]{1,0:T(8,128)(2,1)} %fock_ref.1) | copy-start | bytes 13369348

commit v2 on v1

v2 whole, which is shorter than its diff:
```python
import functools
import math

import jax
import jax.numpy as jnp
from jax import lax
from jax.experimental import pallas as pl
from jax.experimental.pallas import tpu as pltpu
from jax.sharding import Mesh, PartitionSpec as P

F32, BF16 = jnp.float32, jnp.bfloat16
ROWS = ("xl", "y", "z")
BLK = ("xh", "core")
VMEM = pl.BlockSpec(memory_space=pltpu.VMEM)
SMEM = pl.BlockSpec(memory_space=pltpu.SMEM)
MIB = 1 << 20


def call(body, outs, ins, scratch=(), limit=8 * MIB, flops=0, moved=0):
    return pl.pallas_call(
        body,
        out_shape=outs,
        in_specs=ins,
        out_specs=jax.tree.map(lambda _: VMEM, outs),
        scratch_shapes=list(scratch),
        compiler_params=pltpu.CompilerParams(vmem_limit_bytes=limit),
        cost_estimate=pl.CostEstimate(flops=flops, bytes_accessed=moved, transcendentals=0),
    )


def dot(a, b):
    return jnp.dot(a, b, preferred_element_type=F32)


def mask_kernel(size, mask_ref, slab_ref, out_ref, h0_ref, h1_ref):
    panels, blocks = mask_ref.shape
    half = panels // 2
    for j in range(panels):
        ref = (h0_ref, h1_ref)[j // half]
        for i in range(blocks):
            rows = pl.ds(i * size, size)
            tile = slab_ref[rows, pl.ds(j * size, size)]
            tile = jnp.where(mask_ref[j, i] != 0, tile, jnp.zeros_like(tile))
            ref[rows, pl.ds((j % half) * size, size)] = tile
            out_ref[rows, pl.ds(j * size, size)] = tile


def middle_kernel(size, fmask_ref, fock_ref, h0_ref, h1_ref, held_ref, m0_ref, m1_ref, token_ref):
    token_ref[...] = jnp.zeros_like(token_ref)
    blocks, slots = fmask_ref.shape
    for i in range(blocks):
        rows = pl.ds(i * size, size)
        for o in range(slots):
            cols = pl.ds(o * size, size)
            tile = fock_ref[rows, cols]
            held_ref[rows, cols] = jnp.where(fmask_ref[i, o] != 0, tile, jnp.zeros_like(tile))
        fock = held_ref[rows, pl.ds((blocks - i) * size, blocks * size)]
        m0_ref[rows, :] = dot(fock, h0_ref[...])
        m1_ref[rows, :] = dot(fock, h1_ref[...])


def near_kernel(size, h, core_ref, y_ref, rmask_ref, held_ref, mid_ref, low_ref, high_ref, own_ref, near_ref, *rest):
    start = 0
    if h == 1:
        first_ref, opposite_ref, rest = rest[0], rest[1], rest[2:]
        start = first_ref.shape[1]
    out_ref, outt_ref, s0, s1, s2, s3 = rest
    if h == 1:
        out_ref[:, :start] = first_ref[...]
        s2[:start, :] = opposite_ref[...]
    blocks = rmask_ref.shape[1]
    slots = held_ref.shape[1] // size
    panels = mid_ref.shape[1] // size
    for i in range(blocks):
        rows = pl.ds(i * size, size)
        total = mid_ref[rows, :]
        total += dot(held_ref[rows, : (blocks - i) * size], low_ref[i * size :, :])
        total += dot(held_ref[rows, (2 * blocks - i) * size :], high_ref[: (slots - 2 * blocks + i) * size, :])
        for j in range(panels):
            cols = slice(j * size, (j + 1) * size)
            tile = total[:, cols]
            keep = rmask_ref[h * panels + j, i] != 0
            tile = jnp.where(keep, tile, jnp.zeros_like(tile)).astype(BF16)
            out_ref[rows, pl.ds(start + j * size, size)] = tile
            outt_ref[cols, rows] = tile.T
    project(core_ref, y_ref, outt_ref, own_ref, near_ref, (s0, s1, s2.at[pl.ds(start, s0.shape[0]), :], s3))


def project(core_ref, y_ref, outt_ref, same_ref, other_ref, to):
    half = to[0].shape[1]
    for q, ref in enumerate((same_ref, other_ref)):
        for k in range(2):
            terms = dot(outt_ref[...], ref[:, pl.ds(k * half, half)])
            step = ((core_ref[0] ^ q) * 2 + k - y_ref[0] + 4) % 4
            for s, into in enumerate(to):

                @pl.when(step == s)
                def _():
                    into[...] = terms.astype(into.dtype)


def far_kernel(core_ref, y_ref, t0_ref, t1_ref, far_ref, both_ref, *to):
    half = t0_ref.shape[0]
    for k, t in enumerate((t0_ref, t1_ref)):
        project(core_ref, y_ref, t, far_ref, both_ref, [ref.at[pl.ds(k * half, half), :] for ref in to])


def first_sum_kernel(xh_ref, own0, up0, down0, own1, up1, down1, opposite, far, up, cross, down, out_ref):
    count, deep, columns = out_ref.shape
    inner = count // 2
    half = own0.shape[0]
    lower, upper = pl.ds(0, half), pl.ds(half, half)

    def emit(first, cols, *parts):
        total = parts[0]
        for part in parts[1:]:
            total += part.astype(F32)
        turned = total.T.astype(BF16)
        for z in range(inner):
            out_ref[first + z, :, cols] = turned[z * deep : (z + 1) * deep]

    first = xh_ref[0] * inner
    emit(first, lower, own0[...], up0[...], down0[...], opposite[lower, :])
    emit(first, upper, own1[...], up1[...], down1[...], opposite[upper, :])
    first = (1 - xh_ref[0]) * inner
    for cols in (lower, upper):
        emit(first, cols, far[cols, :], up[cols, :], cross[cols, :], down[cols, :])


def last_sum_kernel(factor, in_ref, out_ref):
    total = in_ref[0].astype(F32)
    for s in range(1, in_ref.shape[0]):
        total += in_ref[s].astype(F32)
    out_ref[...] = total * factor


def after(x, *others):
    anywhere = pl.BlockSpec(memory_space=pl.ANY)
    return pl.pallas_call(
        lambda *refs: None,
        out_shape=jax.ShapeDtypeStruct(x.shape, x.dtype),
        in_specs=[anywhere] * (1 + len(others)),
        out_specs=anywhere,
        input_output_aliases={0: 0},
        compiler_params=pltpu.CompilerParams(vmem_limit_bytes=MIB),
    )(x, *others)


def ring(count, step):
    return [(i, (i + step) % count) for i in range(count)]


def on_device(fock_band, fock_slot_mask, orbital_slab, orbital_mask, result_mask):
    blocks, slots = fock_slot_mask.shape
    rows, columns = orbital_slab.shape
    size = rows // blocks
    half = columns // 2
    like = jax.ShapeDtypeStruct
    groups, inner = lax.axis_size(ROWS), lax.axis_size("z")
    xh, core, y = (lax.axis_index(name).reshape(1) for name in ("xh", "core", "y"))
    piece = like((rows, half), BF16)
    slab, h0, h1 = call(
        functools.partial(mask_kernel, size), (like((rows, columns), BF16), piece, piece), [SMEM, VMEM]
    )(orbital_mask.T, orbital_slab)
    up, down, swap = ring(groups, 1), ring(groups, groups - 1), ring(2, 1)
    low0, high0 = lax.ppermute(h0, ROWS, up), lax.ppermute(h0, ROWS, down)
    near_slab = lax.ppermute(slab, "core", swap)
    far_slab = lax.ppermute(slab, "xh", swap)
    held, mid0, mid1, token = call(
        functools.partial(middle_kernel, size),
        (like((rows, slots * size), BF16), *[like((rows, half), F32)] * 2, like((8, size), F32)),
        [SMEM, VMEM, VMEM, VMEM],
        flops=2 * rows * rows * columns,
        moved=4 * rows * slots * size,
    )(fock_slot_mask, fock_band, h0, h1)
    h1 = after(h1, low0, high0, token)
    low1, high1 = lax.ppermute(h1, ROWS, up), lax.ppermute(h1, ROWS, down)
    term, own = like((half, half), BF16), like((half, half), F32)
    long, long_own = like((columns, half), BF16), like((columns, half), F32)
    flipped = like((half, rows), BF16)

    def near(h, mid, low, high, *first):
        width = half if h == 0 else columns
        return call(
            functools.partial(near_kernel, size, h),
            (like((rows, width), BF16), flipped, own, term, term if h == 0 else long, term),
            [SMEM] * 3 + [VMEM] * (6 + len(first)),
            flops=2 * rows * half * (2 * columns + (slots - blocks) * size),
            moved=8 * rows * columns,
        )(core, y, result_mask.T, held, mid, low, high, slab, near_slab, *first)

    def send(part, step):
        return lax.ppermute(part, "y", ring(4, step))

    product0, flipped0, own0, up0, cross0, down0 = near(0, mid0, low0, high0)
    up0, down0 = send(up0, 1), send(down0, 3)
    product, flipped1, own1, up1, cross, down1 = near(1, mid1, low1, high1, product0, cross0)
    up1, down1, cross = send(up1, 1), send(down1, 3), send(cross, 2)
    far_slab = after(far_slab, own1, up0, down0)
    both_slab = lax.ppermute(far_slab, "core", swap)
    flipped1 = after(flipped1, up1, down1)
    far_own, far_up, far_cross, far_down = call(
        far_kernel,
        (long_own, long, long, long),
        [SMEM] * 2 + [VMEM] * 4,
        flops=8 * rows * half * columns,
        moved=8 * rows * columns,
    )(core, y, flipped0, flipped1, far_slab, both_slab)
    far_up, far_down, far_cross = send(far_up, 1), send(far_down, 3), send(far_cross, 2)
    deep = half // inner
    part = call(
        first_sum_kernel, like((2 * inner, deep, columns), BF16), [SMEM] + [VMEM] * 11, moved=8 * rows * half
    )(xh, own0, up0, down0, own1, up1, down1, cross, far_own, far_up, far_cross, far_down)
    part = lax.all_to_all(part, ("xl", "z"), 0, 0, tiled=True)
    factor = 1.0 / math.sqrt(rows * groups)
    projected = call(
        functools.partial(last_sum_kernel, factor), like((deep, columns), F32), [VMEM], moved=4 * deep * columns
    )(part)
    return (product, projected)


def solution(mesh):
    split = Mesh(mesh.devices.reshape(2, 2, 2, 4, 8), BLK + ROWS)
    placed = (P(ROWS, None), P(ROWS, None), P(ROWS, BLK), P(ROWS, BLK), P(ROWS, BLK))
    return jax.shard_map(
        on_device,
        mesh=split,
        in_specs=placed,
        out_specs=(P(ROWS, BLK), P(ROWS, BLK)),
        check_vma=False,
    )
```

time: 114 us -> 114 us (level); the launches traced: 113 us -> 112 us
  blocking collectives: 65.8 us -> 24.2 us
  starting transfers between devices: 7.96 us -> 47.5 us
  waiting for transfers between devices: 22.9 us -> 7.84 us
  local copies, waits for them, and re-layouts: 4.34 us -> 12.3 us
  Pallas kernels: 11.4 us -> 19.3 us
    all_to_all x2 -> x1, blocking collectives: 65.8 us -> 24.2 us  [on_device(): part = lax.all_to_all(part, ('xl', 'z'), 0, 0, tiled=True)]
    ppermute x5 -> x15, starting transfers between devices: 7.96 us -> 47.5 us  [the longest x8 35.4 us: send(): return lax.ppermute(part, 'y', ring(4, step))]
    ppermute x5 -> x15, waiting for transfers between devices: 22.9 us -> 7.84 us  [the longest x8 7.39 us: send(): return lax.ppermute(part, 'y', ring(4, step))]
    unnamed x10 -> x22, local copies, waits for them, and re-layouts: 4.34 us -> 12.3 us
    pallas_call x5 -> x10, Pallas kernels: 11.4 us -> 19.3 us  [the longest x2 7.76 us: near(): call(functools.partial(near_kernel, size, h), (like((rows, width), BF16),...]
  transfers between devices with their start and end apart: 5 -> 15, of which waited for: 2 -> 5; matrix products, arithmetic and copies ran while one was open for 0% -> 0% of each run, Pallas kernels for 5% -> 15%
where the time goes in v2:
time: 114 us; the launch traced here: 112 us
  starting transfers between devices  47.5 us (42%)
  blocking collectives  24.2 us (21%)
  Pallas kernels  19.3 us (17%)
  local copies, waits for them, and re-layouts  12.3 us (11%)
  waiting for transfers between devices  7.84 us (7%)
    ppermute x8, starting transfers between devices, send(): return lax.ppermute(part, 'y', ring(4, step))  35.4 us
    all_to_all x1, blocking collectives, on_device(): part = lax.all_to_all(part, ('xl', 'z'), 0, 0, tiled=True)  24.2 us
    unnamed x22, local copies, waits for them, and re-layouts  12.3 us
    pallas_call x2, Pallas kernels, near(): call(functools.partial(near_kernel, size, h), (like((rows, width), BF16),...  7.76 us
    ppermute x8, waiting for transfers between devices, send(): return lax.ppermute(part, 'y', ring(4, step))  7.39 us
    ppermute x2, starting transfers between devices, on_device(): low0, high0 = (lax.ppermute(h0, ROWS, up), lax.ppermute(h0, ROWS, down))  5.75 us
    pallas_call x1, Pallas kernels, on_device(): call(far_kernel, (long_own, long, long, long), [SMEM] * 2 + [VMEM] * 4, f...  5.5 us
    ppermute x2, starting transfers between devices, on_device(): low1, high1 = (lax.ppermute(h1, ROWS, up), lax.ppermute(h1, ROWS, down))  4.14 us
  transfers between devices with their start and end apart: 15, of which 5 were waited for; matrix products, arithmetic and copies ran while one was open for 0% of the time, Pallas kernels for 15%

profile of v2, /device:TPU:10, one launch (start us, length us, event | category | flops | bytes accessed | tf_op | source)
XLA Modules:
  0.0 111.8 jit_solution(10145764385439404279)
XLA Ops:
  0.6 1.2 %copy-done.5 = bf16[1024,512]{1,0:T(8,128)(2,1)S(1)} copy-done((bf16[1024,512]{1,0:T(8,128)(2,1)S(1)}, bf16[1024,512]{1,0:T(8,128)(2,1)}, u32[]{:S(2)}) %copy-start.5) | copy-done | bytes 1048600
  1.9 0.7 copy-done.10
  2.5 1.7 %shard_map.68 = (bf16[1024,512]{1,0:T(8,128)(2,1)S(1)}, bf16[1024,256]{1,0:T(8,128)(2,1)S(1)}, bf16[1024,256]{1,0:T(8,128)(2,1)}) custom-call(s32[4,8]{1,0:T(4,128)S(1)} %bitcast.7, bf16[1024,512]{1,0:T(8,128)(2,1)S(1)} %copy-done.5), custom_call_target="tpu_custom_call" | custom-call | tf_op jit(solution)/shard_map/pallas_call | solution.py:162
  4.3 1.9 %collective-permute-start = (bf16[1024,256]{1,0:T(8,128)(2,1)S(1)}, bf16[1024,256]{1,0:T(8,128)(2,1)S(1)}, u32[]{:S(2)}, u32[]{:S(2)}) collective-permute-start(bf16[1024,256]{1,0:T(8,128)(2,1)S(1)} %get-tuple-element.25.h0_ref), channel_id=1, source_target_pairs={{0,1},{1,2},{2,3},{3,4},{4,5},{5,6},{6,7},{7,8},{8,9},{9,10},{10,1... | collective-permute-start | bytes 1572872 | tf_op jit(solution)/shard_map/ppermute | solution.py:166
  6.2 3.8 %collective-permute-start.1 = (bf16[1024,256]{1,0:T(8,128)(2,1)S(1)}, bf16[1024,256]{1,0:T(8,128)(2,1)S(1)}, u32[]{:S(2)}, u32[]{:S(2)}) collective-permute-start(bf16[1024,256]{1,0:T(8,128)(2,1)S(1)} %get-tuple-element.25.h0_ref), channel_id=1, source_target_pairs={{0,63},{1,0},{2,1},{3,2},{4,3},{5,4},{6,5},{7,6},{8,7},{9,8},{10,9... | collective-permute-start | bytes 1572872 | tf_op jit(solution)/shard_map/ppermute | solution.py:166
  10.0 2.1 %collective-permute-start.10 = (bf16[1024,512]{1,0:T(8,128)(2,1)S(1)}, bf16[1024,512]{1,0:T(8,128)(2,1)}, u32[]{:S(2)}, u32[]{:S(2)}) collective-permute-start(bf16[1024,512]{1,0:T(8,128)(2,1)S(1)} %get-tuple-element.30.own_ref), channel_id=1, source_target_pairs={{0,128},{128,0},{1,129},{129,1},{2,130},{130,2},{3,131},{131,3},{4... | collective-permute-start | bytes 3145736 | tf_op jit(solution)/shard_map/ppermute | solution.py:168
  12.1 2.3 %copy-done.2 = bf16[1024,2176]{1,0:T(8,128)(2,1)S(1)} copy-done((bf16[1024,2176]{1,0:T(8,128)(2,1)S(1)}, bf16[1024,2176]{1,0:T(8,128)(2,1)}, u32[]{:S(2)}) %copy-start.2) | copy-done | bytes 4456472
  14.4 0.7 copy-done.9
  15.1 3.3 %shard_map.69 = (bf16[1024,2176]{1,0:T(8,128)(2,1)S(1)}, f32[1024,256]{1,0:T(8,128)S(1)}, f32[1024,256]{1,0:T(8,128)S(1)}, f32[8,128]{1,0:T(8,128)S(1)}) custom-call(s32[8,17]{1,0:T(8,128)S(1)} %copy-done.9, bf16[1024,2176]{1,0:T(8,128)(2,1)S(1)} %copy-done.2, bf16[1024,256]{1,0:T(8,128)(2,1)S(1)} %get-tuple-element.25.h0_ref, ...), custom_call_target="tpu_custom_call" | custom-call | flops 1073741824 | bytes 8912896 | tf_op jit(solution)/shard_map/pallas_call | solution.py:169
  18.4 2.0 %copy-done = bf16[1024,2176]{1,0:T(8,128)(2,1)} copy-done((bf16[1024,2176]{1,0:T(8,128)(2,1)}, bf16[1024,2176]{1,0:T(8,128)(2,1)S(1)}, u32[]{:S(2)}) %copy-start) | copy-done | bytes 4456472
  20.4 1.0 copy-done.3
  21.4 1.0 copy-done.6
  22.6 4.1 %collective-permute-start.3 = (bf16[1024,256]{1,0:T(8,128)(2,1)}, bf16[1024,256]{1,0:T(8,128)(2,1)}, u32[]{:S(2)}, u32[]{:S(2)}) collective-permute-start(bf16[1024,256]{1,0:T(8,128)(2,1)} %shard_map.70), channel_id=1, source_target_pairs={{0,63},{1,0},{2,1},{3,2},{4,3},{5,4},{6,5},{7,6},{8,7},{9,8},{10,9... | collective-permute-start | bytes 1572872 | tf_op jit(solution)/shard_map/ppermute | solution.py:177
  26.7 2.3 %copy-done.1 = bf16[1024,2176]{1,0:T(8,128)(2,1)S(1)} copy-done((bf16[1024,2176]{1,0:T(8,128)(2,1)S(1)}, bf16[1024,2176]{1,0:T(8,128)(2,1)}, u32[]{:S(2)}) %copy-start.1) | copy-done | bytes 4456472
  29.0 1.2 %copy-done.4 = f32[1024,256]{1,0:T(8,128)S(1)} copy-done((f32[1024,256]{1,0:T(8,128)S(1)}, f32[1024,256]{1,0:T(8,128)}, u32[]{:S(2)}) %copy-start.4) | copy-done | bytes 1048600
  30.2 3.0 %shard_map.71 = (bf16[1024,256]{1,0:T(8,128)(2,1)S(1)}, bf16[256,1024]{1,0:T(8,128)(2,1)S(1)}, f32[256,256]{1,0:T(8,128)S(1)}, bf16[256,256]{1,0:T(8,128)(2,1)S(...) custom-call(s32[1]{0:T(128)} %bitcast.core_ref, s32[1]{0:T(128)} %bitcast.1.y_ref, s32[4,8]{1,0:T(4,128)S(1)} %bitcast.5, ...), custom_call_target="tpu_custom_call" | custom-call | flops 1140850688 | bytes 4194304 | tf_op jit(solution)/shard_map/pallas_call | solution.py:184
  33.2 1.7 %collective-permute-start.5 = (bf16[256,256]{1,0:T(8,128)(2,1)S(1)}, bf16[256,256]{1,0:T(8,128)(2,1)S(1)}, u32[]{:S(2)}, u32[]{:S(2)}) collective-permute-start(bf16[256,256]{1,0:T(8,128)(2,1)S(1)} %get-tuple-element.36), channel_id=1, source_target_pairs={{0,8},{8,16},{16,24},{24,0},{1,9},{9,17},{17,25},{25,1},{2,10},{10... | collective-permute-start | bytes 393224 | tf_op jit(solution)/shard_map/ppermute | solution.py:193
  34.9 3.7 %collective-permute-start.6 = (bf16[256,256]{1,0:T(8,128)(2,1)S(1)}, bf16[256,256]{1,0:T(8,128)(2,1)S(1)}, u32[]{:S(2)}, u32[]{:S(2)}) collective-permute-start(bf16[256,256]{1,0:T(8,128)(2,1)S(1)} %get-tuple-element.37), channel_id=1, source_target_pairs={{0,24},{8,0},{16,8},{24,16},{1,25},{9,1},{17,9},{25,17},{2,26},{10... | collective-permute-start | bytes 393224 | tf_op jit(solution)/shard_map/ppermute | solution.py:193
  38.8 4.8 %shard_map.72 = (bf16[1024,512]{1,0:T(8,128)(2,1)}, bf16[256,1024]{1,0:T(8,128)(2,1)S(1)}, f32[256,256]{1,0:T(8,128)S(1)}, bf16[256,256]{1,0:T(8,128)(2,1)S(1)},...) custom-call(s32[1]{0:T(128)} %bitcast.core_ref, s32[1]{0:T(128)} %bitcast.1.y_ref, s32[4,8]{1,0:T(4,128)S(1)} %bitcast.6, ...), custom_call_target="tpu_custom_call" | custom-call | flops 1140850688 | bytes 4194304 | tf_op jit(solution)/shard_map/pallas_call | solution.py:184
  43.7 1.9 %collective-permute-start.7 = (bf16[256,256]{1,0:T(8,128)(2,1)S(1)}, bf16[256,256]{1,0:T(8,128)(2,1)S(1)}, u32[]{:S(2)}, u32[]{:S(2)}) collective-permute-start(bf16[256,256]{1,0:T(8,128)(2,1)S(1)} %get-tuple-element.39), channel_id=1, source_target_pairs={{0,8},{8,16},{16,24},{24,0},{1,9},{9,17},{17,25},{25,1},{2,10},{10... | collective-permute-start | bytes 393224 | tf_op jit(solution)/shard_map/ppermute | solution.py:193
  45.6 3.8 %collective-permute-start.8 = (bf16[256,256]{1,0:T(8,128)(2,1)S(1)}, bf16[256,256]{1,0:T(8,128)(2,1)S(1)}, u32[]{:S(2)}, u32[]{:S(2)}) collective-permute-start(bf16[256,256]{1,0:T(8,128)(2,1)S(1)} %get-tuple-element.40), channel_id=1, source_target_pairs={{0,24},{8,0},{16,8},{24,16},{1,25},{9,1},{17,9},{25,17},{2,26},{10... | collective-permute-start | bytes 393224 | tf_op jit(solution)/shard_map/ppermute | solution.py:193
  49.4 13.4 %collective-permute-start.9 = (bf16[512,256]{1,0:T(8,128)(2,1)}, bf16[512,256]{1,0:T(8,128)(2,1)S(1)}, u32[]{:S(2)}, u32[]{:S(2)}) collective-permute-start(bf16[512,256]{1,0:T(8,128)(2,1)} %get-tuple-element.41), channel_id=1, source_target_pairs={{0,16},{8,24},{16,0},{24,8},{1,17},{9,25},{17,1},{25,9},{2,18},{10... | collective-permute-start | bytes 786440 | tf_op jit(solution)/shard_map/ppermute | solution.py:193
  62.8 2.2 %collective-permute-done.8.refs_2_.down1 = bf16[256,256]{1,0:T(8,128)(2,1)S(1)} collective-permute-done((bf16[256,256]{1,0:T(8,128)(2,1)S(1)}, bf16[256,256]{1,0:T(8,128)(2,1)S(1)}, u32[]{:S(2)}, u32[]{:S(2)}) %collective-permute-start.8) | collective-permute-done | bytes 131104 | tf_op jit(solution)/shard_map/ppermute | solution.py:193
  64.9 5.5 %shard_map.75 = (f32[512,256]{1,0:T(8,128)S(1)}, bf16[512,256]{1,0:T(8,128)(2,1)}, bf16[512,256]{1,0:T(8,128)(2,1)}, bf16[512,256]{1,0:T(8,128)(2,1)S(1)}) custom-call(s32[1]{0:T(128)} %bitcast.core_ref, s32[1]{0:T(128)} %bitcast.1.y_ref, bf16[256,1024]{1,0:T(8,128)(2,1)S(1)} %get-tuple-element.42.t0_ref, bf16[256,1024]{1,0:T(8,128)(2,1)S(1)} %shard_map.73.t1_ref, ...), custom_call_target="tpu_custom_call" | custom-call | flops 1073741824 | bytes 4194304 | tf_op jit(solution)/shard_map/pallas_call | solution.py:202
  70.4 2.8 %collective-permute-start.12 = (bf16[512,256]{1,0:T(8,128)(2,1)}, bf16[512,256]{1,0:T(8,128)(2,1)S(1)}, u32[]{:S(2)}, u32[]{:S(2)}) collective-permute-start(bf16[512,256]{1,0:T(8,128)(2,1)} %get-tuple-element.45), channel_id=1, source_target_pairs={{0,8},{8,16},{16,24},{24,0},{1,9},{9,17},{17,25},{25,1},{2,10},{10... | collective-permute-start | bytes 786440 | tf_op jit(solution)/shard_map/ppermute | solution.py:193
  73.2 5.5 %collective-permute-start.13 = (bf16[512,256]{1,0:T(8,128)(2,1)}, bf16[512,256]{1,0:T(8,128)(2,1)S(1)}, u32[]{:S(2)}, u32[]{:S(2)}) collective-permute-start(bf16[512,256]{1,0:T(8,128)(2,1)} %get-tuple-element.46), channel_id=1, source_target_pairs={{0,16},{8,24},{16,0},{24,8},{1,17},{9,25},{17,1},{25,9},{2,18},{10... | collective-permute-start | bytes 786440 | tf_op jit(solution)/shard_map/ppermute | solution.py:193
  78.7 2.6 %collective-permute-start.14 = (bf16[512,256]{1,0:T(8,128)(2,1)S(1)}, bf16[512,256]{1,0:T(8,128)(2,1)S(1)}, u32[]{:S(2)}, u32[]{:S(2)}) collective-permute-start(bf16[512,256]{1,0:T(8,128)(2,1)S(1)} %get-tuple-element.47), channel_id=1, source_target_pairs={{0,24},{8,0},{16,8},{24,16},{1,25},{9,1},{17,9},{25,17},{2,26},{10... | collective-permute-start | bytes 786440 | tf_op jit(solution)/shard_map/ppermute | solution.py:193
  81.3 2.5 %collective-permute-done.13.cross = bf16[512,256]{1,0:T(8,128)(2,1)S(1)} collective-permute-done((bf16[512,256]{1,0:T(8,128)(2,1)}, bf16[512,256]{1,0:T(8,128)(2,1)S(1)}, u32[]{:S(2)}, u32[]{:S(2)}) %collective-permute-start.13) | collective-permute-done | bytes 262176 | tf_op jit(solution)/shard_map/ppermute | solution.py:193
  83.9 2.7 %collective-permute-done.14.down = bf16[512,256]{1,0:T(8,128)(2,1)S(1)} collective-permute-done((bf16[512,256]{1,0:T(8,128)(2,1)S(1)}, bf16[512,256]{1,0:T(8,128)(2,1)S(1)}, u32[]{:S(2)}, u32[]{:S(2)}) %collective-permute-start.14) | collective-permute-done | bytes 262176 | tf_op jit(solution)/shard_map/ppermute | solution.py:193
  86.6 0.3 shard_map.76
  86.9 24.2 %all_to_all.5.in_ref = bf16[16,32,512]{2,1,0:T(8,128)(2,1)S(1)} all-to-all(bf16[16,32,512]{2,1,0:T(8,128)(2,1)S(1)} %shard_map.76), channel_id=1, replica_groups=mesh['xh'=2,'core'=2,'xl'=2,'y'=4,'z'=8] {'xl','z'}, dimensions={0} | all-to-all | bytes 1048576 | tf_op jit(solution)/shard_map/all_to_all | solution.py:214
  111.1 0.7 shard_map.77
  (31 shorter events, 0.6 us)
Async XLA Ops:
  0.6 1.2 %copy-start.5 = (bf16[1024,512]{1,0:T(8,128)(2,1)S(1)}, bf16[1024,512]{1,0:T(8,128)(2,1)}, u32[]{:S(2)}) copy-start(bf16[1024,512]{1,0:T(8,128)(2,1)} %slab_ref.1) | copy-start | bytes 3145732
  1.9 0.7 copy-start.10
  2.5 24.2 %copy-start.8 = (s32[8,4]{0,1:T(4,128)S(1)}, s32[8,4]{0,1:T(4,128)}, u32[]{:S(2)}) copy-start(s32[8,4]{0,1:T(4,128)} %param.9) | copy-start | bytes 388
  4.3 22.5 %collective-permute-start.4 = (bf16[1024,512]{1,0:T(8,128)(2,1)S(1)}, bf16[1024,512]{1,0:T(8,128)(2,1)S(1)}, u32[]{:S(2)}, u32[]{:S(2)}) collective-permute-start(bf16[1024,512]{1,0:T(8,128)(2,1)S(1)} %get-tuple-element.30.own_ref), channel_id=1, source_target_pairs={{0,64},{64,0},{1,65},{65,1},{2,66},{66,2},{3,67},{67,3},{4,68},{68... | collective-permute-start | bytes 3145736 | tf_op jit(solution)/shard_map/ppermute | solution.py:167
  4.3 18.3 %collective-permute-start = (bf16[1024,256]{1,0:T(8,128)(2,1)S(1)}, bf16[1024,256]{1,0:T(8,128)(2,1)S(1)}, u32[]{:S(2)}, u32[]{:S(2)}) collective-permute-start(bf16[1024,256]{1,0:T(8,128)(2,1)S(1)} %get-tuple-element.25.h0_ref), channel_id=1, source_target_pairs={{0,1},{1,2},{2,3},{3,4},{4,5},{5,6},{6,7},{7,8},{8,9},{9,10},{10,1... | collective-permute-start | bytes 1572872 | tf_op jit(solution)/shard_map/ppermute | solution.py:166
  6.2 16.4 %collective-permute-start.1 = (bf16[1024,256]{1,0:T(8,128)(2,1)S(1)}, bf16[1024,256]{1,0:T(8,128)(2,1)S(1)}, u32[]{:S(2)}, u32[]{:S(2)}) collective-permute-start(bf16[1024,256]{1,0:T(8,128)(2,1)S(1)} %get-tuple-element.25.h0_ref), channel_id=1, source_target_pairs={{0,63},{1,0},{2,1},{3,2},{4,3},{5,4},{6,5},{7,6},{8,7},{9,8},{10,9... | collective-permute-start | bytes 1572872 | tf_op jit(solution)/shard_map/ppermute | solution.py:166
  10.0 33.6 %collective-permute-start.10 = (bf16[1024,512]{1,0:T(8,128)(2,1)S(1)}, bf16[1024,512]{1,0:T(8,128)(2,1)}, u32[]{:S(2)}, u32[]{:S(2)}) collective-permute-start(bf16[1024,512]{1,0:T(8,128)(2,1)S(1)} %get-tuple-element.30.own_ref), channel_id=1, source_target_pairs={{0,128},{128,0},{1,129},{129,1},{2,130},{130,2},{3,131},{131,3},{4... | collective-permute-start | bytes 3145736 | tf_op jit(solution)/shard_map/ppermute | solution.py:168
  12.1 2.3 %copy-start.2 = (bf16[1024,2176]{1,0:T(8,128)(2,1)S(1)}, bf16[1024,2176]{1,0:T(8,128)(2,1)}, u32[]{:S(2)}) copy-start(bf16[1024,2176]{1,0:T(8,128)(2,1)} %fock_ref.1) | copy-start | bytes 13369348
  14.4 0.7 copy-start.9
  18.3 2.0 %copy-start = (bf16[1024,2176]{1,0:T(8,128)(2,1)}, bf16[1024,2176]{1,0:T(8,128)(2,1)S(1)}, u32[]{:S(2)}) copy-start(bf16[1024,2176]{1,0:T(8,128)(2,1)S(1)} %get-tuple-element.27.held_ref) | copy-start | bytes 13369348
  20.4 1.0 copy-start.3
  21.4 1.0 copy-start.6
  22.6 16.2 %collective-permute-start.2 = (bf16[1024,256]{1,0:T(8,128)(2,1)}, bf16[1024,256]{1,0:T(8,128)(2,1)}, u32[]{:S(2)}, u32[]{:S(2)}) collective-permute-start(bf16[1024,256]{1,0:T(8,128)(2,1)} %shard_map.70), channel_id=1, source_target_pairs={{0,1},{1,2},{2,3},{3,4},{4,5},{5,6},{6,7},{7,8},{8,9},{9,10},{10,1... | collective-permute-start | bytes 1572872 | tf_op jit(solution)/shard_map/ppermute | solution.py:177
  22.6 16.2 %collective-permute-start.3 = (bf16[1024,256]{1,0:T(8,128)(2,1)}, bf16[1024,256]{1,0:T(8,128)(2,1)}, u32[]{:S(2)}, u32[]{:S(2)}) collective-permute-start(bf16[1024,256]{1,0:T(8,128)(2,1)} %shard_map.70), channel_id=1, source_target_pairs={{0,63},{1,0},{2,1},{3,2},{4,3},{5,4},{6,5},{7,6},{8,7},{9,8},{10,9... | collective-permute-start | bytes 1572872 | tf_op jit(solution)/shard_map/ppermute | solution.py:177
  26.7 2.3 %copy-start.1 = (bf16[1024,2176]{1,0:T(8,128)(2,1)S(1)}, bf16[1024,2176]{1,0:T(8,128)(2,1)}, u32[]{:S(2)}) copy-start(bf16[1024,2176]{1,0:T(8,128)(2,1)} %copy-done) | copy-start | bytes 13369348
  29.0 1.2 %copy-start.4 = (f32[1024,256]{1,0:T(8,128)S(1)}, f32[1024,256]{1,0:T(8,128)}, u32[]{:S(2)}) copy-start(f32[1024,256]{1,0:T(8,128)} %copy-done.3) | copy-start | bytes 3145732
  30.2 8.6 %copy-start.7 = (f32[1024,256]{1,0:T(8,128)S(1)}, f32[1024,256]{1,0:T(8,128)}, u32[]{:S(2)}) copy-start(f32[1024,256]{1,0:T(8,128)} %copy-done.6) | copy-start | bytes 3145732
  33.2 10.3 %collective-permute-start.5 = (bf16[256,256]{1,0:T(8,128)(2,1)S(1)}, bf16[256,256]{1,0:T(8,128)(2,1)S(1)}, u32[]{:S(2)}, u32[]{:S(2)}) collective-permute-start(bf16[256,256]{1,0:T(8,128)(2,1)S(1)} %get-tuple-element.36), channel_id=1, source_target_pairs={{0,8},{8,16},{16,24},{24,0},{1,9},{9,17},{17,25},{25,1},{2,10},{10... | collective-permute-start | bytes 393224 | tf_op jit(solution)/shard_map/ppermute | solution.py:193
  34.9 8.7 %collective-permute-start.6 = (bf16[256,256]{1,0:T(8,128)(2,1)S(1)}, bf16[256,256]{1,0:T(8,128)(2,1)S(1)}, u32[]{:S(2)}, u32[]{:S(2)}) collective-permute-start(bf16[256,256]{1,0:T(8,128)(2,1)S(1)} %get-tuple-element.37), channel_id=1, source_target_pairs={{0,24},{8,0},{16,8},{24,16},{1,25},{9,1},{17,9},{25,17},{2,26},{10... | collective-permute-start | bytes 393224 | tf_op jit(solution)/shard_map/ppermute | solution.py:193
  43.6 21.3 %collective-permute-start.11 = (bf16[1024,512]{1,0:T(8,128)(2,1)}, bf16[1024,512]{1,0:T(8,128)(2,1)S(1)}, u32[]{:S(2)}, u32[]{:S(2)}) collective-permute-start(bf16[1024,512]{1,0:T(8,128)(2,1)} %shard_map.74.far_ref), channel_id=1, source_target_pairs={{0,64},{64,0},{1,65},{65,1},{2,66},{66,2},{3,67},{67,3},{4,68},{68... | collective-permute-start | bytes 3145736 | tf_op jit(solution)/shard_map/ppermute | solution.py:200
  43.7 19.1 %collective-permute-start.7 = (bf16[256,256]{1,0:T(8,128)(2,1)S(1)}, bf16[256,256]{1,0:T(8,128)(2,1)S(1)}, u32[]{:S(2)}, u32[]{:S(2)}) collective-permute-start(bf16[256,256]{1,0:T(8,128)(2,1)S(1)} %get-tuple-element.39), channel_id=1, source_target_pairs={{0,8},{8,16},{16,24},{24,0},{1,9},{9,17},{17,25},{25,1},{2,10},{10... | collective-permute-start | bytes 393224 | tf_op jit(solution)/shard_map/ppermute | solution.py:193
  45.6 19.3 %collective-permute-start.8 = (bf16[256,256]{1,0:T(8,128)(2,1)S(1)}, bf16[256,256]{1,0:T(8,128)(2,1)S(1)}, u32[]{:S(2)}, u32[]{:S(2)}) collective-permute-start(bf16[256,256]{1,0:T(8,128)(2,1)S(1)} %get-tuple-element.40), channel_id=1, source_target_pairs={{0,24},{8,0},{16,8},{24,16},{1,25},{9,1},{17,9},{25,17},{2,26},{10... | collective-permute-start | bytes 393224 | tf_op jit(solution)/shard_map/ppermute | solution.py:193
  49.4 31.9 %collective-permute-start.9 = (bf16[512,256]{1,0:T(8,128)(2,1)}, bf16[512,256]{1,0:T(8,128)(2,1)S(1)}, u32[]{:S(2)}, u32[]{:S(2)}) collective-permute-start(bf16[512,256]{1,0:T(8,128)(2,1)} %get-tuple-element.41), channel_id=1, source_target_pairs={{0,16},{8,24},{16,0},{24,8},{1,17},{9,25},{17,1},{25,9},{2,18},{10... | collective-permute-start | bytes 786440 | tf_op jit(solution)/shard_map/ppermute | solution.py:193
  70.4 10.9 %collective-permute-start.12 = (bf16[512,256]{1,0:T(8,128)(2,1)}, bf16[512,256]{1,0:T(8,128)(2,1)S(1)}, u32[]{:S(2)}, u32[]{:S(2)}) collective-permute-start(bf16[512,256]{1,0:T(8,128)(2,1)} %get-tuple-element.45), channel_id=1, source_target_pairs={{0,8},{8,16},{16,24},{24,0},{1,9},{9,17},{17,25},{25,1},{2,10},{10... | collective-permute-start | bytes 786440 | tf_op jit(solution)/shard_map/ppermute | solution.py:193
  73.2 10.7 %collective-permute-start.13 = (bf16[512,256]{1,0:T(8,128)(2,1)}, bf16[512,256]{1,0:T(8,128)(2,1)S(1)}, u32[]{:S(2)}, u32[]{:S(2)}) collective-permute-start(bf16[512,256]{1,0:T(8,128)(2,1)} %get-tuple-element.46), channel_id=1, source_target_pairs={{0,16},{8,24},{16,0},{24,8},{1,17},{9,25},{17,1},{25,9},{2,18},{10... | collective-permute-start | bytes 786440 | tf_op jit(solution)/shard_map/ppermute | solution.py:193
  78.7 7.9 %collective-permute-start.14 = (bf16[512,256]{1,0:T(8,128)(2,1)S(1)}, bf16[512,256]{1,0:T(8,128)(2,1)S(1)}, u32[]{:S(2)}, u32[]{:S(2)}) collective-permute-start(bf16[512,256]{1,0:T(8,128)(2,1)S(1)} %get-tuple-element.47), channel_id=1, source_target_pairs={{0,24},{8,0},{16,8},{24,16},{1,25},{9,1},{17,9},{25,17},{2,26},{10... | collective-permute-start | bytes 786440 | tf_op jit(solution)/shard_map/ppermute | solution.py:193

commit v3 on v2

v3 whole, which is shorter than its diff:
```python
import functools
import math

import jax
import jax.numpy as jnp
from jax import lax
from jax.experimental import pallas as pl
from jax.experimental.pallas import tpu as pltpu
from jax.sharding import Mesh, PartitionSpec as P

F32, BF16 = jnp.float32, jnp.bfloat16
ROWS = ("xl", "y", "z")
BLK = ("xh", "core")
VMEM = pl.BlockSpec(memory_space=pltpu.VMEM)
SMEM = pl.BlockSpec(memory_space=pltpu.SMEM)
MIB = 1 << 20


def call(body, outs, ins, scratch=(), limit=8 * MIB, flops=0, moved=0):
    return pl.pallas_call(
        body,
        out_shape=outs,
        in_specs=ins,
        out_specs=jax.tree.map(lambda _: VMEM, outs),
        scratch_shapes=list(scratch),
        compiler_params=pltpu.CompilerParams(vmem_limit_bytes=limit),
        cost_estimate=pl.CostEstimate(flops=flops, bytes_accessed=moved, transcendentals=0),
    )


def dot(a, b):
    return jnp.dot(a, b, preferred_element_type=F32)


def mask_kernel(size, mask_ref, slab_hbm, h0_ref, h1_ref, both_ref, held, sems):
    panels, blocks = mask_ref.shape
    half = panels // 2
    copies = [
        pltpu.make_async_copy(slab_hbm.at[pl.ds(i * size, size)], held.at[i], sems.at[i])
        for i in range(blocks)
    ]
    for copy in copies:
        copy.start()
    for i, copy in enumerate(copies):
        copy.wait()
        rows = pl.ds(i * size, size)
        for j in range(panels):
            ref = (h0_ref, h1_ref)[j // half]
            tile = held[i, :, j * size : (j + 1) * size]
            tile = jnp.where(mask_ref[j, i] != 0, tile, jnp.zeros_like(tile))
            ref[rows, pl.ds((j % half) * size, size)] = tile
            both_ref[j // half, rows, pl.ds((j % half) * size, size)] = tile


def middle_kernel(size, fmask_ref, fock_ref, h0_ref, h1_ref, held_ref, m0_ref, m1_ref, token_ref):
    token_ref[...] = jnp.zeros_like(token_ref)
    blocks, slots = fmask_ref.shape
    for i in range(blocks):
        rows = pl.ds(i * size, size)
        for o in range(slots):
            cols = pl.ds(o * size, size)
            tile = fock_ref[rows, cols]
            held_ref[rows, cols] = jnp.where(fmask_ref[i, o] != 0, tile, jnp.zeros_like(tile))
        fock = held_ref[rows, pl.ds((blocks - i) * size, blocks * size)]
        m0_ref[rows, :] = dot(fock, h0_ref[...])
        m1_ref[rows, :] = dot(fock, h1_ref[...])


def pick_kernel(edge, own_ref, crossed_ref, up_ref, down_ref):
    y, z = lax.axis_index("y"), lax.axis_index("z")
    top, bottom = (y == edge[0] - 1) & (z == edge[1] - 1), (y == 0) & (z == 0)
    for ref, cross in ((up_ref, top), (down_ref, bottom)):

        @pl.when(cross)
        def _():
            ref[...] = crossed_ref[...]

        @pl.when(jnp.logical_not(cross))
        def _():
            ref[...] = own_ref[...]


def near_kernel(size, h, rmask_ref, held_ref, mid_ref, low_ref, high_ref, *rest):
    own_refs, near_ref, rest = rest[:2], rest[2], rest[3:]
    start = 0
    if h == 1:
        first_ref, rest = rest[0], rest[1:]
        start = first_ref.shape[1]
    out_ref, outt_ref, terms_ref = rest
    if h == 1:
        out_ref[:, :start] = first_ref[...]
    blocks = rmask_ref.shape[1]
    slots = held_ref.shape[1] // size
    panels = mid_ref.shape[1] // size
    for i in range(blocks):
        rows = pl.ds(i * size, size)
        total = mid_ref[rows, :]
        total += dot(held_ref[rows, : (blocks - i) * size], low_ref[i * size :, :])
        total += dot(held_ref[rows, (2 * blocks - i) * size :], high_ref[: (slots - 2 * blocks + i) * size, :])
        for j in range(panels):
            cols = slice(j * size, (j + 1) * size)
            tile = total[:, cols]
            keep = rmask_ref[h * panels + j, i] != 0
            tile = jnp.where(keep, tile, jnp.zeros_like(tile)).astype(BF16)
            out_ref[rows, pl.ds(start + j * size, size)] = tile
            outt_ref[cols, rows] = tile.T
    core = lax.axis_index("core")
    for k in range(2):
        terms_ref[core * 2 + k] = dot(outt_ref[...], own_refs[k][...]).astype(BF16)
        terms_ref[(1 - core) * 2 + k] = dot(outt_ref[...], near_ref[k]).astype(BF16)


def far_kernel(t0_ref, t1_ref, far_ref, terms_ref):
    half = t0_ref.shape[0]
    for c in range(2):
        for k, t in enumerate((t0_ref, t1_ref)):
            terms_ref[c, pl.ds(k * half, half), :] = dot(t[...], far_ref[c]).astype(BF16)


def gather_kernel(t0_ref, t1_ref, both_ref, near0_ref, near1_ref, far_ref, out_ref):
    half = t0_ref.shape[0]
    core, xh = lax.axis_index("core"), lax.axis_index("xh")
    other = (1 - xh) * 4
    for c in range(2):
        out_ref[other + core * 2 + c] = far_ref[c]
        for k, t in enumerate((t0_ref, t1_ref)):
            out_ref[other + (1 - core) * 2 + c, pl.ds(k * half, half), :] = dot(t[...], both_ref[c]).astype(BF16)
    for s in range(4):
        for k, ref in enumerate((near0_ref, near1_ref)):
            out_ref[xh * 4 + s, pl.ds(k * half, half), :] = ref[s]


def first_sum_kernel(in_ref, out_ref):
    total = in_ref[0].astype(F32)
    for s in range(1, in_ref.shape[0]):
        total += in_ref[s].astype(F32)
    out_ref[...] = total.T.astype(BF16)


def last_sum_kernel(factor, in_ref, out_ref):
    total = in_ref[0].astype(F32)
    for s in range(1, in_ref.shape[0]):
        total += in_ref[s].astype(F32)
    out_ref[...] = total * factor


def after(x, *others):
    anywhere = pl.BlockSpec(memory_space=pl.ANY)
    return pl.pallas_call(
        lambda *refs: None,
        out_shape=jax.ShapeDtypeStruct(x.shape, x.dtype),
        in_specs=[anywhere] * (1 + len(others)),
        out_specs=anywhere,
        input_output_aliases={0: 0},
        compiler_params=pltpu.CompilerParams(vmem_limit_bytes=MIB),
    )(x, *others)


def ring(count, step):
    return [(i, (i + step) % count) for i in range(count)]


def on_device(fock_band, fock_slot_mask, orbital_slab, orbital_mask, result_mask):
    blocks, slots = fock_slot_mask.shape
    rows, columns = orbital_slab.shape
    size = rows // blocks
    half = columns // 2
    like = jax.ShapeDtypeStruct
    groups, wide, deep = lax.axis_size(ROWS), lax.axis_size("y"), lax.axis_size("z")
    plane = wide * deep
    piece = like((rows, half), BF16)
    h0, h1, panels = call(
        functools.partial(mask_kernel, size),
        (piece, piece, like((2, rows, half), BF16)),
        [SMEM, pl.BlockSpec(memory_space=pltpu.HBM)],
        [pltpu.VMEM((blocks, size, columns), BF16), pltpu.SemaphoreType.DMA((blocks,))],
    )(orbital_mask.T, orbital_slab)
    swap = ring(2, 1)
    low0 = lax.ppermute(h0, ROWS, ring(groups, 1))
    high0 = lax.ppermute(h0, ROWS, ring(groups, groups - 1))
    ends = [(i, (i + plane) % groups) for i in range(groups) if i % plane in (0, plane - 1)]
    crossed = lax.ppermute(h1, ROWS, ends)
    far = lax.ppermute(panels, "xh", swap)
    near_panels = lax.ppermute(panels, "core", swap)
    held, mid0, mid1, token = call(
        functools.partial(middle_kernel, size),
        (like((rows, slots * size), BF16), *[like((rows, half), F32)] * 2, like((8, size), F32)),
        [SMEM, VMEM, VMEM, VMEM],
        flops=2 * rows * rows * columns,
        moved=4 * rows * slots * size,
    )(fock_slot_mask, fock_band, h0, h1)
    up1, down1 = call(
        functools.partial(pick_kernel, (wide, deep)), (piece, piece), [VMEM, VMEM], moved=8 * rows * half
    )(h1, after(crossed, low0, high0, token))
    within = [(i, i + 1 if (i + 1) % plane else i + 1 - plane) for i in range(groups)]
    low1 = lax.ppermute(up1, ROWS, within)
    high1 = lax.ppermute(down1, ROWS, [(b, a) for a, b in within])

    def near(h, mid, low, high, *first):
        width = half if h == 0 else columns
        return call(
            functools.partial(near_kernel, size, h),
            (like((rows, width), BF16), like((half, rows), BF16), like((4, half, half), BF16)),
            [SMEM] + [VMEM] * (7 + len(first)),
            flops=2 * rows * half * (2 * columns + (slots - blocks) * size),
            moved=8 * rows * columns,
        )(result_mask.T, held, mid, low, high, h0, h1, near_panels, *first)

    product0, flipped0, terms0 = near(0, mid0, low0, high0)
    product, flipped1, terms1 = near(1, mid1, low1, high1, product0)
    far = after(far, terms1)
    both = lax.ppermute(far, "core", swap)
    far_terms = call(
        far_kernel,
        like((2, columns, half), BF16),
        [VMEM] * 3,
        flops=4 * rows * half * columns,
        moved=8 * rows * half,
    )(flipped0, flipped1, far)
    terms = call(
        gather_kernel,
        like((groups // deep, columns, half), BF16),
        [VMEM] * 6,
        flops=4 * rows * half * columns,
        moved=8 * rows * columns,
    )(flipped0, flipped1, both, terms0, terms1, far_terms)
    terms = lax.all_to_all(terms, ("xl", "y"), 0, 0, tiled=True)
    part = call(first_sum_kernel, like((half, columns), BF16), [VMEM])(terms)
    part = part.reshape(deep, half // deep, columns)
    part = lax.all_to_all(part, "z", 0, 0, tiled=True)
    factor = 1.0 / math.sqrt(rows * groups)
    projected = call(
        functools.partial(last_sum_kernel, factor), like((half // deep, columns), F32), [VMEM]
    )(part)
    return (product, projected)


def solution(mesh):
    split = Mesh(mesh.devices.reshape(2, 2, 2, 4, 8), BLK + ROWS)
    placed = (P(ROWS, None), P(ROWS, None), P(ROWS, BLK), P(ROWS, BLK), P(ROWS, BLK))
    return jax.shard_map(
        on_device,
        mesh=split,
        in_specs=placed,
        out_specs=(P(ROWS, BLK), P(ROWS, BLK)),
        check_vma=False,
    )
```

time: 114 us -> 104 us (0.912); the launches traced: 112 us -> 104 us
  starting transfers between devices: 47.5 us -> 13 us
  blocking collectives: 24.2 us -> 54.3 us
  waiting for transfers between devices: 7.84 us -> 18.4 us
  local copies, waits for them, and re-layouts: 12.3 us -> 4.85 us
  Pallas kernels: 19.3 us -> 12.7 us
    ppermute x15 -> x8, starting transfers between devices: 47.5 us -> 13 us  [the longest x1 5.82 us: on_device(): high0 = lax.ppermute(h0, ROWS, ring(groups, groups - 1))]
    all_to_all x1 -> x2, blocking collectives: 24.2 us -> 54.3 us  [the longest x1 37.2 us: on_device(): terms = lax.all_to_all(terms, ('xl', 'y'), 0, 0, tiled=True)]
    ppermute x15 -> x8, waiting for transfers between devices: 7.84 us -> 18.4 us  [the longest x1 9.06 us: on_device(): low1 = lax.ppermute(up1, ROWS, within)]
    unnamed x22 -> x10, local copies, waits for them, and re-layouts: 12.3 us -> 4.85 us
    pallas_call x4 -> x6, Pallas kernels: 8.23 us -> 4.86 us  [the longest x1 2.34 us: on_device(): call(functools.partial(mask_kernel, size), (piece, piece, like((2, rows,...]
    pallas_call x2, Pallas kernels: 7.76 us -> 5.04 us  [near(): call(functools.partial(near_kernel, size, h), (like((rows, width), BF16),...]
  transfers between devices with their start and end apart: 15 -> 8, of which waited for: 5 -> 4; matrix products, arithmetic and copies ran while one was open for 0% -> 0% of each run, Pallas kernels for 15% -> 8%
where the time goes in v3:
time: 104 us
  blocking collectives  54.3 us (52%)
  waiting for transfers between devices  18.4 us (18%)
  starting transfers between devices  13 us (12%)
  Pallas kernels  12.7 us (12%)
  local copies, waits for them, and re-layouts  4.85 us (5%)
    all_to_all x1, blocking collectives, on_device(): terms = lax.all_to_all(terms, ('xl', 'y'), 0, 0, tiled=True)  37.2 us
    all_to_all x1, blocking collectives, on_device(): part = lax.all_to_all(part, 'z', 0, 0, tiled=True)  17.1 us
    ppermute x1, waiting for transfers between devices, on_device(): low1 = lax.ppermute(up1, ROWS, within)  9.06 us
    ppermute x1, starting transfers between devices, on_device(): high0 = lax.ppermute(h0, ROWS, ring(groups, groups - 1))  5.82 us
    pallas_call x2, Pallas kernels, near(): call(functools.partial(near_kernel, size, h), (like((rows, width), BF16),...  5.04 us
    unnamed x10, local copies, waits for them, and re-layouts  4.85 us
    ppermute x1, waiting for transfers between devices, on_device(): low0 = lax.ppermute(h0, ROWS, ring(groups, 1))  4.31 us
    ppermute x1, starting transfers between devices, on_device(): high1 = lax.ppermute(down1, ROWS, [(b, a) for a, b in within])  4.12 us
  transfers between devices with their start and end apart: 8, of which 4 were waited for; matrix products, arithmetic and copies ran while one was open for 0% of the time, Pallas kernels for 8%

profile of v3, /device:TPU:10, one launch (start us, length us, event | category | flops | bytes accessed | tf_op | source)
XLA Modules:
  0.0 104.0 jit_solution(2682741648642767127)
XLA Ops:
  0.6 1.2 %copy-done.1 = bf16[1024,512]{1,0:T(8,128)(2,1)S(1)} copy-done((bf16[1024,512]{1,0:T(8,128)(2,1)S(1)}, bf16[1024,512]{1,0:T(8,128)(2,1)}, u32[]{:S(2)}) %copy-start.1) | copy-done | bytes 1048600
  1.9 0.7 copy-done.4
  2.5 2.3 %shard_map.68 = (bf16[1024,256]{1,0:T(8,128)(2,1)S(1)}, bf16[1024,256]{1,0:T(8,128)(2,1)S(1)}, bf16[2,1024,256]{2,1,0:T(8,128)(2,1)S(1)}) custom-call(s32[4,8]{1,0:T(4,128)S(1)} %bitcast.6, bf16[1024,512]{1,0:T(8,128)(2,1)S(1)} %copy-done.1), custom_call_target="tpu_custom_call" | custom-call | tf_op jit(solution)/shard_map/pallas_call | solution.py:172
  4.9 0.0 copy-start.2
  4.9 0.1 collective-permute-start.5
  5.0 5.8 %collective-permute-start.2 = (bf16[1024,256]{1,0:T(8,128)(2,1)S(1)}, bf16[1024,256]{1,0:T(8,128)(2,1)S(1)}, u32[]{:S(2)}, u32[]{:S(2)}) collective-permute-start(bf16[1024,256]{1,0:T(8,128)(2,1)S(1)} %get-tuple-element.17.h0_ref.rest_0_), channel_id=1, source_target_pairs={{0,63},{1,0},{2,1},{3,2},{4,3},{5,4},{6,5},{7,6},{8,7},{9,8},{10,9... | collective-permute-start | bytes 1572872 | tf_op jit(solution)/shard_map/ppermute | solution.py:180
  10.8 0.0 collective-permute-start.1
  10.8 0.7 collective-permute-start
  11.5 2.2 %collective-permute-start.6 = (bf16[2,1024,256]{2,1,0:T(8,128)(2,1)S(1)}, bf16[2,1024,256]{2,1,0:T(8,128)(2,1)S(1)}, u32[]{:S(2)}, u32[]{:S(2)}) collective-permute-start(bf16[2,1024,256]{2,1,0:T(8,128)(2,1)S(1)} %get-tuple-element.24), channel_id=1, source_target_pairs={{0,128},{128,0},{1,129},{129,1},{2,130},{130,2},{3,131},{131,3},{4... | collective-permute-start | bytes 3145736 | tf_op jit(solution)/shard_map/ppermute | solution.py:183
  13.7 2.3 %copy-done = bf16[1024,2176]{1,0:T(8,128)(2,1)S(1)} copy-done((bf16[1024,2176]{1,0:T(8,128)(2,1)S(1)}, bf16[1024,2176]{1,0:T(8,128)(2,1)}, u32[]{:S(2)}) %copy-start) | copy-done | bytes 4456472
  16.0 0.7 copy-done.3
  16.7 2.8 %shard_map.69 = (bf16[1024,2176]{1,0:T(8,128)(2,1)S(1)}, f32[1024,256]{1,0:T(8,128)S(1)}, f32[1024,256]{1,0:T(8,128)S(1)}, f32[8,128]{1,0:T(8,128)S(1)}) custom-call(s32[8,17]{1,0:T(8,128)S(1)} %copy-done.3, bf16[1024,2176]{1,0:T(8,128)(2,1)S(1)} %copy-done, bf16[1024,256]{1,0:T(8,128)(2,1)S(1)} %get-tuple-element.17.h0_ref.rest_0_, ...), custom_call_target="tpu_custom_call" | custom-call | flops 1073741824 | bytes 8912896 | tf_op jit(solution)/shard_map/pallas_call | solution.py:185
  19.5 3.1 %collective-permute-done.2.refs_2_.high_ref = bf16[1024,256]{1,0:T(8,128)(2,1)S(1)} collective-permute-done((bf16[1024,256]{1,0:T(8,128)(2,1)S(1)}, bf16[1024,256]{1,0:T(8,128)(2,1)S(1)}, u32[]{:S(2)}, u32[]{:S(2)}) %collective-permute-start.2) | collective-permute-done | bytes 524320 | tf_op jit(solution)/shard_map/ppermute | solution.py:180
  22.6 4.3 %collective-permute-done.1.refs_1_.low_ref = bf16[1024,256]{1,0:T(8,128)(2,1)S(1)} collective-permute-done((bf16[1024,256]{1,0:T(8,128)(2,1)S(1)}, bf16[1024,256]{1,0:T(8,128)(2,1)S(1)}, u32[]{:S(2)}, u32[]{:S(2)}) %collective-permute-start.1) | collective-permute-done | bytes 524320 | tf_op jit(solution)/shard_map/ppermute | solution.py:179
  26.9 0.0 collective-permute-done.refs_0_
  26.9 0.1 shard_map.71
  27.0 0.1 collective-permute-start.3
  27.1 4.1 %collective-permute-start.4 = (bf16[1024,256]{1,0:T(8,128)(2,1)S(1)}, bf16[1024,256]{1,0:T(8,128)(2,1)S(1)}, u32[]{:S(2)}, u32[]{:S(2)}) collective-permute-start(bf16[1024,256]{1,0:T(8,128)(2,1)S(1)} %get-tuple-element.23), channel_id=1, source_target_pairs={{1,0},{2,1},{3,2},{4,3},{5,4},{6,5},{7,6},{8,7},{9,8},{10,9},{11,1... | collective-permute-start | bytes 1572872 | tf_op jit(solution)/shard_map/ppermute | solution.py:197
  31.2 0.0 collective-permute-done.5.rest_2_
  31.2 2.1 %shard_map.72 = (bf16[1024,256]{1,0:T(8,128)(2,1)S(1)}, bf16[256,1024]{1,0:T(8,128)(2,1)S(1)}, bf16[4,256,256]{2,1,0:T(8,128)(2,1)S(1)}) custom-call(s32[4,8]{1,0:T(4,128)S(1)} %bitcast.4, bf16[1024,2176]{1,0:T(8,128)(2,1)S(1)} %get-tuple-element.19.held_ref, f32[1024,256]{1,0:T(8,128)S(1)} %get-tuple-element.25.mid_ref, ...), custom_call_target="tpu_custom_call" | custom-call | flops 1140850688 | bytes 4194304 | tf_op jit(solution)/shard_map/pallas_call | solution.py:201
  33.3 9.1 %collective-permute-done.3.low_ref = bf16[1024,256]{1,0:T(8,128)(2,1)S(1)} collective-permute-done((bf16[1024,256]{1,0:T(8,128)(2,1)S(1)}, bf16[1024,256]{1,0:T(8,128)(2,1)S(1)}, u32[]{:S(2)}, u32[]{:S(2)}) %collective-permute-start.3) | collective-permute-done | bytes 524320 | tf_op jit(solution)/shard_map/ppermute | solution.py:196
  42.3 0.0 collective-permute-done.4.high_ref
  42.3 3.0 %shard_map.73 = (bf16[1024,512]{1,0:T(8,128)(2,1)}, bf16[256,1024]{1,0:T(8,128)(2,1)S(1)}, bf16[4,256,256]{2,1,0:T(8,128)(2,1)S(1)}) custom-call(s32[4,8]{1,0:T(4,128)S(1)} %bitcast.5, bf16[1024,2176]{1,0:T(8,128)(2,1)S(1)} %get-tuple-element.19.held_ref, f32[1024,256]{1,0:T(8,128)S(1)} %get-tuple-element.20.mid_ref, ...), custom_call_target="tpu_custom_call" | custom-call | flops 1140850688 | bytes 4194304 | tf_op jit(solution)/shard_map/pallas_call | solution.py:201
  45.3 0.0 collective-permute-done.6.refs_0_
  45.3 0.0 collective-permute-start.7
  45.3 0.7 shard_map.75.far_ref
  46.1 1.9 %collective-permute-done.7.both_ref = bf16[2,1024,256]{2,1,0:T(8,128)(2,1)S(1)} collective-permute-done((bf16[2,1024,256]{2,1,0:T(8,128)(2,1)S(1)}, bf16[2,1024,256]{2,1,0:T(8,128)(2,1)S(1)}, u32[]{:S(2)}, u32[]{:S(2)}) %collective-permute-start.7) | collective-permute-done | bytes 1048608 | tf_op jit(solution)/shard_map/ppermute | solution.py:212
  48.0 0.7 shard_map.76
  48.7 37.2 %all_to_all.10.in_ref = bf16[8,512,256]{2,1,0:T(8,128)(2,1)S(1)} all-to-all(bf16[8,512,256]{2,1,0:T(8,128)(2,1)S(1)} %shard_map.76), channel_id=1, replica_groups=mesh['xh'=2,'core'=2,'xl'=2,'y'=4,'z'=8] {'xl','y'}, dimensions={0} | all-to-all | bytes 4194304 | tf_op jit(solution)/shard_map/all_to_all | solution.py:227
  85.9 0.3 shard_map.77
  86.2 17.1 %all_to_all.11.in_ref = bf16[8,32,512]{2,1,0:T(8,128)(2,1)S(1)} all-to-all(bf16[8,32,512]{2,1,0:T(8,128)(2,1)S(1)} %bitcast.3), channel_id=1, replica_groups=mesh['xh'=2,'core'=2,'xl'=2,'y'=4,'z'=8] {'z'}, dimensions={0} | all-to-all | bytes 524288 | tf_op jit(solution)/shard_map/all_to_all | solution.py:230
  103.4 0.7 shard_map.78
  (7 shorter events, 0.0 us)
Async XLA Ops:
  0.6 1.2 %copy-start.1 = (bf16[1024,512]{1,0:T(8,128)(2,1)S(1)}, bf16[1024,512]{1,0:T(8,128)(2,1)}, u32[]{:S(2)}) copy-start(bf16[1024,512]{1,0:T(8,128)(2,1)} %slab_hbm.1) | copy-start | bytes 3145732
  1.9 0.7 copy-start.4
  4.9 26.3 %copy-start.2 = (s32[8,4]{0,1:T(4,128)S(1)}, s32[8,4]{0,1:T(4,128)}, u32[]{:S(2)}) copy-start(s32[8,4]{0,1:T(4,128)} %param.9) | copy-start | bytes 388
  4.9 26.3 %collective-permute-start.5 = (bf16[2,1024,256]{2,1,0:T(8,128)(2,1)S(1)}, bf16[2,1024,256]{2,1,0:T(8,128)(2,1)S(1)}, u32[]{:S(2)}, u32[]{:S(2)}) collective-permute-start(bf16[2,1024,256]{2,1,0:T(8,128)(2,1)S(1)} %get-tuple-element.24), channel_id=1, source_target_pairs={{0,64},{64,0},{1,65},{65,1},{2,66},{66,2},{3,67},{67,3},{4,68},{68... | collective-permute-start | bytes 3145736 | tf_op jit(solution)/shard_map/ppermute | solution.py:184
  5.0 17.6 %collective-permute-start.2 = (bf16[1024,256]{1,0:T(8,128)(2,1)S(1)}, bf16[1024,256]{1,0:T(8,128)(2,1)S(1)}, u32[]{:S(2)}, u32[]{:S(2)}) collective-permute-start(bf16[1024,256]{1,0:T(8,128)(2,1)S(1)} %get-tuple-element.17.h0_ref.rest_0_), channel_id=1, source_target_pairs={{0,63},{1,0},{2,1},{3,2},{4,3},{5,4},{6,5},{7,6},{8,7},{9,8},{10,9... | collective-permute-start | bytes 1572872 | tf_op jit(solution)/shard_map/ppermute | solution.py:180
  10.8 16.1 %collective-permute-start.1 = (bf16[1024,256]{1,0:T(8,128)(2,1)S(1)}, bf16[1024,256]{1,0:T(8,128)(2,1)S(1)}, u32[]{:S(2)}, u32[]{:S(2)}) collective-permute-start(bf16[1024,256]{1,0:T(8,128)(2,1)S(1)} %get-tuple-element.17.h0_ref.rest_0_), channel_id=1, source_target_pairs={{0,1},{1,2},{2,3},{3,4},{4,5},{5,6},{6,7},{7,8},{8,9},{9,10},{10,1... | collective-permute-start | bytes 1572872 | tf_op jit(solution)/shard_map/ppermute | solution.py:179
  10.8 16.1 %collective-permute-start = (bf16[1024,256]{1,0:T(8,128)(2,1)S(1)}, bf16[1024,256]{1,0:T(8,128)(2,1)S(1)}, u32[]{:S(2)}, u32[]{:S(2)}) collective-permute-start(bf16[1024,256]{1,0:T(8,128)(2,1)S(1)} %get-tuple-element.18.h1_ref.own_ref.rest_1_), channel_id=1, source_target_pairs={{0,32},{31,63},{32,0},{63,31},{64,96},{95,127},{96,64},{127,95},{1... | collective-permute-start | bytes 1572872 | tf_op jit(solution)/shard_map/ppermute | solution.py:182
  11.5 33.8 %collective-permute-start.6 = (bf16[2,1024,256]{2,1,0:T(8,128)(2,1)S(1)}, bf16[2,1024,256]{2,1,0:T(8,128)(2,1)S(1)}, u32[]{:S(2)}, u32[]{:S(2)}) collective-permute-start(bf16[2,1024,256]{2,1,0:T(8,128)(2,1)S(1)} %get-tuple-element.24), channel_id=1, source_target_pairs={{0,128},{128,0},{1,129},{129,1},{2,130},{130,2},{3,131},{131,3},{4... | collective-permute-start | bytes 3145736 | tf_op jit(solution)/shard_map/ppermute | solution.py:183
  13.7 2.3 %copy-start = (bf16[1024,2176]{1,0:T(8,128)(2,1)S(1)}, bf16[1024,2176]{1,0:T(8,128)(2,1)}, u32[]{:S(2)}) copy-start(bf16[1024,2176]{1,0:T(8,128)(2,1)} %fock_ref.1) | copy-start | bytes 13369348
  16.0 0.7 copy-start.3
  27.0 15.3 %collective-permute-start.3 = (bf16[1024,256]{1,0:T(8,128)(2,1)S(1)}, bf16[1024,256]{1,0:T(8,128)(2,1)S(1)}, u32[]{:S(2)}, u32[]{:S(2)}) collective-permute-start(bf16[1024,256]{1,0:T(8,128)(2,1)S(1)} %get-tuple-element.22), channel_id=1, source_target_pairs={{0,1},{1,2},{2,3},{3,4},{4,5},{5,6},{6,7},{7,8},{8,9},{9,10},{10,1... | collective-permute-start | bytes 1572872 | tf_op jit(solution)/shard_map/ppermute | solution.py:196
  27.1 15.3 %collective-permute-start.4 = (bf16[1024,256]{1,0:T(8,128)(2,1)S(1)}, bf16[1024,256]{1,0:T(8,128)(2,1)S(1)}, u32[]{:S(2)}, u32[]{:S(2)}) collective-permute-start(bf16[1024,256]{1,0:T(8,128)(2,1)S(1)} %get-tuple-element.23), channel_id=1, source_target_pairs={{1,0},{2,1},{3,2},{4,3},{5,4},{6,5},{7,6},{8,7},{9,8},{10,9},{11,1... | collective-permute-start | bytes 1572872 | tf_op jit(solution)/shard_map/ppermute | solution.py:197
  45.3 2.7 %collective-permute-start.7 = (bf16[2,1024,256]{2,1,0:T(8,128)(2,1)S(1)}, bf16[2,1024,256]{2,1,0:T(8,128)(2,1)S(1)}, u32[]{:S(2)}, u32[]{:S(2)}) collective-permute-start(bf16[2,1024,256]{2,1,0:T(8,128)(2,1)S(1)} %shard_map.74.far_ref), channel_id=1, source_target_pairs={{0,64},{64,0},{1,65},{65,1},{2,66},{66,2},{3,67},{67,3},{4,68},{68... | collective-permute-start | bytes 3145736 | tf_op jit(solution)/shard_map/ppermute | solution.py:212

commit v4 on v3

--- a/solution.py
+++ b/solution.py
@@ -13,15 +13,16 @@
 BLK = ("xh", "core")
 VMEM = pl.BlockSpec(memory_space=pltpu.VMEM)
 SMEM = pl.BlockSpec(memory_space=pltpu.SMEM)
+HBM = pl.BlockSpec(memory_space=pltpu.HBM)
 MIB = 1 << 20
 
 
-def call(body, outs, ins, scratch=(), limit=8 * MIB, flops=0, moved=0):
+def call(body, outs, ins, scratch=(), limit=8 * MIB, flops=0, moved=0, place=VMEM):
     return pl.pallas_call(
         body,
         out_shape=outs,
         in_specs=ins,
-        out_specs=jax.tree.map(lambda _: VMEM, outs),
+        out_specs=jax.tree.map(lambda _: place, outs),
         scratch_shapes=list(scratch),
         compiler_params=pltpu.CompilerParams(vmem_limit_bytes=limit),
         cost_estimate=pl.CostEstimate(flops=flops, bytes_accessed=moved, transcendentals=0),
@@ -32,28 +33,30 @@
     return jnp.dot(a, b, preferred_element_type=F32)
 
 
-def mask_kernel(size, mask_ref, slab_hbm, h0_ref, h1_ref, both_ref, held, sems):
+def mask_kernel(size, mask_ref, slab_hbm, h0_hbm, h1_hbm, both_hbm, loaded, kept, in_sems, out_sems):
     panels, blocks = mask_ref.shape
     half = panels // 2
-    copies = [
-        pltpu.make_async_copy(slab_hbm.at[pl.ds(i * size, size)], held.at[i], sems.at[i])
-        for i in range(blocks)
-    ]
-    for copy in copies:
-        copy.start()
-    for i, copy in enumerate(copies):
-        copy.wait()
-        rows = pl.ds(i * size, size)
+    at = [pl.ds(i * size, size) for i in range(blocks)]
+    loads = [pltpu.make_async_copy(slab_hbm.at[at[i]], loaded.at[at[i]], in_sems.at[i]) for i in range(blocks)]
+    for load in loads:
+        load.start()
+    stores = []
+    for i, load in enumerate(loads):
+        load.wait()
         for j in range(panels):
-            ref = (h0_ref, h1_ref)[j // half]
-            tile = held[i, :, j * size : (j + 1) * size]
+            tile = loaded[at[i], pl.ds(j * size, size)]
             tile = jnp.where(mask_ref[j, i] != 0, tile, jnp.zeros_like(tile))
-            ref[rows, pl.ds((j % half) * size, size)] = tile
-            both_ref[j // half, rows, pl.ds((j % half) * size, size)] = tile
-
-
-def middle_kernel(size, fmask_ref, fock_ref, h0_ref, h1_ref, held_ref, m0_ref, m1_ref, token_ref):
-    token_ref[...] = jnp.zeros_like(token_ref)
+            kept[j // half, at[i], pl.ds((j % half) * size, size)] = tile
+        for h, ref in enumerate((h0_hbm, h1_hbm)):
+            stores.append(pltpu.make_async_copy(kept.at[h, at[i]], ref.at[at[i]], out_sems.at[i, 2 * h]))
+            stores.append(pltpu.make_async_copy(kept.at[h, at[i]], both_hbm.at[h, at[i]], out_sems.at[i, 2 * h + 1]))
+        for store in stores[-4:]:
+            store.start()
+    for store in stores:
+        store.wait()
+
+
+def middle_kernel(size, fmask_ref, fock_ref, h0_ref, h1_ref, held_ref, m0_ref, m1_ref):
     blocks, slots = fmask_ref.shape
     for i in range(blocks):
         rows = pl.ds(i * size, size)
@@ -172,8 +175,15 @@
     h0, h1, panels = call(
         functools.partial(mask_kernel, size),
         (piece, piece, like((2, rows, half), BF16)),
-        [SMEM, pl.BlockSpec(memory_space=pltpu.HBM)],
-        [pltpu.VMEM((blocks, size, columns), BF16), pltpu.SemaphoreType.DMA((blocks,))],
+        [SMEM, HBM],
+        [
+            pltpu.VMEM((rows, columns), BF16),
+            pltpu.VMEM((2, rows, half), BF16),
+            pltpu.SemaphoreType.DMA((blocks,)),
+            pltpu.SemaphoreType.DMA((blocks, 4)),
+        ],
+        limit=60 * MIB,
+        place=HBM,
     )(orbital_mask.T, orbital_slab)
     swap = ring(2, 1)
     low0 = lax.ppermute(h0, ROWS, ring(groups, 1))
@@ -182,16 +192,16 @@
     crossed = lax.ppermute(h1, ROWS, ends)
     far = lax.ppermute(panels, "xh", swap)
     near_panels = lax.ppermute(panels, "core", swap)
-    held, mid0, mid1, token = call(
+    held, mid0, mid1 = call(
         functools.partial(middle_kernel, size),
-        (like((rows, slots * size), BF16), *[like((rows, half), F32)] * 2, like((8, size), F32)),
+        (like((rows, slots * size), BF16), *[like((rows, half), F32)] * 2),
         [SMEM, VMEM, VMEM, VMEM],
         flops=2 * rows * rows * columns,
         moved=4 * rows * slots * size,
     )(fock_slot_mask, fock_band, h0, h1)
     up1, down1 = call(
         functools.partial(pick_kernel, (wide, deep)), (piece, piece), [VMEM, VMEM], moved=8 * rows * half
-    )(h1, after(crossed, low0, high0, token))
+    )(h1, after(crossed, near_panels))
     within = [(i, i + 1 if (i + 1) % plane else i + 1 - plane) for i in range(groups)]
     low1 = lax.ppermute(up1, ROWS, within)
     high1 = lax.ppermute(down1, ROWS, [(b, a) for a, b in within])

time: 104 us -> 98.3 us (0.945)
  waiting for transfers between devices: 18.4 us -> 14 us
  blocking collectives: 54.3 us -> 50.6 us
  local copies, waits for them, and re-layouts: 4.85 us -> 6.07 us
    ppermute x1, waiting for transfers between devices: 3.11 us -> 0.01 us  [on_device(): high0 = lax.ppermute(h0, ROWS, ring(groups, groups - 1))]
    all_to_all x1, blocking collectives: 17.1 us -> 14.5 us  [on_device(): part = lax.all_to_all(part, 'z', 0, 0, tiled=True)]
    unnamed x10 -> x12, local copies, waits for them, and re-layouts: 4.85 us -> 6.07 us
    all_to_all x1, blocking collectives: 37.2 us -> 36 us  [on_device(): terms = lax.all_to_all(terms, ('xl', 'y'), 0, 0, tiled=True)]
  transfers between devices with their start and end apart: 8 -> 8, of which waited for: 4 -> 3; matrix products, arithmetic and copies ran while one was open for 0% -> 0% of each run, Pallas kernels for 8% -> 9%
where the time goes in v4:
time: 98.3 us; the launch traced here: 97.9 us
  blocking collectives  50.6 us (51%)
  waiting for transfers between devices  14 us (14%)
  Pallas kernels  13.5 us (14%)
  starting transfers between devices  13 us (13%)
  local copies, waits for them, and re-layouts  6.07 us (6%)
    all_to_all x1, blocking collectives, on_device(): terms = lax.all_to_all(terms, ('xl', 'y'), 0, 0, tiled=True)  36 us
    all_to_all x1, blocking collectives, on_device(): part = lax.all_to_all(part, 'z', 0, 0, tiled=True)  14.5 us
    ppermute x1, waiting for transfers between devices, on_device(): low1 = lax.ppermute(up1, ROWS, within)  8.19 us
    unnamed x12, local copies, waits for them, and re-layouts  6.07 us
    ppermute x1, starting transfers between devices, on_device(): high0 = lax.ppermute(h0, ROWS, ring(groups, groups - 1))  5.74 us
    pallas_call x2, Pallas kernels, near(): call(functools.partial(near_kernel, size, h), (like((rows, width), BF16),...  4.92 us
    ppermute x1, starting transfers between devices, on_device(): high1 = lax.ppermute(down1, ROWS, [(b, a) for a, b in within])  4.2 us
    ppermute x1, waiting for transfers between devices, on_device(): low0 = lax.ppermute(h0, ROWS, ring(groups, 1))  3.84 us
  transfers between devices with their start and end apart: 8, of which 3 were waited for; matrix products, arithmetic and copies ran while one was open for 0% of the time, Pallas kernels for 9%

profile of v4, /device:TPU:10, one launch (start us, length us, event | category | flops | bytes accessed | tf_op | source)
XLA Modules:
  0.0 97.9 jit_solution(5307070890740637444)
XLA Ops:
  0.6 3.2 %shard_map.68 = (bf16[1024,256]{1,0:T(8,128)(2,1)}, bf16[1024,256]{1,0:T(8,128)(2,1)}, bf16[2,1024,256]{2,1,0:T(8,128)(2,1)}) custom-call(s32[4,8]{1,0:T(4,128)} %bitcast.6, bf16[1024,512]{1,0:T(8,128)(2,1)} %slab_hbm.1), custom_call_target="tpu_custom_call" | custom-call | tf_op jit(solution)/shard_map/pallas_call | solution.py:175
  3.9 0.0 copy-start.4
  3.9 0.1 collective-permute-start.1
  4.0 0.7 collective-permute-start
  4.7 2.2 %collective-permute-start.6 = (bf16[2,1024,256]{2,1,0:T(8,128)(2,1)}, bf16[2,1024,256]{2,1,0:T(8,128)(2,1)S(1)}, u32[]{:S(2)}, u32[]{:S(2)}) collective-permute-start(bf16[2,1024,256]{2,1,0:T(8,128)(2,1)} %get-tuple-element.20), channel_id=1, source_target_pairs={{0,128},{128,0},{1,129},{129,1},{2,130},{130,2},{3,131},{131,3},{4... | collective-permute-start | bytes 3145736 | tf_op jit(solution)/shard_map/ppermute | solution.py:193
  6.9 5.7 %collective-permute-start.5 = (bf16[1024,256]{1,0:T(8,128)(2,1)}, bf16[1024,256]{1,0:T(8,128)(2,1)S(1)}, u32[]{:S(2)}, u32[]{:S(2)}) collective-permute-start(bf16[1024,256]{1,0:T(8,128)(2,1)} %get-tuple-element.16.h0_ref.rest_0_), channel_id=1, source_target_pairs={{0,63},{1,0},{2,1},{3,2},{4,3},{5,4},{6,5},{7,6},{8,7},{9,8},{10,9... | collective-permute-start | bytes 1572872 | tf_op jit(solution)/shard_map/ppermute | solution.py:190
  12.7 0.0 collective-permute-start.4
  12.7 0.0 collective-permute-done.refs_0_
  12.7 0.0 collective-permute-done.1.refs_1_.rest_2_
  12.7 1.0 %copy-done = bf16[1024,256]{1,0:T(8,128)(2,1)S(1)} copy-done((bf16[1024,256]{1,0:T(8,128)(2,1)S(1)}, bf16[1024,256]{1,0:T(8,128)(2,1)}, u32[]{:S(2)}) %copy-start) | copy-done | bytes 524312
  13.7 0.1 shard_map.71
  13.8 0.1 collective-permute-start.2
  13.9 4.2 %collective-permute-start.3 = (bf16[1024,256]{1,0:T(8,128)(2,1)S(1)}, bf16[1024,256]{1,0:T(8,128)(2,1)S(1)}, u32[]{:S(2)}, u32[]{:S(2)}) collective-permute-start(bf16[1024,256]{1,0:T(8,128)(2,1)S(1)} %get-tuple-element.22), channel_id=1, source_target_pairs={{1,0},{2,1},{3,2},{4,3},{5,4},{6,5},{7,6},{8,7},{9,8},{10,9},{11,1... | collective-permute-start | bytes 1572872 | tf_op jit(solution)/shard_map/ppermute | solution.py:207
  18.1 1.0 %copy-done.1 = bf16[1024,256]{1,0:T(8,128)(2,1)S(1)} copy-done((bf16[1024,256]{1,0:T(8,128)(2,1)S(1)}, bf16[1024,256]{1,0:T(8,128)(2,1)}, u32[]{:S(2)}) %copy-start.1) | copy-done | bytes 524312
  19.1 1.0 %copy-done.2 = bf16[1024,256]{1,0:T(8,128)(2,1)S(1)} copy-done((bf16[1024,256]{1,0:T(8,128)(2,1)S(1)}, bf16[1024,256]{1,0:T(8,128)(2,1)}, u32[]{:S(2)}) %copy-start.2) | copy-done | bytes 524312
  20.2 2.3 %copy-done.3 = bf16[1024,2176]{1,0:T(8,128)(2,1)S(1)} copy-done((bf16[1024,2176]{1,0:T(8,128)(2,1)S(1)}, bf16[1024,2176]{1,0:T(8,128)(2,1)}, u32[]{:S(2)}) %copy-start.3) | copy-done | bytes 4456472
  22.4 0.7 copy-done.5
  23.1 2.8 %shard_map.69 = (bf16[1024,2176]{1,0:T(8,128)(2,1)S(1)}, f32[1024,256]{1,0:T(8,128)S(1)}, f32[1024,256]{1,0:T(8,128)S(1)}) custom-call(s32[8,17]{1,0:T(8,128)S(1)} %copy-done.5, bf16[1024,2176]{1,0:T(8,128)(2,1)S(1)} %copy-done.3, bf16[1024,256]{1,0:T(8,128)(2,1)S(1)} %copy-done.2, bf16[1024,256]{1,0:T(8,128)(2,1)S(1)} %copy-done.1), custom_call_target="tpu_custom_call" | custom-call | flops 1073741824 | bytes 8912896 | tf_op jit(solution)/shard_map/pallas_call | solution.py:195
  25.9 0.0 collective-permute-done.5.high_ref
  25.9 3.8 %collective-permute-done.4.low_ref = bf16[1024,256]{1,0:T(8,128)(2,1)S(1)} collective-permute-done((bf16[1024,256]{1,0:T(8,128)(2,1)}, bf16[1024,256]{1,0:T(8,128)(2,1)S(1)}, u32[]{:S(2)}, u32[]{:S(2)}) %collective-permute-start.4) | collective-permute-done | bytes 524320 | tf_op jit(solution)/shard_map/ppermute | solution.py:189
  29.8 2.0 %shard_map.72 = (bf16[1024,256]{1,0:T(8,128)(2,1)S(1)}, bf16[256,1024]{1,0:T(8,128)(2,1)S(1)}, bf16[4,256,256]{2,1,0:T(8,128)(2,1)S(1)}) custom-call(s32[4,8]{1,0:T(4,128)S(1)} %bitcast.4, bf16[1024,2176]{1,0:T(8,128)(2,1)S(1)} %get-tuple-element.18.held_ref, f32[1024,256]{1,0:T(8,128)S(1)} %get-tuple-element.23.mid_ref, ...), custom_call_target="tpu_custom_call" | custom-call | flops 1140850688 | bytes 4194304 | tf_op jit(solution)/shard_map/pallas_call | solution.py:211
  31.8 8.2 %collective-permute-done.2.low_ref = bf16[1024,256]{1,0:T(8,128)(2,1)S(1)} collective-permute-done((bf16[1024,256]{1,0:T(8,128)(2,1)S(1)}, bf16[1024,256]{1,0:T(8,128)(2,1)S(1)}, u32[]{:S(2)}, u32[]{:S(2)}) %collective-permute-start.2) | collective-permute-done | bytes 524320 | tf_op jit(solution)/shard_map/ppermute | solution.py:206
  40.0 0.0 collective-permute-done.3.high_ref
  40.0 2.9 %shard_map.73 = (bf16[1024,512]{1,0:T(8,128)(2,1)}, bf16[256,1024]{1,0:T(8,128)(2,1)S(1)}, bf16[4,256,256]{2,1,0:T(8,128)(2,1)S(1)}) custom-call(s32[4,8]{1,0:T(4,128)S(1)} %bitcast.5, bf16[1024,2176]{1,0:T(8,128)(2,1)S(1)} %get-tuple-element.18.held_ref, f32[1024,256]{1,0:T(8,128)S(1)} %get-tuple-element.19.mid_ref, ...), custom_call_target="tpu_custom_call" | custom-call | flops 1140850688 | bytes 4194304 | tf_op jit(solution)/shard_map/pallas_call | solution.py:211
  42.9 0.0 collective-permute-done.6.refs_0_
  42.9 0.7 shard_map.75.far_ref
  43.6 1.9 %collective-permute-done.7.both_ref = bf16[2,1024,256]{2,1,0:T(8,128)(2,1)S(1)} collective-permute-done((bf16[2,1024,256]{2,1,0:T(8,128)(2,1)S(1)}, bf16[2,1024,256]{2,1,0:T(8,128)(2,1)S(1)}, u32[]{:S(2)}, u32[]{:S(2)}) %collective-permute-start.7) | collective-permute-done | bytes 1048608 | tf_op jit(solution)/shard_map/ppermute | solution.py:222
  45.6 0.7 shard_map.76
  46.3 36.0 %all_to_all.10.in_ref = bf16[8,512,256]{2,1,0:T(8,128)(2,1)S(1)} all-to-all(bf16[8,512,256]{2,1,0:T(8,128)(2,1)S(1)} %shard_map.76), channel_id=1, replica_groups=mesh['xh'=2,'core'=2,'xl'=2,'y'=4,'z'=8] {'xl','y'}, dimensions={0} | all-to-all | bytes 4194304 | tf_op jit(solution)/shard_map/all_to_all | solution.py:237
  82.3 0.3 shard_map.77
  82.7 14.5 %all_to_all.11.in_ref = bf16[8,32,512]{2,1,0:T(8,128)(2,1)S(1)} all-to-all(bf16[8,32,512]{2,1,0:T(8,128)(2,1)S(1)} %bitcast.3), channel_id=1, replica_groups=mesh['xh'=2,'core'=2,'xl'=2,'y'=4,'z'=8] {'z'}, dimensions={0} | all-to-all | bytes 524288 | tf_op jit(solution)/shard_map/all_to_all | solution.py:240
  97.2 0.7 shard_map.78
  (9 shorter events, 0.0 us)
Async XLA Ops:
  3.9 25.9 %copy-start.4 = (s32[8,4]{0,1:T(4,128)S(1)}, s32[8,4]{0,1:T(4,128)}, u32[]{:S(2)}) copy-start(s32[8,4]{0,1:T(4,128)} %param.9) | copy-start | bytes 388
  3.9 8.8 %collective-permute-start.1 = (bf16[2,1024,256]{2,1,0:T(8,128)(2,1)}, bf16[2,1024,256]{2,1,0:T(8,128)(2,1)S(1)}, u32[]{:S(2)}, u32[]{:S(2)}) collective-permute-start(bf16[2,1024,256]{2,1,0:T(8,128)(2,1)} %get-tuple-element.20), channel_id=1, source_target_pairs={{0,64},{64,0},{1,65},{65,1},{2,66},{66,2},{3,67},{67,3},{4,68},{68... | collective-permute-start | bytes 3145736 | tf_op jit(solution)/shard_map/ppermute | solution.py:194
  4.0 8.7 %collective-permute-start = (bf16[1024,256]{1,0:T(8,128)(2,1)}, bf16[1024,256]{1,0:T(8,128)(2,1)S(1)}, u32[]{:S(2)}, u32[]{:S(2)}) collective-permute-start(bf16[1024,256]{1,0:T(8,128)(2,1)} %get-tuple-element.17.h1_ref.own_ref.rest_1_), channel_id=1, source_target_pairs={{0,32},{31,63},{32,0},{63,31},{64,96},{95,127},{96,64},{127,95},{1... | collective-permute-start | bytes 1572872 | tf_op jit(solution)/shard_map/ppermute | solution.py:192
  4.7 38.2 %collective-permute-start.6 = (bf16[2,1024,256]{2,1,0:T(8,128)(2,1)}, bf16[2,1024,256]{2,1,0:T(8,128)(2,1)S(1)}, u32[]{:S(2)}, u32[]{:S(2)}) collective-permute-start(bf16[2,1024,256]{2,1,0:T(8,128)(2,1)} %get-tuple-element.20), channel_id=1, source_target_pairs={{0,128},{128,0},{1,129},{129,1},{2,130},{130,2},{3,131},{131,3},{4... | collective-permute-start | bytes 3145736 | tf_op jit(solution)/shard_map/ppermute | solution.py:193
  6.9 19.0 %collective-permute-start.5 = (bf16[1024,256]{1,0:T(8,128)(2,1)}, bf16[1024,256]{1,0:T(8,128)(2,1)S(1)}, u32[]{:S(2)}, u32[]{:S(2)}) collective-permute-start(bf16[1024,256]{1,0:T(8,128)(2,1)} %get-tuple-element.16.h0_ref.rest_0_), channel_id=1, source_target_pairs={{0,63},{1,0},{2,1},{3,2},{4,3},{5,4},{6,5},{7,6},{8,7},{9,8},{10,9... | collective-permute-start | bytes 1572872 | tf_op jit(solution)/shard_map/ppermute | solution.py:190
  12.7 17.1 %collective-permute-start.4 = (bf16[1024,256]{1,0:T(8,128)(2,1)}, bf16[1024,256]{1,0:T(8,128)(2,1)S(1)}, u32[]{:S(2)}, u32[]{:S(2)}) collective-permute-start(bf16[1024,256]{1,0:T(8,128)(2,1)} %get-tuple-element.16.h0_ref.rest_0_), channel_id=1, source_target_pairs={{0,1},{1,2},{2,3},{3,4},{4,5},{5,6},{6,7},{7,8},{8,9},{9,10},{10,1... | collective-permute-start | bytes 1572872 | tf_op jit(solution)/shard_map/ppermute | solution.py:189
  12.7 1.0 %copy-start = (bf16[1024,256]{1,0:T(8,128)(2,1)S(1)}, bf16[1024,256]{1,0:T(8,128)(2,1)}, u32[]{:S(2)}) copy-start(bf16[1024,256]{1,0:T(8,128)(2,1)} %get-tuple-element.17.h1_ref.own_ref.rest_1_) | copy-start | bytes 1572868
  13.8 26.2 %collective-permute-start.2 = (bf16[1024,256]{1,0:T(8,128)(2,1)S(1)}, bf16[1024,256]{1,0:T(8,128)(2,1)S(1)}, u32[]{:S(2)}, u32[]{:S(2)}) collective-permute-start(bf16[1024,256]{1,0:T(8,128)(2,1)S(1)} %get-tuple-element.21), channel_id=1, source_target_pairs={{0,1},{1,2},{2,3},{3,4},{4,5},{5,6},{6,7},{7,8},{8,9},{9,10},{10,1... | collective-permute-start | bytes 1572872 | tf_op jit(solution)/shard_map/ppermute | solution.py:206
  13.9 26.1 %collective-permute-start.3 = (bf16[1024,256]{1,0:T(8,128)(2,1)S(1)}, bf16[1024,256]{1,0:T(8,128)(2,1)S(1)}, u32[]{:S(2)}, u32[]{:S(2)}) collective-permute-start(bf16[1024,256]{1,0:T(8,128)(2,1)S(1)} %get-tuple-element.22), channel_id=1, source_target_pairs={{1,0},{2,1},{3,2},{4,3},{5,4},{6,5},{7,6},{8,7},{9,8},{10,9},{11,1... | collective-permute-start | bytes 1572872 | tf_op jit(solution)/shard_map/ppermute | solution.py:207
  18.1 1.0 %copy-start.1 = (bf16[1024,256]{1,0:T(8,128)(2,1)S(1)}, bf16[1024,256]{1,0:T(8,128)(2,1)}, u32[]{:S(2)}) copy-start(bf16[1024,256]{1,0:T(8,128)(2,1)} %get-tuple-element.17.h1_ref.own_ref.rest_1_) | copy-start | bytes 1572868
  19.1 1.0 %copy-start.2 = (bf16[1024,256]{1,0:T(8,128)(2,1)S(1)}, bf16[1024,256]{1,0:T(8,128)(2,1)}, u32[]{:S(2)}) copy-start(bf16[1024,256]{1,0:T(8,128)(2,1)} %get-tuple-element.16.h0_ref.rest_0_) | copy-start | bytes 1572868
  20.2 2.3 %copy-start.3 = (bf16[1024,2176]{1,0:T(8,128)(2,1)S(1)}, bf16[1024,2176]{1,0:T(8,128)(2,1)}, u32[]{:S(2)}) copy-start(bf16[1024,2176]{1,0:T(8,128)(2,1)} %fock_ref.1) | copy-start | bytes 13369348
  22.4 0.7 copy-start.5
  42.9 2.7 %collective-permute-start.7 = (bf16[2,1024,256]{2,1,0:T(8,128)(2,1)S(1)}, bf16[2,1024,256]{2,1,0:T(8,128)(2,1)S(1)}, u32[]{:S(2)}, u32[]{:S(2)}) collective-permute-start(bf16[2,1024,256]{2,1,0:T(8,128)(2,1)S(1)} %shard_map.74.far_ref), channel_id=1, source_target_pairs={{0,64},{64,0},{1,65},{65,1},{2,66},{66,2},{3,67},{67,3},{4,68},{68... | collective-permute-start | bytes 3145736 | tf_op jit(solution)/shard_map/ppermute | solution.py:222

commit v5 on v4

--- a/solution.py
+++ b/solution.py
@@ -83,15 +83,16 @@
             ref[...] = own_ref[...]
 
 
-def near_kernel(size, h, rmask_ref, held_ref, mid_ref, low_ref, high_ref, *rest):
-    own_refs, near_ref, rest = rest[:2], rest[2], rest[3:]
+def near_kernel(size, h, rmask_ref, held_ref, mid_ref, low_ref, high_ref, own0_ref, own1_ref, near_ref, *rest):
     start = 0
     if h == 1:
-        first_ref, rest = rest[0], rest[1:]
+        (first_ref, *earlier), rest = rest[:5], rest[5:]
         start = first_ref.shape[1]
-    out_ref, outt_ref, terms_ref = rest
+    out_ref, outt_ref, *to = rest
     if h == 1:
         out_ref[:, :start] = first_ref[...]
+        for ref, part in zip(to, earlier):
+            ref[:start, :] = part[...]
     blocks = rmask_ref.shape[1]
     slots = held_ref.shape[1] // size
     panels = mid_ref.shape[1] // size
@@ -107,37 +108,41 @@
             tile = jnp.where(keep, tile, jnp.zeros_like(tile)).astype(BF16)
             out_ref[rows, pl.ds(start + j * size, size)] = tile
             outt_ref[cols, rows] = tile.T
-    core = lax.axis_index("core")
-    for k in range(2):
-        terms_ref[core * 2 + k] = dot(outt_ref[...], own_refs[k][...]).astype(BF16)
-        terms_ref[(1 - core) * 2 + k] = dot(outt_ref[...], near_ref[k]).astype(BF16)
-
-
-def far_kernel(t0_ref, t1_ref, far_ref, terms_ref):
+    project(outt_ref, ((own0_ref, own1_ref), (near_ref.at[0], near_ref.at[1])), [ref.at[pl.ds(start, outt_ref.shape[0]), :] for ref in to])
+
+
+def project(outt_ref, panels, to):
+    core, y = lax.axis_index("core"), lax.axis_index("y")
+    for q, halves in enumerate(panels):
+        for k, ref in enumerate(halves):
+            terms = dot(outt_ref[...], ref[...])
+            step = lax.rem((core ^ q) * 2 + k - y + 4, 4)
+            for s, into in enumerate(to):
+
+                @pl.when(step == s)
+                def _():
+                    into[...] = terms.astype(into.dtype)
+
+
+def far_kernel(t0_ref, t1_ref, far_ref, both_ref, *to):
     half = t0_ref.shape[0]
-    for c in range(2):
-        for k, t in enumerate((t0_ref, t1_ref)):
-            terms_ref[c, pl.ds(k * half, half), :] = dot(t[...], far_ref[c]).astype(BF16)
-
-
-def gather_kernel(t0_ref, t1_ref, both_ref, near0_ref, near1_ref, far_ref, out_ref):
-    half = t0_ref.shape[0]
-    core, xh = lax.axis_index("core"), lax.axis_index("xh")
-    other = (1 - xh) * 4
-    for c in range(2):
-        out_ref[other + core * 2 + c] = far_ref[c]
-        for k, t in enumerate((t0_ref, t1_ref)):
-            out_ref[other + (1 - core) * 2 + c, pl.ds(k * half, half), :] = dot(t[...], both_ref[c]).astype(BF16)
-    for s in range(4):
-        for k, ref in enumerate((near0_ref, near1_ref)):
-            out_ref[xh * 4 + s, pl.ds(k * half, half), :] = ref[s]
-
-
-def first_sum_kernel(in_ref, out_ref):
-    total = in_ref[0].astype(F32)
-    for s in range(1, in_ref.shape[0]):
-        total += in_ref[s].astype(F32)
-    out_ref[...] = total.T.astype(BF16)
+    panels = [(ref.at[0], ref.at[1]) for ref in (far_ref, both_ref)]
+    for k, t in enumerate((t0_ref, t1_ref)):
+        project(t, panels, [ref.at[pl.ds(k * half, half), :] for ref in to])
+
+
+def first_sum_kernel(*refs):
+    out_ref = refs[-1]
+    count, deep, _ = out_ref.shape
+    inner = count // 2
+    xh = lax.axis_index("xh")
+    for f, parts in enumerate((refs[:4], refs[4:8])):
+        total = parts[0][...]
+        for part in parts[1:]:
+            total += part[...].astype(F32)
+        turned = total.T.astype(BF16)
+        for z in range(inner):
+            out_ref[(xh ^ f) * inner + z] = turned[z * deep : (z + 1) * deep]
 
 
 def last_sum_kernel(factor, in_ref, out_ref):
@@ -206,38 +211,38 @@
     low1 = lax.ppermute(up1, ROWS, within)
     high1 = lax.ppermute(down1, ROWS, [(b, a) for a, b in within])
 
+    own, long = like((columns, half), F32), like((columns, half), BF16)
+    square = [like((half, half), kind) for kind in (F32, BF16, BF16, BF16)]
+
     def near(h, mid, low, high, *first):
-        width = half if h == 0 else columns
         return call(
             functools.partial(near_kernel, size, h),
-            (like((rows, width), BF16), like((half, rows), BF16), like((4, half, half), BF16)),
+            (like((rows, half * (h + 1)), BF16), like((half, rows), BF16), *(square, (own, long, long, long))[h]),
             [SMEM] + [VMEM] * (7 + len(first)),
             flops=2 * rows * half * (2 * columns + (slots - blocks) * size),
             moved=8 * rows * columns,
         )(result_mask.T, held, mid, low, high, h0, h1, near_panels, *first)
 
-    product0, flipped0, terms0 = near(0, mid0, low0, high0)
-    product, flipped1, terms1 = near(1, mid1, low1, high1, product0)
-    far = after(far, terms1)
+    def send(*parts):
+        return [lax.ppermute(part, "y", ring(wide, s + 1)) for s, part in enumerate(parts)]
+
+    product0, flipped0, *parts = near(0, mid0, low0, high0)
+    product, flipped1, near_own, *parts = near(1, mid1, low1, high1, product0, *parts)
+    near_got = send(*parts)
+    far = after(far, *near_got)
     both = lax.ppermute(far, "core", swap)
-    far_terms = call(
+    far_own, *parts = call(
         far_kernel,
-        like((2, columns, half), BF16),
-        [VMEM] * 3,
-        flops=4 * rows * half * columns,
-        moved=8 * rows * half,
-    )(flipped0, flipped1, far)
-    terms = call(
-        gather_kernel,
-        like((groups // deep, columns, half), BF16),
-        [VMEM] * 6,
-        flops=4 * rows * half * columns,
+        (own, long, long, long),
+        [VMEM] * 4,
+        flops=8 * rows * half * columns,
         moved=8 * rows * columns,
-    )(flipped0, flipped1, both, terms0, terms1, far_terms)
-    terms = lax.all_to_all(terms, ("xl", "y"), 0, 0, tiled=True)
-    part = call(first_sum_kernel, like((half, columns), BF16), [VMEM])(terms)
-    part = part.reshape(deep, half // deep, columns)
-    part = lax.all_to_all(part, "z", 0, 0, tiled=True)
+    )(flipped0, flipped1, far, both)
+    far_got = send(*parts)
+    part = call(first_sum_kernel, like((2 * deep, half // deep, columns), BF16), [VMEM] * 8, moved=8 * rows * half)(
+        near_own, *near_got, far_own, *far_got
+    )
+    part = lax.all_to_all(part, ("xl", "z"), 0, 0, tiled=True)
     factor = 1.0 / math.sqrt(rows * groups)
     projected = call(
         functools.partial(last_sum_kernel, factor), like((half // deep, columns), F32), [VMEM]

time: 98.3 us -> 108 us (1.099); the launches traced: 97.9 us -> 106 us
  blocking collectives: 50.6 us -> 18 us
  waiting for transfers between devices: 14 us -> 34.4 us
  starting transfers between devices: 13 us -> 29 us
  Pallas kernels: 13.5 us -> 17.6 us
    all_to_all x2 -> x1, blocking collectives: 50.6 us -> 18 us  [on_device(): part = lax.all_to_all(part, ('xl', 'z'), 0, 0, tiled=True)]
    ppermute x0 -> x6, waiting for transfers between devices: none -> 20.7 us  [send(): lax.ppermute(part, 'y', ring(wide, s + 1))]
    ppermute x0 -> x6, starting transfers between devices: none -> 16 us  [send(): lax.ppermute(part, 'y', ring(wide, s + 1))]
    pallas_call x5 -> x4, Pallas kernels: 6.69 us -> 10.8 us  [the longest x2 7.06 us: near(): call(functools.partial(near_kernel, size, h), (like((rows, half * (h + 1)...]
  transfers between devices with their start and end apart: 8 -> 14, of which waited for: 3 -> 9; matrix products, arithmetic and copies ran while one was open for 0% -> 0% of each run, Pallas kernels for 9% -> 9%
where the time goes in v5:
time: 108 us; the launch traced here: 106 us
  waiting for transfers between devices  34.4 us (32%)
  starting transfers between devices  29 us (27%)
  blocking collectives  18 us (17%)
  Pallas kernels  17.6 us (16%)
  local copies, waits for them, and re-layouts  6.07 us (6%)
    ppermute x6, waiting for transfers between devices, send(): lax.ppermute(part, 'y', ring(wide, s + 1))  20.7 us
    all_to_all x1, blocking collectives, on_device(): part = lax.all_to_all(part, ('xl', 'z'), 0, 0, tiled=True)  18 us
    ppermute x6, starting transfers between devices, send(): lax.ppermute(part, 'y', ring(wide, s + 1))  16 us
    ppermute x1, waiting for transfers between devices, on_device(): low1 = lax.ppermute(up1, ROWS, within)  7.17 us
    pallas_call x2, Pallas kernels, near(): call(functools.partial(near_kernel, size, h), (like((rows, half * (h + 1)...  7.06 us
    unnamed x12, local copies, waits for them, and re-layouts  6.07 us
    ppermute x1, starting transfers between devices, on_device(): high0 = lax.ppermute(h0, ROWS, ring(groups, groups - 1))  5.74 us
    ppermute x1, starting transfers between devices, on_device(): high1 = lax.ppermute(down1, ROWS, [(b, a) for a, b in within])  4.2 us
  transfers between devices with their start and end apart: 14, of which 9 were waited for; matrix products, arithmetic and copies ran while one was open for 0% of the time, Pallas kernels for 9%

profile of v5, /device:TPU:10, one launch (start us, length us, event | category | flops | bytes accessed | tf_op | source)
XLA Modules:
  0.0 105.9 jit_solution(14486725202454380402)
XLA Ops:
  0.6 3.3 %shard_map.68 = (bf16[1024,256]{1,0:T(8,128)(2,1)}, bf16[1024,256]{1,0:T(8,128)(2,1)}, bf16[2,1024,256]{2,1,0:T(8,128)(2,1)}) custom-call(s32[4,8]{1,0:T(4,128)} %bitcast.4, bf16[1024,512]{1,0:T(8,128)(2,1)} %slab_hbm.1), custom_call_target="tpu_custom_call" | custom-call | tf_op jit(solution)/shard_map/pallas_call | solution.py:180
  3.9 0.1 collective-permute-start.1
  4.0 0.7 collective-permute-start
  4.7 2.2 %collective-permute-start.9 = (bf16[2,1024,256]{2,1,0:T(8,128)(2,1)}, bf16[2,1024,256]{2,1,0:T(8,128)(2,1)S(1)}, u32[]{:S(2)}, u32[]{:S(2)}) collective-permute-start(bf16[2,1024,256]{2,1,0:T(8,128)(2,1)} %get-tuple-element.30), channel_id=1, source_target_pairs={{0,128},{128,0},{1,129},{129,1},{2,130},{130,2},{3,131},{131,3},{4... | collective-permute-start | bytes 3145736 | tf_op jit(solution)/shard_map/ppermute | solution.py:198
  6.9 5.7 %collective-permute-start.5 = (bf16[1024,256]{1,0:T(8,128)(2,1)}, bf16[1024,256]{1,0:T(8,128)(2,1)S(1)}, u32[]{:S(2)}, u32[]{:S(2)}) collective-permute-start(bf16[1024,256]{1,0:T(8,128)(2,1)} %get-tuple-element.26.h0_ref.own0_ref), channel_id=1, source_target_pairs={{0,63},{1,0},{2,1},{3,2},{4,3},{5,4},{6,5},{7,6},{8,7},{9,8},{10,9... | collective-permute-start | bytes 1572872 | tf_op jit(solution)/shard_map/ppermute | solution.py:195
  12.7 1.0 copy-done
  13.9 4.2 %collective-permute-start.3 = (bf16[1024,256]{1,0:T(8,128)(2,1)S(1)}, bf16[1024,256]{1,0:T(8,128)(2,1)S(1)}, u32[]{:S(2)}, u32[]{:S(2)}) collective-permute-start(bf16[1024,256]{1,0:T(8,128)(2,1)S(1)} %get-tuple-element.32), channel_id=1, source_target_pairs={{1,0},{2,1},{3,2},{4,3},{5,4},{6,5},{7,6},{8,7},{9,8},{10,9},{11,1... | collective-permute-start | bytes 1572872 | tf_op jit(solution)/shard_map/ppermute | solution.py:212
  18.1 1.0 copy-done.1
  19.1 1.0 copy-done.2
  20.2 2.3 %copy-done.3 = bf16[1024,2176]{1,0:T(8,128)(2,1)S(1)} copy-done((bf16[1024,2176]{1,0:T(8,128)(2,1)S(1)}, bf16[1024,2176]{1,0:T(8,128)(2,1)}, u32[]{:S(2)}) %copy-start.3) | copy-done | bytes 4456472
  22.4 0.7 copy-done.5
  23.1 2.8 %shard_map.69 = (bf16[1024,2176]{1,0:T(8,128)(2,1)S(1)}, f32[1024,256]{1,0:T(8,128)S(1)}, f32[1024,256]{1,0:T(8,128)S(1)}) custom-call(s32[8,17]{1,0:T(8,128)S(1)} %copy-done.5, bf16[1024,2176]{1,0:T(8,128)(2,1)S(1)} %copy-done.3, bf16[1024,256]{1,0:T(8,128)(2,1)S(1)} %copy-done.2, bf16[1024,256]{1,0:T(8,128)(2,1)S(1)} %copy-done.1), custom_call_target="tpu_custom_call" | custom-call | flops 1073741824 | bytes 8912896 | tf_op jit(solution)/shard_map/pallas_call | solution.py:200
  25.9 3.8 %collective-permute-done.4.low_ref = bf16[1024,256]{1,0:T(8,128)(2,1)S(1)} collective-permute-done((bf16[1024,256]{1,0:T(8,128)(2,1)}, bf16[1024,256]{1,0:T(8,128)(2,1)S(1)}, u32[]{:S(2)}, u32[]{:S(2)}) %collective-permute-start.4) | collective-permute-done | bytes 524320 | tf_op jit(solution)/shard_map/ppermute | solution.py:194
  29.8 3.0 %shard_map.72 = (bf16[1024,256]{1,0:T(8,128)(2,1)S(1)}, bf16[256,1024]{1,0:T(8,128)(2,1)S(1)}, f32[256,256]{1,0:T(8,128)S(1)}, bf16[256,256]{1,0:T(8,128)(2,1)S(...) custom-call(s32[4,8]{1,0:T(4,128)S(1)} %bitcast.2, bf16[1024,2176]{1,0:T(8,128)(2,1)S(1)} %get-tuple-element.28.held_ref, ...), custom_call_target="tpu_custom_call" | custom-call | flops 1140850688 | bytes 4194304 | tf_op jit(solution)/shard_map/pallas_call | solution.py:218
  32.8 7.2 %collective-permute-done.2.low_ref = bf16[1024,256]{1,0:T(8,128)(2,1)S(1)} collective-permute-done((bf16[1024,256]{1,0:T(8,128)(2,1)S(1)}, bf16[1024,256]{1,0:T(8,128)(2,1)S(1)}, u32[]{:S(2)}, u32[]{:S(2)}) %collective-permute-start.2) | collective-permute-done | bytes 524320 | tf_op jit(solution)/shard_map/ppermute | solution.py:211
  40.0 4.1 %shard_map.73 = (bf16[1024,512]{1,0:T(8,128)(2,1)}, bf16[256,1024]{1,0:T(8,128)(2,1)S(1)}, f32[512,256]{1,0:T(8,128)S(1)}, bf16[512,256]{1,0:T(8,128)(2,1)S(1)},...) custom-call(s32[4,8]{1,0:T(4,128)S(1)} %bitcast.3, bf16[1024,2176]{1,0:T(8,128)(2,1)S(1)} %get-tuple-element.28.held_ref, ...), custom_call_target="tpu_custom_call" | custom-call | flops 1140850688 | bytes 4194304 | tf_op jit(solution)/shard_map/pallas_call | solution.py:218
  44.0 1.6 %collective-permute-start.6 = (bf16[512,256]{1,0:T(8,128)(2,1)S(1)}, bf16[512,256]{1,0:T(8,128)(2,1)S(1)}, u32[]{:S(2)}, u32[]{:S(2)}) collective-permute-start(bf16[512,256]{1,0:T(8,128)(2,1)S(1)} %get-tuple-element.41), channel_id=1, source_target_pairs={{0,8},{8,16},{16,24},{24,0},{1,9},{9,17},{17,25},{25,1},{2,10},{10... | collective-permute-start | bytes 786440 | tf_op jit(solution)/shard_map/ppermute | solution.py:227
  45.6 8.7 %collective-permute-start.7 = (bf16[512,256]{1,0:T(8,128)(2,1)S(1)}, bf16[512,256]{1,0:T(8,128)(2,1)S(1)}, u32[]{:S(2)}, u32[]{:S(2)}) collective-permute-start(bf16[512,256]{1,0:T(8,128)(2,1)S(1)} %get-tuple-element.42), channel_id=1, source_target_pairs={{0,16},{8,24},{16,0},{24,8},{1,17},{9,25},{17,1},{25,9},{2,18},{10... | collective-permute-start | bytes 786440 | tf_op jit(solution)/shard_map/ppermute | solution.py:227
  54.3 5.1 %collective-permute-done.6.refs_1_ = bf16[512,256]{1,0:T(8,128)(2,1)S(1)} collective-permute-done((bf16[512,256]{1,0:T(8,128)(2,1)S(1)}, bf16[512,256]{1,0:T(8,128)(2,1)S(1)}, u32[]{:S(2)}, u32[]{:S(2)}) %collective-permute-start.6) | collective-permute-done | bytes 262176 | tf_op jit(solution)/shard_map/ppermute | solution.py:227
  59.5 2.1 %collective-permute-done.7.refs_2_ = bf16[512,256]{1,0:T(8,128)(2,1)S(1)} collective-permute-done((bf16[512,256]{1,0:T(8,128)(2,1)S(1)}, bf16[512,256]{1,0:T(8,128)(2,1)S(1)}, u32[]{:S(2)}, u32[]{:S(2)}) %collective-permute-start.7) | collective-permute-done | bytes 262176 | tf_op jit(solution)/shard_map/ppermute | solution.py:227
  61.6 3.2 %collective-permute-done.8.refs_3_ = bf16[512,256]{1,0:T(8,128)(2,1)S(1)} collective-permute-done((bf16[512,256]{1,0:T(8,128)(2,1)S(1)}, bf16[512,256]{1,0:T(8,128)(2,1)S(1)}, u32[]{:S(2)}, u32[]{:S(2)}) %collective-permute-start.8) | collective-permute-done | bytes 262176 | tf_op jit(solution)/shard_map/ppermute | solution.py:227
  64.8 2.7 %collective-permute-done.10.both_ref = bf16[2,1024,256]{2,1,0:T(8,128)(2,1)S(1)} collective-permute-done((bf16[2,1024,256]{2,1,0:T(8,128)(2,1)S(1)}, bf16[2,1024,256]{2,1,0:T(8,128)(2,1)S(1)}, u32[]{:S(2)}, u32[]{:S(2)}) %collective-permute-start.10) | collective-permute-done | bytes 1048608 | tf_op jit(solution)/shard_map/ppermute | solution.py:233
  67.5 3.4 %shard_map.75 = (f32[512,256]{1,0:T(8,128)S(1)}, bf16[512,256]{1,0:T(8,128)(2,1)S(1)}, bf16[512,256]{1,0:T(8,128)(2,1)S(1)}, bf16[512,256]{1,0:T(8,128)(2,1)S(1)}) custom-call(bf16[256,1024]{1,0:T(8,128)(2,1)S(1)} %get-tuple-element.44.t0_ref, bf16[256,1024]{1,0:T(8,128)(2,1)S(1)} %get-tuple-element.45.t1_ref, bf16[2,1024,256]{2,1,0:T(8,128)(2,1)S(1)} %shard_map.74.far_ref, ...), custom_call_target="tpu_custom_call" | custom-call | flops 1073741824 | bytes 4194304 | tf_op jit(solution)/shard_map/pallas_call | solution.py:234
  70.9 0.7 collective-permute-start.11
  71.6 3.3 %collective-permute-start.12 = (bf16[512,256]{1,0:T(8,128)(2,1)S(1)}, bf16[512,256]{1,0:T(8,128)(2,1)S(1)}, u32[]{:S(2)}, u32[]{:S(2)}) collective-permute-start(bf16[512,256]{1,0:T(8,128)(2,1)S(1)} %get-tuple-element.48), channel_id=1, source_target_pairs={{0,16},{8,24},{16,0},{24,8},{1,17},{9,25},{17,1},{25,9},{2,18},{10... | collective-permute-start | bytes 786440 | tf_op jit(solution)/shard_map/ppermute | solution.py:227
  74.8 1.7 %collective-permute-start.13 = (bf16[512,256]{1,0:T(8,128)(2,1)S(1)}, bf16[512,256]{1,0:T(8,128)(2,1)S(1)}, u32[]{:S(2)}, u32[]{:S(2)}) collective-permute-start(bf16[512,256]{1,0:T(8,128)(2,1)S(1)} %get-tuple-element.49), channel_id=1, source_target_pairs={{0,24},{8,0},{16,8},{24,16},{1,25},{9,1},{17,9},{25,17},{2,26},{10... | collective-permute-start | bytes 786440 | tf_op jit(solution)/shard_map/ppermute | solution.py:227
  76.6 3.6 %collective-permute-done.11.refs_5_ = bf16[512,256]{1,0:T(8,128)(2,1)S(1)} collective-permute-done((bf16[512,256]{1,0:T(8,128)(2,1)S(1)}, bf16[512,256]{1,0:T(8,128)(2,1)S(1)}, u32[]{:S(2)}, u32[]{:S(2)}) %collective-permute-start.11) | collective-permute-done | bytes 262176 | tf_op jit(solution)/shard_map/ppermute | solution.py:227
  80.1 2.2 %collective-permute-done.12.refs_6_ = bf16[512,256]{1,0:T(8,128)(2,1)S(1)} collective-permute-done((bf16[512,256]{1,0:T(8,128)(2,1)S(1)}, bf16[512,256]{1,0:T(8,128)(2,1)S(1)}, u32[]{:S(2)}, u32[]{:S(2)}) %collective-permute-start.12) | collective-permute-done | bytes 262176 | tf_op jit(solution)/shard_map/ppermute | solution.py:227
  82.3 4.5 %collective-permute-done.13.refs_7_ = bf16[512,256]{1,0:T(8,128)(2,1)S(1)} collective-permute-done((bf16[512,256]{1,0:T(8,128)(2,1)S(1)}, bf16[512,256]{1,0:T(8,128)(2,1)S(1)}, u32[]{:S(2)}, u32[]{:S(2)}) %collective-permute-start.13) | collective-permute-done | bytes 262176 | tf_op jit(solution)/shard_map/ppermute | solution.py:227
  86.8 0.3 shard_map.76
  87.1 18.0 %all_to_all.5.in_ref = bf16[16,32,512]{2,1,0:T(8,128)(2,1)S(1)} all-to-all(bf16[16,32,512]{2,1,0:T(8,128)(2,1)S(1)} %shard_map.76), channel_id=1, replica_groups=mesh['xh'=2,'core'=2,'xl'=2,'y'=4,'z'=8] {'xl','z'}, dimensions={0} | all-to-all | bytes 1048576 | tf_op jit(solution)/shard_map/all_to_all | solution.py:245
  105.2 0.7 shard_map.77
  (19 shorter events, 0.2 us)
Async XLA Ops:
  3.9 25.9 %copy-start.4 = (s32[8,4]{0,1:T(4,128)S(1)}, s32[8,4]{0,1:T(4,128)}, u32[]{:S(2)}) copy-start(s32[8,4]{0,1:T(4,128)} %param.9) | copy-start | bytes 388
  3.9 8.8 %collective-permute-start.1 = (bf16[2,1024,256]{2,1,0:T(8,128)(2,1)}, bf16[2,1024,256]{2,1,0:T(8,128)(2,1)S(1)}, u32[]{:S(2)}, u32[]{:S(2)}) collective-permute-start(bf16[2,1024,256]{2,1,0:T(8,128)(2,1)} %get-tuple-element.30), channel_id=1, source_target_pairs={{0,64},{64,0},{1,65},{65,1},{2,66},{66,2},{3,67},{67,3},{4,68},{68... | collective-permute-start | bytes 3145736 | tf_op jit(solution)/shard_map/ppermute | solution.py:199
  4.0 8.7 %collective-permute-start = (bf16[1024,256]{1,0:T(8,128)(2,1)}, bf16[1024,256]{1,0:T(8,128)(2,1)S(1)}, u32[]{:S(2)}, u32[]{:S(2)}) collective-permute-start(bf16[1024,256]{1,0:T(8,128)(2,1)} %get-tuple-element.27.h1_ref.own_ref.own1_ref), channel_id=1, source_target_pairs={{0,32},{31,63},{32,0},{63,31},{64,96},{95,127},{96,64},{127,95},{1... | collective-permute-start | bytes 1572872 | tf_op jit(solution)/shard_map/ppermute | solution.py:197
  4.7 49.6 %collective-permute-start.9 = (bf16[2,1024,256]{2,1,0:T(8,128)(2,1)}, bf16[2,1024,256]{2,1,0:T(8,128)(2,1)S(1)}, u32[]{:S(2)}, u32[]{:S(2)}) collective-permute-start(bf16[2,1024,256]{2,1,0:T(8,128)(2,1)} %get-tuple-element.30), channel_id=1, source_target_pairs={{0,128},{128,0},{1,129},{129,1},{2,130},{130,2},{3,131},{131,3},{4... | collective-permute-start | bytes 3145736 | tf_op jit(solution)/shard_map/ppermute | solution.py:198
  6.9 19.0 %collective-permute-start.5 = (bf16[1024,256]{1,0:T(8,128)(2,1)}, bf16[1024,256]{1,0:T(8,128)(2,1)S(1)}, u32[]{:S(2)}, u32[]{:S(2)}) collective-permute-start(bf16[1024,256]{1,0:T(8,128)(2,1)} %get-tuple-element.26.h0_ref.own0_ref), channel_id=1, source_target_pairs={{0,63},{1,0},{2,1},{3,2},{4,3},{5,4},{6,5},{7,6},{8,7},{9,8},{10,9... | collective-permute-start | bytes 1572872 | tf_op jit(solution)/shard_map/ppermute | solution.py:195
  12.7 17.1 %collective-permute-start.4 = (bf16[1024,256]{1,0:T(8,128)(2,1)}, bf16[1024,256]{1,0:T(8,128)(2,1)S(1)}, u32[]{:S(2)}, u32[]{:S(2)}) collective-permute-start(bf16[1024,256]{1,0:T(8,128)(2,1)} %get-tuple-element.26.h0_ref.own0_ref), channel_id=1, source_target_pairs={{0,1},{1,2},{2,3},{3,4},{4,5},{5,6},{6,7},{7,8},{8,9},{9,10},{10,1... | collective-permute-start | bytes 1572872 | tf_op jit(solution)/shard_map/ppermute | solution.py:194
  12.7 1.0 copy-start
  13.8 26.2 %collective-permute-start.2 = (bf16[1024,256]{1,0:T(8,128)(2,1)S(1)}, bf16[1024,256]{1,0:T(8,128)(2,1)S(1)}, u32[]{:S(2)}, u32[]{:S(2)}) collective-permute-start(bf16[1024,256]{1,0:T(8,128)(2,1)S(1)} %get-tuple-element.31), channel_id=1, source_target_pairs={{0,1},{1,2},{2,3},{3,4},{4,5},{5,6},{6,7},{7,8},{8,9},{9,10},{10,1... | collective-permute-start | bytes 1572872 | tf_op jit(solution)/shard_map/ppermute | solution.py:211
  13.9 26.1 %collective-permute-start.3 = (bf16[1024,256]{1,0:T(8,128)(2,1)S(1)}, bf16[1024,256]{1,0:T(8,128)(2,1)S(1)}, u32[]{:S(2)}, u32[]{:S(2)}) collective-permute-start(bf16[1024,256]{1,0:T(8,128)(2,1)S(1)} %get-tuple-element.32), channel_id=1, source_target_pairs={{1,0},{2,1},{3,2},{4,3},{5,4},{6,5},{7,6},{8,7},{9,8},{10,9},{11,1... | collective-permute-start | bytes 1572872 | tf_op jit(solution)/shard_map/ppermute | solution.py:212
  18.1 1.0 copy-start.1
  19.1 1.0 copy-start.2
  20.2 2.3 %copy-start.3 = (bf16[1024,2176]{1,0:T(8,128)(2,1)S(1)}, bf16[1024,2176]{1,0:T(8,128)(2,1)}, u32[]{:S(2)}) copy-start(bf16[1024,2176]{1,0:T(8,128)(2,1)} %fock_ref.1) | copy-start | bytes 13369348
  22.4 0.7 copy-start.5
  44.0 15.4 %collective-permute-start.6 = (bf16[512,256]{1,0:T(8,128)(2,1)S(1)}, bf16[512,256]{1,0:T(8,128)(2,1)S(1)}, u32[]{:S(2)}, u32[]{:S(2)}) collective-permute-start(bf16[512,256]{1,0:T(8,128)(2,1)S(1)} %get-tuple-element.41), channel_id=1, source_target_pairs={{0,8},{8,16},{16,24},{24,0},{1,9},{9,17},{17,25},{25,1},{2,10},{10... | collective-permute-start | bytes 786440 | tf_op jit(solution)/shard_map/ppermute | solution.py:227
  45.6 16.0 %collective-permute-start.7 = (bf16[512,256]{1,0:T(8,128)(2,1)S(1)}, bf16[512,256]{1,0:T(8,128)(2,1)S(1)}, u32[]{:S(2)}, u32[]{:S(2)}) collective-permute-start(bf16[512,256]{1,0:T(8,128)(2,1)S(1)} %get-tuple-element.42), channel_id=1, source_target_pairs={{0,16},{8,24},{16,0},{24,8},{1,17},{9,25},{17,1},{25,9},{2,18},{10... | collective-permute-start | bytes 786440 | tf_op jit(solution)/shard_map/ppermute | solution.py:227
  54.3 10.5 %collective-permute-start.8 = (bf16[512,256]{1,0:T(8,128)(2,1)S(1)}, bf16[512,256]{1,0:T(8,128)(2,1)S(1)}, u32[]{:S(2)}, u32[]{:S(2)}) collective-permute-start(bf16[512,256]{1,0:T(8,128)(2,1)S(1)} %get-tuple-element.43), channel_id=1, source_target_pairs={{0,24},{8,0},{16,8},{24,16},{1,25},{9,1},{17,9},{25,17},{2,26},{10... | collective-permute-start | bytes 786440 | tf_op jit(solution)/shard_map/ppermute | solution.py:227
  64.8 2.7 %collective-permute-start.10 = (bf16[2,1024,256]{2,1,0:T(8,128)(2,1)S(1)}, bf16[2,1024,256]{2,1,0:T(8,128)(2,1)S(1)}, u32[]{:S(2)}, u32[]{:S(2)}) collective-permute-start(bf16[2,1024,256]{2,1,0:T(8,128)(2,1)S(1)} %shard_map.74.far_ref), channel_id=1, source_target_pairs={{0,64},{64,0},{1,65},{65,1},{2,66},{66,2},{3,67},{67,3},{4,68},{68... | collective-permute-start | bytes 3145736 | tf_op jit(solution)/shard_map/ppermute | solution.py:233
  70.9 9.2 %collective-permute-start.11 = (bf16[512,256]{1,0:T(8,128)(2,1)S(1)}, bf16[512,256]{1,0:T(8,128)(2,1)S(1)}, u32[]{:S(2)}, u32[]{:S(2)}) collective-permute-start(bf16[512,256]{1,0:T(8,128)(2,1)S(1)} %get-tuple-element.47), channel_id=1, source_target_pairs={{0,8},{8,16},{16,24},{24,0},{1,9},{9,17},{17,25},{25,1},{2,10},{10... | collective-permute-start | bytes 786440 | tf_op jit(solution)/shard_map/ppermute | solution.py:227
  71.6 10.7 %collective-permute-start.12 = (bf16[512,256]{1,0:T(8,128)(2,1)S(1)}, bf16[512,256]{1,0:T(8,128)(2,1)S(1)}, u32[]{:S(2)}, u32[]{:S(2)}) collective-permute-start(bf16[512,256]{1,0:T(8,128)(2,1)S(1)} %get-tuple-element.48), channel_id=1, source_target_pairs={{0,16},{8,24},{16,0},{24,8},{1,17},{9,25},{17,1},{25,9},{2,18},{10... | collective-permute-start | bytes 786440 | tf_op jit(solution)/shard_map/ppermute | solution.py:227
  74.8 11.9 %collective-permute-start.13 = (bf16[512,256]{1,0:T(8,128)(2,1)S(1)}, bf16[512,256]{1,0:T(8,128)(2,1)S(1)}, u32[]{:S(2)}, u32[]{:S(2)}) collective-permute-start(bf16[512,256]{1,0:T(8,128)(2,1)S(1)} %get-tuple-element.49), channel_id=1, source_target_pairs={{0,24},{8,0},{16,8},{24,16},{1,25},{9,1},{17,9},{25,17},{2,26},{10... | collective-permute-start | bytes 786440 | tf_op jit(solution)/shard_map/ppermute | solution.py:227

commit v6 on v5

v6 whole, which is shorter than its diff:
```python
import functools
import math

import jax
import jax.numpy as jnp
from jax import lax
from jax.experimental import pallas as pl
from jax.experimental.pallas import tpu as pltpu
from jax.sharding import Mesh, PartitionSpec as P

F32, BF16 = jnp.float32, jnp.bfloat16
ROWS = ("xl", "y", "z")
BLK = ("xh", "core")
VMEM = pl.BlockSpec(memory_space=pltpu.VMEM)
SMEM = pl.BlockSpec(memory_space=pltpu.SMEM)
HBM = pl.BlockSpec(memory_space=pltpu.HBM)
MIB = 1 << 20


def call(body, outs, ins, scratch=(), limit=8 * MIB, flops=0, moved=0, place=VMEM):
    return pl.pallas_call(
        body,
        out_shape=outs,
        in_specs=ins,
        out_specs=jax.tree.map(lambda _: place, outs),
        scratch_shapes=list(scratch),
        compiler_params=pltpu.CompilerParams(vmem_limit_bytes=limit),
        cost_estimate=pl.CostEstimate(flops=flops, bytes_accessed=moved, transcendentals=0),
    )


def dot(a, b):
    return jnp.dot(a, b, preferred_element_type=F32)


def mask_kernel(size, mask_ref, slab_hbm, out_hbm, held, in_sems, out_sems):
    panels, blocks = mask_ref.shape
    at = [pl.ds(i * size, size) for i in range(blocks)]
    loads = [pltpu.make_async_copy(slab_hbm.at[at[i]], held.at[at[i]], in_sems.at[i]) for i in range(blocks)]
    stores = [pltpu.make_async_copy(held.at[at[i]], out_hbm.at[at[i]], out_sems.at[i]) for i in range(blocks)]
    for load in loads:
        load.start()
    for i in range(blocks):
        loads[i].wait()
        for j in range(panels):
            cols = pl.ds(j * size, size)
            tile = held[at[i], cols]
            held[at[i], cols] = jnp.where(mask_ref[j, i] != 0, tile, jnp.zeros_like(tile))
        stores[i].start()
    for store in stores:
        store.wait()


def middle_kernel(size, fmask_ref, fock_ref, slab_ref, held_ref, mid_ref, again_ref):
    again_ref[...] = slab_ref[...]
    blocks, slots = fmask_ref.shape
    for i in range(blocks):
        rows = pl.ds(i * size, size)
        for o in range(slots):
            cols = pl.ds(o * size, size)
            tile = fock_ref[rows, cols]
            held_ref[rows, cols] = jnp.where(fmask_ref[i, o] != 0, tile, jnp.zeros_like(tile))
        mid_ref[rows, :] = dot(held_ref[rows, pl.ds((blocks - i) * size, blocks * size)], slab_ref[...])


def near_kernel(size, rmask_ref, held_ref, mid_ref, low_ref, high_ref, own_ref, near_ref, out_ref, outt_ref, *to):
    panels, blocks = rmask_ref.shape
    slots = held_ref.shape[1] // size
    for i in range(blocks):
        rows = pl.ds(i * size, size)
        total = mid_ref[rows, :]
        total += dot(held_ref[rows, : (blocks - i) * size], low_ref[i * size :, :])
        total += dot(held_ref[rows, (2 * blocks - i) * size :], high_ref[: (slots - 2 * blocks + i) * size, :])
        for j in range(panels):
            cols = slice(j * size, (j + 1) * size)
            tile = total[:, cols]
            tile = jnp.where(rmask_ref[j, i] != 0, tile, jnp.zeros_like(tile)).astype(BF16)
            out_ref[rows, cols] = tile
            outt_ref[cols, rows] = tile.T
    half = to[0].shape[1]
    for q, ref in enumerate((own_ref, near_ref)):
        for k in range(2):
            project(outt_ref, ref[:, pl.ds(k * half, half)], q, k, enumerate(to))


def project(outt_ref, panel, q, k, to):
    terms = dot(outt_ref[...], panel)
    step = lax.rem((lax.axis_index("core") ^ q) * 2 + k - lax.axis_index("y") + 4, 4)
    for s, into in to:

        @pl.when(step == s)
        def _():
            into[...] = terms.astype(into.dtype)


def merge_kernel(edge, early_hbm, late_hbm, out_hbm, sem):
    y, z = lax.axis_index("y"), lax.axis_index("z")

    @pl.when(crossing(edge, y, z))
    def _():
        copy = pltpu.make_async_copy(late_hbm, out_hbm, sem)
        copy.start()
        copy.wait()


def crossing(edge, y, z):
    return ((y == edge[0] - 1) & (z == 0)) | ((y == 0) & (z == edge[1] - 1))


def far_kernel(outt_ref, far_ref, both_ref, *to):
    half = to[0].shape[1]
    for q, ref in enumerate((far_ref, both_ref)):
        for k in range(2):
            project(outt_ref, ref[:, pl.ds(k * half, half)], q, k, enumerate(to))


def first_sum_kernel(*refs):
    out_ref = refs[-1]
    count, deep, _ = out_ref.shape
    inner = count // 2
    xh = lax.axis_index("xh")
    for f, parts in enumerate((refs[:4], refs[4:8])):
        total = parts[0][...]
        for part in parts[1:]:
            total += part[...].astype(F32)
        turned = total.T.astype(BF16)
        for z in range(inner):
            out_ref[(xh ^ f) * inner + z] = turned[z * deep : (z + 1) * deep]


def last_sum_kernel(factor, in_ref, out_ref):
    total = in_ref[0].astype(F32)
    for s in range(1, in_ref.shape[0]):
        total += in_ref[s].astype(F32)
    out_ref[...] = total * factor


def after(x, *others):
    anywhere = pl.BlockSpec(memory_space=pl.ANY)
    return pl.pallas_call(
        lambda *refs: None,
        out_shape=jax.ShapeDtypeStruct(x.shape, x.dtype),
        in_specs=[anywhere] * (1 + len(others)),
        out_specs=anywhere,
        input_output_aliases={0: 0},
        compiler_params=pltpu.CompilerParams(vmem_limit_bytes=MIB),
    )(x, *others)


def ring(count, step):
    return [(i, (i + step) % count) for i in range(count)]


def on_device(fock_band, fock_slot_mask, orbital_slab, orbital_mask, result_mask):
    blocks, slots = fock_slot_mask.shape
    rows, columns = orbital_slab.shape
    size = rows // blocks
    half = columns // 2
    like = jax.ShapeDtypeStruct
    groups, wide, deep = lax.axis_size(ROWS), lax.axis_size("y"), lax.axis_size("z")
    whole = like((rows, columns), BF16)
    slab = call(
        functools.partial(mask_kernel, size),
        whole,
        [SMEM, HBM],
        [pltpu.VMEM((rows, columns), BF16), *[pltpu.SemaphoreType.DMA((blocks,))] * 2],
        limit=60 * MIB,
        place=HBM,
    )(orbital_mask.T, orbital_slab)
    swap = ring(2, 1)
    low = lax.ppermute(slab, ROWS, ring(groups, 1))
    high = lax.ppermute(slab, ROWS, ring(groups, groups - 1))
    near_slab = lax.ppermute(slab, "core", swap)
    edge = (wide, deep)
    pairs = [], []
    for i in range(2 * groups):
        late = crossing(edge, i // deep % wide, i % deep)
        pairs[late].append((i, (i + groups) % (2 * groups)))
    early_far = lax.ppermute(slab, ("xh", *ROWS), pairs[0])
    held, mid, again = call(
        functools.partial(middle_kernel, size),
        (like((rows, slots * size), BF16), like((rows, columns), F32), whole),
        [SMEM, VMEM, VMEM],
        flops=2 * rows * rows * columns,
        moved=4 * rows * slots * size,
    )(fock_slot_mask, fock_band, slab)
    late_far = lax.ppermute(after(again, low, high, early_far), ("xh", *ROWS), pairs[1])
    own, long = like((columns, half), F32), like((columns, half), BF16)
    product, flipped, near_own, *parts = call(
        functools.partial(near_kernel, size),
        (whole, like((columns, rows), BF16), own, long, long, long),
        [SMEM] + [VMEM] * 6,
        flops=2 * rows * columns * (2 * columns + (slots - blocks) * size),
        moved=16 * rows * columns,
        limit=16 * MIB,
    )(result_mask.T, held, mid, low, high, slab, near_slab)

    def send(part, step):
        return lax.ppermute(part, "y", ring(wide, step))

    near_got = [send(part, step + 1) for step, part in enumerate(parts)]

    anywhere = pl.BlockSpec(memory_space=pl.ANY)
    far = pl.pallas_call(
        functools.partial(merge_kernel, edge),
        out_shape=whole,
        in_specs=[anywhere] * 2,
        out_specs=anywhere,
        scratch_shapes=[pltpu.SemaphoreType.DMA],
        input_output_aliases={0: 0},
        compiler_params=pltpu.CompilerParams(vmem_limit_bytes=MIB),
    )(early_far, after(late_far, *near_got))
    both = lax.ppermute(far, "core", swap)
    far_own, *parts = call(
        far_kernel,
        (own, long, long, long),
        [VMEM] * 3,
        flops=4 * rows * columns * columns,
        moved=16 * rows * half,
    )(flipped, far, both)
    far_got = [send(part, step + 1) for step, part in enumerate(parts)]
    part = call(first_sum_kernel, like((2 * deep, half // deep, columns), BF16), [VMEM] * 8, moved=8 * rows * half)(
        near_own, *near_got, far_own, *far_got
    )
    part = lax.all_to_all(part, ("xl", "z"), 0, 0, tiled=True)
    factor = 1.0 / math.sqrt(rows * groups)
    projected = call(
        functools.partial(last_sum_kernel, factor), like((half // deep, columns), F32), [VMEM]
    )(part)
    return (product, projected)


def solution(mesh):
    split = Mesh(mesh.devices.reshape(2, 2, 2, 4, 8), BLK + ROWS)
    placed = (P(ROWS, None), P(ROWS, None), P(ROWS, BLK), P(ROWS, BLK), P(ROWS, BLK))
    return jax.shard_map(
        on_device,
        mesh=split,
        in_specs=placed,
        out_specs=(P(ROWS, BLK), P(ROWS, BLK)),
        check_vma=False,
    )
```

time: 108 us -> 105 us (0.972)
  starting transfers between devices: 29 us -> 21.2 us
  waiting for transfers between devices: 34.4 us -> 40.3 us
  blocking collectives: 18 us -> 20.3 us
  local copies, waits for them, and re-layouts: 6.07 us -> 4.17 us
  Pallas kernels: 17.6 us -> 15.9 us
    ppermute x13 -> x11, starting transfers between devices: 29 us -> 21.1 us  [the longest x6 10.4 us: send(): return lax.ppermute(part, 'y', ring(wide, step))]
    ppermute x13 -> x11, waiting for transfers between devices: 31.7 us -> 37.7 us  [the longest x6 20.7 us: send(): return lax.ppermute(part, 'y', ring(wide, step))]
    all_to_all x1, blocking collectives: 18 us -> 20.3 us  [on_device(): part = lax.all_to_all(part, ('xl', 'z'), 0, 0, tiled=True)]
    unnamed x12 -> x10, local copies, waits for them, and re-layouts: 6.07 us -> 4.17 us
    pallas_call x5 -> x4, Pallas kernels: 13.8 us -> 12 us  [the longest x1 5.99 us: on_device(): call(functools.partial(near_kernel, size), (whole, like((columns, rows),...]
  transfers between devices with their start and end apart: 14 -> 12, of which waited for: 9 -> 8; matrix products, arithmetic and copies ran while one was open for 0% -> 0% of each run, Pallas kernels for 9% -> 9%
where the time goes in v6:
time: 105 us; the launch traced here: 103 us
  waiting for transfers between devices  40.3 us (38%)
  starting transfers between devices  21.2 us (20%)
  blocking collectives  20.3 us (19%)
  Pallas kernels  15.9 us (15%)
  local copies, waits for them, and re-layouts  4.17 us (4%)
    ppermute x6, waiting for transfers between devices, send(): return lax.ppermute(part, 'y', ring(wide, step))  20.7 us
    all_to_all x1, blocking collectives, on_device(): part = lax.all_to_all(part, ('xl', 'z'), 0, 0, tiled=True)  20.3 us
    ppermute x1, waiting for transfers between devices, on_device(): low = lax.ppermute(slab, ROWS, ring(groups, 1))  12.1 us
    ppermute x6, starting transfers between devices, send(): return lax.ppermute(part, 'y', ring(wide, step))  10.4 us
    pallas_call x1, Pallas kernels, on_device(): call(functools.partial(near_kernel, size), (whole, like((columns, rows),...  5.99 us
    ppermute x1, waiting for transfers between devices, on_device(): early_far = lax.ppermute(slab, ('xh', *ROWS), pairs[0])  4.93 us
    unnamed x10, local copies, waits for them, and re-layouts  4.17 us
    ppermute x1, starting transfers between devices, on_device(): early_far = lax.ppermute(slab, ('xh', *ROWS), pairs[0])  4.02 us
  transfers between devices with their start and end apart: 12, of which 8 were waited for; matrix products, arithmetic and copies ran while one was open for 0% of the time, Pallas kernels for 9%

profile of v6, /device:TPU:10, one launch (start us, length us, event | category | flops | bytes accessed | tf_op | source)
XLA Modules:
  0.0 102.7 jit_solution(16865325349826112155)
XLA Ops:
  0.6 2.9 %shard_map.68.slab_ref.own_ref = bf16[1024,512]{1,0:T(8,128)(2,1)} custom-call(s32[4,8]{1,0:T(4,128)} %bitcast.3, bf16[1024,512]{1,0:T(8,128)(2,1)} %slab_hbm.1), custom_call_target="tpu_custom_call" | custom-call | tf_op jit(solution)/shard_map/pallas_call | solution.py:162
  3.6 2.0 %collective-permute-start = (bf16[1024,512]{1,0:T(8,128)(2,1)}, bf16[1024,512]{1,0:T(8,128)(2,1)S(1)}, u32[]{:S(2)}, u32[]{:S(2)}) collective-permute-start(bf16[1024,512]{1,0:T(8,128)(2,1)} %shard_map.68.slab_ref.own_ref), channel_id=1, source_target_pairs={{0,1},{1,2},{2,3},{3,4},{4,5},{5,6},{6,7},{7,8},{8,9},{9,10},{10,1... | collective-permute-start | bytes 3145736 | tf_op jit(solution)/shard_map/ppermute | solution.py:171
  5.6 3.9 %collective-permute-start.1 = (bf16[1024,512]{1,0:T(8,128)(2,1)}, bf16[1024,512]{1,0:T(8,128)(2,1)S(1)}, u32[]{:S(2)}, u32[]{:S(2)}) collective-permute-start(bf16[1024,512]{1,0:T(8,128)(2,1)} %shard_map.68.slab_ref.own_ref), channel_id=1, source_target_pairs={{0,63},{1,0},{2,1},{3,2},{4,3},{5,4},{6,5},{7,6},{8,7},{9,8},{10,9... | collective-permute-start | bytes 3145736 | tf_op jit(solution)/shard_map/ppermute | solution.py:172
  9.5 4.0 %collective-permute-start.6 = (bf16[1024,512]{1,0:T(8,128)(2,1)}, bf16[1024,512]{1,0:T(8,128)(2,1)S(1)}, u32[]{:S(2)}, u32[]{:S(2)}) collective-permute-start(bf16[1024,512]{1,0:T(8,128)(2,1)} %shard_map.68.slab_ref.own_ref), channel_id=1, source_target_pairs={{0,128},{1,129},{2,130},{3,131},{4,132},{5,133},{6,134},{8,136},{9... | collective-permute-start | bytes 3145736 | tf_op jit(solution)/shard_map/ppermute | solution.py:179
  13.5 0.1 collective-permute-start.2
  13.6 1.2 %copy-done = bf16[1024,512]{1,0:T(8,128)(2,1)S(1)} copy-done((bf16[1024,512]{1,0:T(8,128)(2,1)S(1)}, bf16[1024,512]{1,0:T(8,128)(2,1)}, u32[]{:S(2)}) %copy-start) | copy-done | bytes 1048600
  14.9 2.3 %copy-done.2 = bf16[1024,2176]{1,0:T(8,128)(2,1)S(1)} copy-done((bf16[1024,2176]{1,0:T(8,128)(2,1)S(1)}, bf16[1024,2176]{1,0:T(8,128)(2,1)}, u32[]{:S(2)}) %copy-start.2) | copy-done | bytes 4456472
  17.1 0.7 copy-done.3
  17.8 2.9 %shard_map.69 = (bf16[1024,2176]{1,0:T(8,128)(2,1)S(1)}, f32[1024,512]{1,0:T(8,128)S(1)}, bf16[1024,512]{1,0:T(8,128)(2,1)S(1)}) custom-call(s32[8,17]{1,0:T(8,128)S(1)} %copy-done.3, bf16[1024,2176]{1,0:T(8,128)(2,1)S(1)} %copy-done.2, bf16[1024,512]{1,0:T(8,128)(2,1)S(1)} %copy-done), custom_call_target="tpu_custom_call" | custom-call | flops 1073741824 | bytes 8912896 | tf_op jit(solution)/shard_map/pallas_call | solution.py:180
  20.7 12.1 %collective-permute-done.low_ref.refs_1_ = bf16[1024,512]{1,0:T(8,128)(2,1)S(1)} collective-permute-done((bf16[1024,512]{1,0:T(8,128)(2,1)}, bf16[1024,512]{1,0:T(8,128)(2,1)S(1)}, u32[]{:S(2)}, u32[]{:S(2)}) %collective-permute-start) | collective-permute-done | bytes 1048608 | tf_op jit(solution)/shard_map/ppermute | solution.py:171
  32.8 0.0 collective-permute-done.1.high_ref.refs_2_
  32.8 4.9 %collective-permute-done.6.refs_3_.early_hbm = bf16[1024,512]{1,0:T(8,128)(2,1)S(1)} collective-permute-done((bf16[1024,512]{1,0:T(8,128)(2,1)}, bf16[1024,512]{1,0:T(8,128)(2,1)S(1)}, u32[]{:S(2)}, u32[]{:S(2)}) %collective-permute-start.6) | collective-permute-done | bytes 1048608 | tf_op jit(solution)/shard_map/ppermute | solution.py:179
  37.7 0.7 collective-permute-start.7
  38.4 0.0 collective-permute-done.2.near_ref
  38.5 6.0 %shard_map.70 = (bf16[1024,512]{1,0:T(8,128)(2,1)}, bf16[512,1024]{1,0:T(8,128)(2,1)S(1)}, f32[512,256]{1,0:T(8,128)S(1)}, bf16[512,256]{1,0:T(8,128)(2,1)S(1)},...) custom-call(s32[4,8]{1,0:T(4,128)S(1)} %bitcast.2, bf16[1024,2176]{1,0:T(8,128)(2,1)S(1)} %get-tuple-element.15.held_ref, ...), custom_call_target="tpu_custom_call" | custom-call | flops 2281701376 | bytes 8388608 | tf_op jit(solution)/shard_map/pallas_call | solution.py:189
  44.5 1.6 %collective-permute-start.3 = (bf16[512,256]{1,0:T(8,128)(2,1)S(1)}, bf16[512,256]{1,0:T(8,128)(2,1)S(1)}, u32[]{:S(2)}, u32[]{:S(2)}) collective-permute-start(bf16[512,256]{1,0:T(8,128)(2,1)S(1)} %get-tuple-element.19), channel_id=1, source_target_pairs={{0,8},{8,16},{16,24},{24,0},{1,9},{9,17},{17,25},{25,1},{2,10},{10... | collective-permute-start | bytes 786440 | tf_op jit(solution)/shard_map/ppermute | solution.py:199
  46.0 3.5 %collective-permute-start.4 = (bf16[512,256]{1,0:T(8,128)(2,1)S(1)}, bf16[512,256]{1,0:T(8,128)(2,1)S(1)}, u32[]{:S(2)}, u32[]{:S(2)}) collective-permute-start(bf16[512,256]{1,0:T(8,128)(2,1)S(1)} %get-tuple-element.20), channel_id=1, source_target_pairs={{0,16},{8,24},{16,0},{24,8},{1,17},{9,25},{17,1},{25,9},{2,18},{10... | collective-permute-start | bytes 786440 | tf_op jit(solution)/shard_map/ppermute | solution.py:199
  49.5 5.1 %collective-permute-done.3.refs_1_ = bf16[512,256]{1,0:T(8,128)(2,1)S(1)} collective-permute-done((bf16[512,256]{1,0:T(8,128)(2,1)S(1)}, bf16[512,256]{1,0:T(8,128)(2,1)S(1)}, u32[]{:S(2)}, u32[]{:S(2)}) %collective-permute-start.3) | collective-permute-done | bytes 262176 | tf_op jit(solution)/shard_map/ppermute | solution.py:199
  54.7 2.1 %collective-permute-done.4.refs_2_ = bf16[512,256]{1,0:T(8,128)(2,1)S(1)} collective-permute-done((bf16[512,256]{1,0:T(8,128)(2,1)S(1)}, bf16[512,256]{1,0:T(8,128)(2,1)S(1)}, u32[]{:S(2)}, u32[]{:S(2)}) %collective-permute-start.4) | collective-permute-done | bytes 262176 | tf_op jit(solution)/shard_map/ppermute | solution.py:199
  56.8 3.1 %collective-permute-done.5.refs_3_ = bf16[512,256]{1,0:T(8,128)(2,1)S(1)} collective-permute-done((bf16[512,256]{1,0:T(8,128)(2,1)S(1)}, bf16[512,256]{1,0:T(8,128)(2,1)S(1)}, u32[]{:S(2)}, u32[]{:S(2)}) %collective-permute-start.5) | collective-permute-done | bytes 262176 | tf_op jit(solution)/shard_map/ppermute | solution.py:199
  60.0 0.1 collective-permute-start.8
  60.1 2.6 %collective-permute-done.8.both_ref = bf16[1024,512]{1,0:T(8,128)(2,1)S(1)} collective-permute-done((bf16[1024,512]{1,0:T(8,128)(2,1)S(1)}, bf16[1024,512]{1,0:T(8,128)(2,1)S(1)}, u32[]{:S(2)}, u32[]{:S(2)}) %collective-permute-start.8) | collective-permute-done | bytes 1048608 | tf_op jit(solution)/shard_map/ppermute | solution.py:213
  62.7 3.0 %shard_map.74 = (f32[512,256]{1,0:T(8,128)S(1)}, bf16[512,256]{1,0:T(8,128)(2,1)S(1)}, bf16[512,256]{1,0:T(8,128)(2,1)S(1)}, bf16[512,256]{1,0:T(8,128)(2,1)S(1)}) custom-call(bf16[512,1024]{1,0:T(8,128)(2,1)S(1)} %get-tuple-element.22.outt_ref, bf16[1024,512]{1,0:T(8,128)(2,1)S(1)} %shard_map.73.far_ref, bf16[1024,512]{1,0:T(8,128)(2,1)S(1)} %collective-permute-done.8.both_ref), custom_call_target="tpu_custom_call" | custom-call | flops 1073741824 | bytes 4194304 | tf_op jit(solution)/shard_map/pallas_call | solution.py:214
  65.8 3.3 %collective-permute-start.10 = (bf16[512,256]{1,0:T(8,128)(2,1)S(1)}, bf16[512,256]{1,0:T(8,128)(2,1)S(1)}, u32[]{:S(2)}, u32[]{:S(2)}) collective-permute-start(bf16[512,256]{1,0:T(8,128)(2,1)S(1)} %get-tuple-element.26), channel_id=1, source_target_pairs={{0,16},{8,24},{16,0},{24,8},{1,17},{9,25},{17,1},{25,9},{2,18},{10... | collective-permute-start | bytes 786440 | tf_op jit(solution)/shard_map/ppermute | solution.py:199
  69.1 0.0 collective-permute-start.11
  69.1 2.0 %collective-permute-start.9 = (bf16[512,256]{1,0:T(8,128)(2,1)S(1)}, bf16[512,256]{1,0:T(8,128)(2,1)S(1)}, u32[]{:S(2)}, u32[]{:S(2)}) collective-permute-start(bf16[512,256]{1,0:T(8,128)(2,1)S(1)} %get-tuple-element.25), channel_id=1, source_target_pairs={{0,8},{8,16},{16,24},{24,0},{1,9},{9,17},{17,25},{25,1},{2,10},{10... | collective-permute-start | bytes 786440 | tf_op jit(solution)/shard_map/ppermute | solution.py:199
  71.1 5.5 %collective-permute-done.10.refs_6_ = bf16[512,256]{1,0:T(8,128)(2,1)S(1)} collective-permute-done((bf16[512,256]{1,0:T(8,128)(2,1)S(1)}, bf16[512,256]{1,0:T(8,128)(2,1)S(1)}, u32[]{:S(2)}, u32[]{:S(2)}) %collective-permute-start.10) | collective-permute-done | bytes 262176 | tf_op jit(solution)/shard_map/ppermute | solution.py:199
  76.6 4.8 %collective-permute-done.11.refs_7_ = bf16[512,256]{1,0:T(8,128)(2,1)S(1)} collective-permute-done((bf16[512,256]{1,0:T(8,128)(2,1)S(1)}, bf16[512,256]{1,0:T(8,128)(2,1)S(1)}, u32[]{:S(2)}, u32[]{:S(2)}) %collective-permute-start.11) | collective-permute-done | bytes 262176 | tf_op jit(solution)/shard_map/ppermute | solution.py:199
  81.3 0.0 collective-permute-done.9.refs_5_
  81.3 0.3 shard_map.75
  81.7 20.3 %all_to_all.5.in_ref = bf16[16,32,512]{2,1,0:T(8,128)(2,1)S(1)} all-to-all(bf16[16,32,512]{2,1,0:T(8,128)(2,1)S(1)} %shard_map.75), channel_id=1, replica_groups=mesh['xh'=2,'core'=2,'xl'=2,'y'=4,'z'=8] {'xl','z'}, dimensions={0} | all-to-all | bytes 1048576 | tf_op jit(solution)/shard_map/all_to_all | solution.py:225
  102.0 0.7 shard_map.76
  (12 shorter events, 0.0 us)
Async XLA Ops:
  0.6 37.8 %copy-start.4 = (s32[8,4]{0,1:T(4,128)S(1)}, s32[8,4]{0,1:T(4,128)}, u32[]{:S(2)}) copy-start(s32[8,4]{0,1:T(4,128)} %param.9) | copy-start | bytes 388
  3.6 29.2 %collective-permute-start = (bf16[1024,512]{1,0:T(8,128)(2,1)}, bf16[1024,512]{1,0:T(8,128)(2,1)S(1)}, u32[]{:S(2)}, u32[]{:S(2)}) collective-permute-start(bf16[1024,512]{1,0:T(8,128)(2,1)} %shard_map.68.slab_ref.own_ref), channel_id=1, source_target_pairs={{0,1},{1,2},{2,3},{3,4},{4,5},{5,6},{6,7},{7,8},{8,9},{9,10},{10,1... | collective-permute-start | bytes 3145736 | tf_op jit(solution)/shard_map/ppermute | solution.py:171
  5.6 27.2 %collective-permute-start.1 = (bf16[1024,512]{1,0:T(8,128)(2,1)}, bf16[1024,512]{1,0:T(8,128)(2,1)S(1)}, u32[]{:S(2)}, u32[]{:S(2)}) collective-permute-start(bf16[1024,512]{1,0:T(8,128)(2,1)} %shard_map.68.slab_ref.own_ref), channel_id=1, source_target_pairs={{0,63},{1,0},{2,1},{3,2},{4,3},{5,4},{6,5},{7,6},{8,7},{9,8},{10,9... | collective-permute-start | bytes 3145736 | tf_op jit(solution)/shard_map/ppermute | solution.py:172
  9.5 28.2 %collective-permute-start.6 = (bf16[1024,512]{1,0:T(8,128)(2,1)}, bf16[1024,512]{1,0:T(8,128)(2,1)S(1)}, u32[]{:S(2)}, u32[]{:S(2)}) collective-permute-start(bf16[1024,512]{1,0:T(8,128)(2,1)} %shard_map.68.slab_ref.own_ref), channel_id=1, source_target_pairs={{0,128},{1,129},{2,130},{3,131},{4,132},{5,133},{6,134},{8,136},{9... | collective-permute-start | bytes 3145736 | tf_op jit(solution)/shard_map/ppermute | solution.py:179
  13.5 24.9 %collective-permute-start.2 = (bf16[1024,512]{1,0:T(8,128)(2,1)}, bf16[1024,512]{1,0:T(8,128)(2,1)S(1)}, u32[]{:S(2)}, u32[]{:S(2)}) collective-permute-start(bf16[1024,512]{1,0:T(8,128)(2,1)} %shard_map.68.slab_ref.own_ref), channel_id=1, source_target_pairs={{0,64},{64,0},{1,65},{65,1},{2,66},{66,2},{3,67},{67,3},{4,68},{68... | collective-permute-start | bytes 3145736 | tf_op jit(solution)/shard_map/ppermute | solution.py:173
  13.6 1.2 %copy-start = (bf16[1024,512]{1,0:T(8,128)(2,1)S(1)}, bf16[1024,512]{1,0:T(8,128)(2,1)}, u32[]{:S(2)}) copy-start(bf16[1024,512]{1,0:T(8,128)(2,1)} %shard_map.68.slab_ref.own_ref) | copy-start | bytes 3145732
  14.8 2.3 %copy-start.2 = (bf16[1024,2176]{1,0:T(8,128)(2,1)S(1)}, bf16[1024,2176]{1,0:T(8,128)(2,1)}, u32[]{:S(2)}) copy-start(bf16[1024,2176]{1,0:T(8,128)(2,1)} %fock_ref.1) | copy-start | bytes 13369348
  17.1 0.7 copy-start.3
  17.8 20.7 %copy-start.1 = (bf16[1024,512]{1,0:T(8,128)(2,1)S(1)}, bf16[1024,512]{1,0:T(8,128)(2,1)}, u32[]{:S(2)}) copy-start(bf16[1024,512]{1,0:T(8,128)(2,1)} %shard_map.68.slab_ref.own_ref) | copy-start | bytes 3145732
  37.7 22.3 %collective-permute-start.7 = (bf16[1024,512]{1,0:T(8,128)(2,1)S(1)}, bf16[1024,512]{1,0:T(8,128)(2,1)S(1)}, u32[]{:S(2)}, u32[]{:S(2)}) collective-permute-start(bf16[1024,512]{1,0:T(8,128)(2,1)S(1)} %shard_map.71), channel_id=1, source_target_pairs={{7,135},{24,152},{39,167},{56,184},{135,7},{152,24},{167,39},{184,... | collective-permute-start | bytes 3145736 | tf_op jit(solution)/shard_map/ppermute | solution.py:187
  44.5 10.2 %collective-permute-start.3 = (bf16[512,256]{1,0:T(8,128)(2,1)S(1)}, bf16[512,256]{1,0:T(8,128)(2,1)S(1)}, u32[]{:S(2)}, u32[]{:S(2)}) collective-permute-start(bf16[512,256]{1,0:T(8,128)(2,1)S(1)} %get-tuple-element.19), channel_id=1, source_target_pairs={{0,8},{8,16},{16,24},{24,0},{1,9},{9,17},{17,25},{25,1},{2,10},{10... | collective-permute-start | bytes 786440 | tf_op jit(solution)/shard_map/ppermute | solution.py:199
  46.0 10.8 %collective-permute-start.4 = (bf16[512,256]{1,0:T(8,128)(2,1)S(1)}, bf16[512,256]{1,0:T(8,128)(2,1)S(1)}, u32[]{:S(2)}, u32[]{:S(2)}) collective-permute-start(bf16[512,256]{1,0:T(8,128)(2,1)S(1)} %get-tuple-element.20), channel_id=1, source_target_pairs={{0,16},{8,24},{16,0},{24,8},{1,17},{9,25},{17,1},{25,9},{2,18},{10... | collective-permute-start | bytes 786440 | tf_op jit(solution)/shard_map/ppermute | solution.py:199
  49.5 10.4 %collective-permute-start.5 = (bf16[512,256]{1,0:T(8,128)(2,1)S(1)}, bf16[512,256]{1,0:T(8,128)(2,1)S(1)}, u32[]{:S(2)}, u32[]{:S(2)}) collective-permute-start(bf16[512,256]{1,0:T(8,128)(2,1)S(1)} %get-tuple-element.21), channel_id=1, source_target_pairs={{0,24},{8,0},{16,8},{24,16},{1,25},{9,1},{17,9},{25,17},{2,26},{10... | collective-permute-start | bytes 786440 | tf_op jit(solution)/shard_map/ppermute | solution.py:199
  60.0 2.7 %collective-permute-start.8 = (bf16[1024,512]{1,0:T(8,128)(2,1)S(1)}, bf16[1024,512]{1,0:T(8,128)(2,1)S(1)}, u32[]{:S(2)}, u32[]{:S(2)}) collective-permute-start(bf16[1024,512]{1,0:T(8,128)(2,1)S(1)} %shard_map.73.far_ref), channel_id=1, source_target_pairs={{0,64},{64,0},{1,65},{65,1},{2,66},{66,2},{3,67},{67,3},{4,68},{68... | collective-permute-start | bytes 3145736 | tf_op jit(solution)/shard_map/ppermute | solution.py:213
  65.8 10.8 %collective-permute-start.10 = (bf16[512,256]{1,0:T(8,128)(2,1)S(1)}, bf16[512,256]{1,0:T(8,128)(2,1)S(1)}, u32[]{:S(2)}, u32[]{:S(2)}) collective-permute-start(bf16[512,256]{1,0:T(8,128)(2,1)S(1)} %get-tuple-element.26), channel_id=1, source_target_pairs={{0,16},{8,24},{16,0},{24,8},{1,17},{9,25},{17,1},{25,9},{2,18},{10... | collective-permute-start | bytes 786440 | tf_op jit(solution)/shard_map/ppermute | solution.py:199
  69.1 12.3 %collective-permute-start.11 = (bf16[512,256]{1,0:T(8,128)(2,1)S(1)}, bf16[512,256]{1,0:T(8,128)(2,1)S(1)}, u32[]{:S(2)}, u32[]{:S(2)}) collective-permute-start(bf16[512,256]{1,0:T(8,128)(2,1)S(1)} %get-tuple-element.27), channel_id=1, source_target_pairs={{0,24},{8,0},{16,8},{24,16},{1,25},{9,1},{17,9},{25,17},{2,26},{10... | collective-permute-start | bytes 786440 | tf_op jit(solution)/shard_map/ppermute | solution.py:199
  69.1 12.3 %collective-permute-start.9 = (bf16[512,256]{1,0:T(8,128)(2,1)S(1)}, bf16[512,256]{1,0:T(8,128)(2,1)S(1)}, u32[]{:S(2)}, u32[]{:S(2)}) collective-permute-start(bf16[512,256]{1,0:T(8,128)(2,1)S(1)} %get-tuple-element.25), channel_id=1, source_target_pairs={{0,8},{8,16},{16,24},{24,0},{1,9},{9,17},{17,25},{25,1},{2,10},{10... | collective-permute-start | bytes 786440 | tf_op jit(solution)/shard_map/ppermute | solution.py:199

commit v7 on v6

v7 whole, which is shorter than its diff:
```python
import functools
import math

import jax
import jax.numpy as jnp
from jax import lax
from jax.experimental import pallas as pl
from jax.experimental.pallas import tpu as pltpu
from jax.sharding import Mesh, PartitionSpec as P

F32, BF16 = jnp.float32, jnp.bfloat16
ROWS = ("xl", "y", "z")
BLK = ("xh", "core")
VMEM = pl.BlockSpec(memory_space=pltpu.VMEM)
SMEM = pl.BlockSpec(memory_space=pltpu.SMEM)
HBM = pl.BlockSpec(memory_space=pltpu.HBM)
MIB = 1 << 20


def call(body, outs, ins, scratch=(), limit=8 * MIB, flops=0, moved=0, place=VMEM):
    return pl.pallas_call(
        body,
        out_shape=outs,
        in_specs=ins,
        out_specs=jax.tree.map(lambda _: place, outs),
        scratch_shapes=list(scratch),
        compiler_params=pltpu.CompilerParams(vmem_limit_bytes=limit),
        cost_estimate=pl.CostEstimate(flops=flops, bytes_accessed=moved, transcendentals=0),
    )


def dot(a, b):
    return jnp.dot(a, b, preferred_element_type=F32)


def mask_kernel(size, mask_ref, slab_hbm, out_hbm, top_hbm, low_hbm, held, in_sems, out_sems):
    panels, blocks = mask_ref.shape
    at = [pl.ds(i * size, size) for i in range(blocks)]
    loads = [pltpu.make_async_copy(slab_hbm.at[at[i]], held.at[at[i]], in_sems.at[i]) for i in range(blocks)]
    stores = []
    for load in loads:
        load.start()
    for i in range(blocks):
        loads[i].wait()
        for j in range(panels):
            cols = pl.ds(j * size, size)
            tile = held[at[i], cols]
            held[at[i], cols] = jnp.where(mask_ref[j, i] != 0, tile, jnp.zeros_like(tile))
        part = (top_hbm, low_hbm)[i // (blocks // 2)].at[at[i % (blocks // 2)]]
        for k, to in enumerate((out_hbm.at[at[i]], part)):
            stores.append(pltpu.make_async_copy(held.at[at[i]], to, out_sems.at[i, k]))
            stores[-1].start()
    for store in stores:
        store.wait()


def middle_kernel(size, fmask_ref, fock_ref, slab_ref, held_ref, mid_ref):
    blocks, slots = fmask_ref.shape
    for i in range(blocks):
        rows = pl.ds(i * size, size)
        for o in range(slots):
            cols = pl.ds(o * size, size)
            tile = fock_ref[rows, cols]
            held_ref[rows, cols] = jnp.where(fmask_ref[i, o] != 0, tile, jnp.zeros_like(tile))
        mid_ref[rows, :] = dot(held_ref[rows, pl.ds((blocks - i) * size, blocks * size)], slab_ref[...])


def product_kernel(size, rmask_ref, held_ref, mid_ref, low_ref, high_ref, out_ref, outt_ref):
    panels, blocks = rmask_ref.shape
    slots = held_ref.shape[1] // size
    for i in range(blocks):
        rows = pl.ds(i * size, size)
        total = mid_ref[rows, :]
        total += dot(held_ref[rows, : (blocks - i) * size], low_ref[i * size :, :])
        total += dot(held_ref[rows, (2 * blocks - i) * size :], high_ref[: (slots - 2 * blocks + i) * size, :])
        for j in range(panels):
            cols = slice(j * size, (j + 1) * size)
            tile = total[:, cols]
            tile = jnp.where(rmask_ref[j, i] != 0, tile, jnp.zeros_like(tile)).astype(BF16)
            out_ref[rows, cols] = tile
            outt_ref[cols, rows] = tile.T


def merge_kernel(edge, direct_hbm, top_hbm, low_hbm, out_hbm, sems):
    @pl.when(crossing(edge, lax.axis_index("y"), lax.axis_index("z")))
    def _():
        count = top_hbm.shape[0]
        copies = [
            pltpu.make_async_copy(part, out_hbm.at[pl.ds(k * count, count)], sems.at[k])
            for k, part in enumerate((top_hbm, low_hbm))
        ]
        for copy in copies:
            copy.start()
        for copy in copies:
            copy.wait()


def crossing(edge, y, z):
    return ((y == edge[0] - 1) & (z == 0)) | ((y == 0) & (z == edge[1] - 1))


def terms_kernel(flipped_ref, *refs):
    *panel_refs, out_ref = refs
    half = out_ref.shape[2]
    core = lax.axis_index("core")
    for q, ref in enumerate(panel_refs):
        for k in range(2):
            terms = dot(flipped_ref[...], ref[:, pl.ds(k * half, half)]).astype(BF16)
            at = k if len(panel_refs) == 1 else (core ^ q) * 2 + k
            out_ref[at] = terms


def gather_kernel(flipped_ref, both_ref, near_ref, far_ref, out_ref):
    half = out_ref.shape[2]
    core, xh = lax.axis_index("core"), lax.axis_index("xh")
    other = (1 - xh) * 4
    for k in range(2):
        terms = dot(flipped_ref[...], both_ref[:, pl.ds(k * half, half)])
        out_ref[other + (1 - core) * 2 + k] = terms.astype(BF16)
        out_ref[other + core * 2 + k] = far_ref[k]
    for s in range(4):
        out_ref[xh * 4 + s] = near_ref[s]


def first_sum_kernel(in_ref, out_ref):
    total = in_ref[0].astype(F32)
    for s in range(1, in_ref.shape[0]):
        total += in_ref[s].astype(F32)
    out_ref[...] = total.T.astype(BF16)


def last_sum_kernel(factor, in_ref, out_ref):
    total = in_ref[0].astype(F32)
    for s in range(1, in_ref.shape[0]):
        total += in_ref[s].astype(F32)
    out_ref[...] = total * factor


def after(x, *others):
    anywhere = pl.BlockSpec(memory_space=pl.ANY)
    return pl.pallas_call(
        lambda *refs: None,
        out_shape=jax.ShapeDtypeStruct(x.shape, x.dtype),
        in_specs=[anywhere] * (1 + len(others)),
        out_specs=anywhere,
        input_output_aliases={0: 0},
        compiler_params=pltpu.CompilerParams(vmem_limit_bytes=MIB),
    )(x, *others)


def ring(count, step):
    return [(i, (i + step) % count) for i in range(count)]


def on_device(fock_band, fock_slot_mask, orbital_slab, orbital_mask, result_mask):
    blocks, slots = fock_slot_mask.shape
    rows, columns = orbital_slab.shape
    size = rows // blocks
    half = columns // 2
    like = jax.ShapeDtypeStruct
    groups, wide, deep = lax.axis_size(ROWS), lax.axis_size("y"), lax.axis_size("z")
    whole, part = like((rows, columns), BF16), like((rows // 2, columns), BF16)
    slab, top, bottom = call(
        functools.partial(mask_kernel, size),
        (whole, part, part),
        [SMEM, HBM],
        [
            pltpu.VMEM((rows, columns), BF16),
            pltpu.SemaphoreType.DMA((blocks,)),
            pltpu.SemaphoreType.DMA((blocks, 2)),
        ],
        limit=60 * MIB,
        place=HBM,
    )(orbital_mask.T, orbital_slab)
    swap = ring(2, 1)
    low = lax.ppermute(slab, ROWS, ring(groups, 1))
    high = lax.ppermute(slab, ROWS, ring(groups, groups - 1))
    near_slab = lax.ppermute(slab, "core", swap)
    edge = (wide, deep)
    every = ("xh", *ROWS)
    direct, out, back = [], ([], []), ([], [])
    for i in range(2 * groups):
        partner = (i + groups) % (2 * groups)
        y, z = i // deep % wide, i % deep
        if not crossing(edge, y, z):
            direct.append((i, partner))
            continue
        for k, shift in enumerate((1, wide - 1)):
            relay = i + ((y + shift) % wide - y) * deep
            out[k].append((i, relay))
            back[k].append((relay, partner))
    far = lax.ppermute(slab, every, direct)
    sent = [lax.ppermute(x, every, pairs) for x, pairs in zip((top, bottom), out)]
    late = [lax.ppermute(x, every, pairs) for x, pairs in zip(sent, back)]
    held, mid = call(
        functools.partial(middle_kernel, size),
        (like((rows, slots * size), BF16), like((rows, columns), F32)),
        [SMEM, VMEM, VMEM],
        flops=2 * rows * rows * columns,
        moved=4 * rows * slots * size,
    )(fock_slot_mask, fock_band, slab)
    product, flipped = call(
        functools.partial(product_kernel, size),
        (whole, like((columns, rows), BF16)),
        [SMEM] + [VMEM] * 4,
        flops=2 * rows * columns * (slots - blocks) * size,
        moved=16 * rows * columns,
    )(result_mask.T, held, mid, low, high)
    anywhere = pl.BlockSpec(memory_space=pl.ANY)
    far = pl.pallas_call(
        functools.partial(merge_kernel, edge),
        out_shape=whole,
        in_specs=[anywhere] * 3,
        out_specs=anywhere,
        scratch_shapes=[pltpu.SemaphoreType.DMA((2,))],
        input_output_aliases={0: 0},
        compiler_params=pltpu.CompilerParams(vmem_limit_bytes=MIB),
    )(far, late[0], after(late[1], flipped))
    both = lax.ppermute(far, "core", swap)

    def terms(count, *panels):
        return call(
            terms_kernel,
            like((count, columns, half), BF16),
            [VMEM] * (1 + len(panels)),
            flops=2 * rows * columns * count * half,
            moved=2 * rows * columns * 4,
        )(flipped, *panels)

    pieces = call(
        gather_kernel,
        like((8, columns, half), BF16),
        [VMEM] * 4,
        flops=2 * rows * columns * columns,
        moved=8 * rows * columns,
    )(flipped, both, terms(4, slab, near_slab), terms(2, far))
    pieces = lax.all_to_all(pieces, ("xl", "y"), 0, 0, tiled=True)
    part = call(first_sum_kernel, like((half, columns), BF16), [VMEM])(pieces)
    part = part.reshape(deep, half // deep, columns)
    part = lax.all_to_all(part, "z", 0, 0, tiled=True)
    factor = 1.0 / math.sqrt(rows * groups)
    projected = call(
        functools.partial(last_sum_kernel, factor), like((half // deep, columns), F32), [VMEM]
    )(part)
    return (product, projected)


def solution(mesh):
    split = Mesh(mesh.devices.reshape(2, 2, 2, 4, 8), BLK + ROWS)
    placed = (P(ROWS, None), P(ROWS, None), P(ROWS, BLK), P(ROWS, BLK), P(ROWS, BLK))
    return jax.shard_map(
        on_device,
        mesh=split,
        in_specs=placed,
        out_specs=(P(ROWS, BLK), P(ROWS, BLK)),
        check_vma=False,
    )
```

time: 105 us -> 116 us (1.10); the launches traced: 103 us -> 115 us
  blocking collectives: 20.3 us -> 71.8 us
  waiting for transfers between devices: 40.3 us -> 12.6 us
  starting transfers between devices: 21.2 us -> 12.9 us
  Pallas kernels: 15.9 us -> 12.8 us
    all_to_all x1 -> x2, blocking collectives: 20.3 us -> 71.8 us  [the longest x1 54.7 us: on_device(): pieces = lax.all_to_all(pieces, ('xl', 'y'), 0, 0, tiled=True)]
    ppermute x8 -> x5, waiting for transfers between devices: 25.6 us -> 2.65 us  [the longest x1 2.64 us: on_device(): far = lax.ppermute(slab, every, direct)]
    ppermute x8 -> x5, starting transfers between devices: 15.1 us -> 6.93 us  [the longest x1 4.03 us: on_device(): far = lax.ppermute(slab, every, direct)]
    pallas_call x4 -> x6, Pallas kernels: 12.3 us -> 9.26 us  [the longest x1 3.13 us: on_device(): call(functools.partial(mask_kernel, size), (whole, part, part), [SMEM, HB...]
    ppermute x1, waiting for transfers between devices: 12.1 us -> 9.29 us  [on_device(): low = lax.ppermute(slab, ROWS, ring(groups, 1))]
    ppermute x1, waiting for transfers between devices: 2.65 us -> 0.66 us  [on_device(): both = lax.ppermute(far, 'core', swap)]
    unnamed x10 -> x8, local copies, waits for them, and re-layouts: 4.17 us -> 4.17 us
  transfers between devices with their start and end apart: 12 -> 9, of which waited for: 8 -> 3; matrix products, arithmetic and copies ran while one was open for 0% -> 0% of each run, Pallas kernels for 9% -> 7%
where the time goes in v7:
time: 116 us; the launch traced here: 115 us
  blocking collectives  71.8 us (62%)
  starting transfers between devices  12.9 us (11%)
  Pallas kernels  12.8 us (11%)
  waiting for transfers between devices  12.6 us (11%)
  local copies, waits for them, and re-layouts  4.17 us (4%)
    all_to_all x1, blocking collectives, on_device(): pieces = lax.all_to_all(pieces, ('xl', 'y'), 0, 0, tiled=True)  54.7 us
    all_to_all x1, blocking collectives, on_device(): part = lax.all_to_all(part, 'z', 0, 0, tiled=True)  17.2 us
    ppermute x1, waiting for transfers between devices, on_device(): low = lax.ppermute(slab, ROWS, ring(groups, 1))  9.29 us
    unnamed x8, local copies, waits for them, and re-layouts  4.17 us
    ppermute x1, starting transfers between devices, on_device(): far = lax.ppermute(slab, every, direct)  4.03 us
    ppermute x1, starting transfers between devices, on_device(): high = lax.ppermute(slab, ROWS, ring(groups, groups - 1))  3.91 us
    pallas_call x1, Pallas kernels, on_device(): call(functools.partial(mask_kernel, size), (whole, part, part), [SMEM, HB...  3.13 us
    pallas_call x1, Pallas kernels, on_device(): call(functools.partial(product_kernel, size), (whole, like((columns, rows...  3.11 us
  transfers between devices with their start and end apart: 9, of which 3 were waited for; matrix products, arithmetic and copies ran while one was open for 0% of the time, Pallas kernels for 7%

profile of v7, /device:TPU:10, one launch (start us, length us, event | category | flops | bytes accessed | tf_op | source)
XLA Modules:
  0.0 115.1 jit_solution(17992805598973742982)
XLA Ops:
  0.6 3.1 %shard_map.68 = (bf16[1024,512]{1,0:T(8,128)(2,1)}, bf16[512,512]{1,0:T(8,128)(2,1)}, bf16[512,512]{1,0:T(8,128)(2,1)}) custom-call(s32[4,8]{1,0:T(4,128)} %bitcast.5, bf16[1024,512]{1,0:T(8,128)(2,1)} %slab_hbm.1), custom_call_target="tpu_custom_call" | custom-call | tf_op jit(solution)/shard_map/pallas_call | solution.py:163
  3.8 2.0 %collective-permute-start = (bf16[1024,512]{1,0:T(8,128)(2,1)}, bf16[1024,512]{1,0:T(8,128)(2,1)S(1)}, u32[]{:S(2)}, u32[]{:S(2)}) collective-permute-start(bf16[1024,512]{1,0:T(8,128)(2,1)} %get-tuple-element.9.slab_ref.refs_0_), channel_id=1, source_target_pairs={{0,1},{1,2},{2,3},{3,4},{4,5},{5,6},{6,7},{7,8},{8,9},{9,10},{10,1... | collective-permute-start | bytes 3145736 | tf_op jit(solution)/shard_map/ppermute | solution.py:176
  5.8 3.9 %collective-permute-start.1 = (bf16[1024,512]{1,0:T(8,128)(2,1)}, bf16[1024,512]{1,0:T(8,128)(2,1)S(1)}, u32[]{:S(2)}, u32[]{:S(2)}) collective-permute-start(bf16[1024,512]{1,0:T(8,128)(2,1)} %get-tuple-element.9.slab_ref.refs_0_), channel_id=1, source_target_pairs={{0,63},{1,0},{2,1},{3,2},{4,3},{5,4},{6,5},{7,6},{8,7},{9,8},{10,9... | collective-permute-start | bytes 3145736 | tf_op jit(solution)/shard_map/ppermute | solution.py:177
  9.7 0.8 collective-permute-start.5
  10.5 4.0 %collective-permute-start.2 = (bf16[1024,512]{1,0:T(8,128)(2,1)}, bf16[1024,512]{1,0:T(8,128)(2,1)S(1)}, u32[]{:S(2)}, u32[]{:S(2)}) collective-permute-start(bf16[1024,512]{1,0:T(8,128)(2,1)} %get-tuple-element.9.slab_ref.refs_0_), channel_id=1, source_target_pairs={{0,128},{1,129},{2,130},{3,131},{4,132},{5,133},{6,134},{8,136},{9... | collective-permute-start | bytes 3145736 | tf_op jit(solution)/shard_map/ppermute | solution.py:192
  14.5 0.7 collective-permute-start.3
  15.2 0.0 collective-permute-done.5
  15.3 0.7 collective-permute-start.6
  16.0 0.0 collective-permute-done.3
  16.0 0.7 collective-permute-start.4
  16.7 0.0 copy-start
  16.7 2.3 %copy-done = bf16[1024,2176]{1,0:T(8,128)(2,1)S(1)} copy-done((bf16[1024,2176]{1,0:T(8,128)(2,1)S(1)}, bf16[1024,2176]{1,0:T(8,128)(2,1)}, u32[]{:S(2)}) %copy-start) | copy-done | bytes 4456472
  18.9 1.2 %copy-done.1 = bf16[1024,512]{1,0:T(8,128)(2,1)S(1)} copy-done((bf16[1024,512]{1,0:T(8,128)(2,1)S(1)}, bf16[1024,512]{1,0:T(8,128)(2,1)}, u32[]{:S(2)}) %copy-start.1) | copy-done | bytes 1048600
  20.2 0.7 copy-done.2
  20.8 2.8 %shard_map.69 = (bf16[1024,2176]{1,0:T(8,128)(2,1)S(1)}, f32[1024,512]{1,0:T(8,128)S(1)}) custom-call(s32[8,17]{1,0:T(8,128)S(1)} %copy-done.2, bf16[1024,2176]{1,0:T(8,128)(2,1)S(1)} %copy-done, bf16[1024,512]{1,0:T(8,128)(2,1)S(1)} %copy-done.1), custom_call_target="tpu_custom_call" | custom-call | flops 1073741824 | bytes 8912896 | tf_op jit(solution)/shard_map/pallas_call | solution.py:195
  23.7 9.3 %collective-permute-done.low_ref = bf16[1024,512]{1,0:T(8,128)(2,1)S(1)} collective-permute-done((bf16[1024,512]{1,0:T(8,128)(2,1)}, bf16[1024,512]{1,0:T(8,128)(2,1)S(1)}, u32[]{:S(2)}, u32[]{:S(2)}) %collective-permute-start) | collective-permute-done | bytes 1048608 | tf_op jit(solution)/shard_map/ppermute | solution.py:176
  33.0 0.0 collective-permute-start.8
  33.0 0.0 collective-permute-done.1.high_ref
  33.0 3.1 %shard_map.70 = (bf16[1024,512]{1,0:T(8,128)(2,1)}, bf16[512,1024]{1,0:T(8,128)(2,1)S(1)}) custom-call(s32[4,8]{1,0:T(4,128)S(1)} %bitcast.4, bf16[1024,2176]{1,0:T(8,128)(2,1)S(1)} %get-tuple-element.10.held_ref, f32[1024,512]{1,0:T(8,128)S(1)} %get-tuple-element.11.mid_ref, bf16[1024,512]{1,0:T(8,128)(2,1)S(1)} %collective-permute-done.low_ref, ...), custom_call_target="tpu_custom_call" | custom-call | flops 1207959552 | bytes 8388608 | tf_op jit(solution)/shard_map/pallas_call | solution.py:202
  36.1 0.0 collective-permute-done.6.refs_0_
  36.1 2.6 %collective-permute-done.2.direct_hbm = bf16[1024,512]{1,0:T(8,128)(2,1)S(1)} collective-permute-done((bf16[1024,512]{1,0:T(8,128)(2,1)}, bf16[1024,512]{1,0:T(8,128)(2,1)S(1)}, u32[]{:S(2)}, u32[]{:S(2)}) %collective-permute-start.2) | collective-permute-done | bytes 1048608 | tf_op jit(solution)/shard_map/ppermute | solution.py:192
  38.7 0.0 collective-permute-done.4.top_hbm
  38.8 0.1 collective-permute-start.7
  38.9 0.7 shard_map.74.far_ref
  39.6 0.0 collective-permute-done.8.refs_1_
  39.6 1.3 %shard_map.73.near_ref = bf16[4,512,256]{2,1,0:T(8,128)(2,1)S(1)} custom-call(bf16[512,1024]{1,0:T(8,128)(2,1)S(1)} %get-tuple-element.13.refs_1_.flipped_ref, bf16[1024,512]{1,0:T(8,128)(2,1)S(1)} %copy-done.1, bf16[1024,512]{1,0:T(8,128)(2,1)S(1)} %collective-permute-done.8.refs_1_), custom_call_target="tpu_custom_call" | custom-call | flops 1073741824 | bytes 4194304 | tf_op jit(solution)/shard_map/pallas_call | solution.py:222
  40.8 0.7 collective-permute-done.7.both_ref
  41.5 0.7 shard_map.75
  42.2 54.7 %all_to_all.10.in_ref = bf16[8,512,256]{2,1,0:T(8,128)(2,1)S(1)} all-to-all(bf16[8,512,256]{2,1,0:T(8,128)(2,1)S(1)} %shard_map.75), channel_id=1, replica_groups=mesh['xh'=2,'core'=2,'xl'=2,'y'=4,'z'=8] {'xl','y'}, dimensions={0} | all-to-all | bytes 4194304 | tf_op jit(solution)/shard_map/all_to_all | solution.py:237
  96.9 0.3 shard_map.76
  97.3 17.2 %all_to_all.11.in_ref = bf16[8,32,512]{2,1,0:T(8,128)(2,1)S(1)} all-to-all(bf16[8,32,512]{2,1,0:T(8,128)(2,1)S(1)} %bitcast.3), channel_id=1, replica_groups=mesh['xh'=2,'core'=2,'xl'=2,'y'=4,'z'=8] {'z'}, dimensions={0} | all-to-all | bytes 524288 | tf_op jit(solution)/shard_map/all_to_all | solution.py:240
  114.4 0.7 shard_map.77
  (6 shorter events, 0.0 us)
Async XLA Ops:
  3.8 29.2 %collective-permute-start = (bf16[1024,512]{1,0:T(8,128)(2,1)}, bf16[1024,512]{1,0:T(8,128)(2,1)S(1)}, u32[]{:S(2)}, u32[]{:S(2)}) collective-permute-start(bf16[1024,512]{1,0:T(8,128)(2,1)} %get-tuple-element.9.slab_ref.refs_0_), channel_id=1, source_target_pairs={{0,1},{1,2},{2,3},{3,4},{4,5},{5,6},{6,7},{7,8},{8,9},{9,10},{10,1... | collective-permute-start | bytes 3145736 | tf_op jit(solution)/shard_map/ppermute | solution.py:176
  5.8 27.2 %collective-permute-start.1 = (bf16[1024,512]{1,0:T(8,128)(2,1)}, bf16[1024,512]{1,0:T(8,128)(2,1)S(1)}, u32[]{:S(2)}, u32[]{:S(2)}) collective-permute-start(bf16[1024,512]{1,0:T(8,128)(2,1)} %get-tuple-element.9.slab_ref.refs_0_), channel_id=1, source_target_pairs={{0,63},{1,0},{2,1},{3,2},{4,3},{5,4},{6,5},{7,6},{8,7},{9,8},{10,9... | collective-permute-start | bytes 3145736 | tf_op jit(solution)/shard_map/ppermute | solution.py:177
  9.7 23.3 %copy-start.3 = (s32[8,4]{0,1:T(4,128)S(1)}, s32[8,4]{0,1:T(4,128)}, u32[]{:S(2)}) copy-start(s32[8,4]{0,1:T(4,128)} %param.9) | copy-start | bytes 388
  9.7 5.6 %collective-permute-start.5 = (bf16[512,512]{1,0:T(8,128)(2,1)}, bf16[512,512]{1,0:T(8,128)(2,1)S(1)}, u32[]{:S(2)}, u32[]{:S(2)}) collective-permute-start(bf16[512,512]{1,0:T(8,128)(2,1)} %get-tuple-element.15), channel_id=1, source_target_pairs={{7,31},{24,16},{39,63},{56,48},{135,159},{152,144},{167,191},{184,... | collective-permute-start | bytes 1572872 | tf_op jit(solution)/shard_map/ppermute | solution.py:193
  10.5 28.2 %collective-permute-start.2 = (bf16[1024,512]{1,0:T(8,128)(2,1)}, bf16[1024,512]{1,0:T(8,128)(2,1)S(1)}, u32[]{:S(2)}, u32[]{:S(2)}) collective-permute-start(bf16[1024,512]{1,0:T(8,128)(2,1)} %get-tuple-element.9.slab_ref.refs_0_), channel_id=1, source_target_pairs={{0,128},{1,129},{2,130},{3,131},{4,132},{5,133},{6,134},{8,136},{9... | collective-permute-start | bytes 3145736 | tf_op jit(solution)/shard_map/ppermute | solution.py:192
  14.5 1.4 %collective-permute-start.3 = (bf16[512,512]{1,0:T(8,128)(2,1)}, bf16[512,512]{1,0:T(8,128)(2,1)S(1)}, u32[]{:S(2)}, u32[]{:S(2)}) collective-permute-start(bf16[512,512]{1,0:T(8,128)(2,1)} %get-tuple-element.14), channel_id=1, source_target_pairs={{7,15},{24,0},{39,47},{56,32},{135,143},{152,128},{167,175},{184,1... | collective-permute-start | bytes 1572872 | tf_op jit(solution)/shard_map/ppermute | solution.py:193
  15.3 20.8 %collective-permute-start.6 = (bf16[512,512]{1,0:T(8,128)(2,1)S(1)}, bf16[512,512]{1,0:T(8,128)(2,1)S(1)}, u32[]{:S(2)}, u32[]{:S(2)}) collective-permute-start(bf16[512,512]{1,0:T(8,128)(2,1)S(1)} %collective-permute-done.5), channel_id=1, source_target_pairs={{31,135},{16,152},{63,167},{48,184},{159,7},{144,24},{191,39},{176... | collective-permute-start | bytes 1572872 | tf_op jit(solution)/shard_map/ppermute | solution.py:194
  16.0 22.8 %collective-permute-start.4 = (bf16[512,512]{1,0:T(8,128)(2,1)S(1)}, bf16[512,512]{1,0:T(8,128)(2,1)S(1)}, u32[]{:S(2)}, u32[]{:S(2)}) collective-permute-start(bf16[512,512]{1,0:T(8,128)(2,1)S(1)} %collective-permute-done.3), channel_id=1, source_target_pairs={{15,135},{0,152},{47,167},{32,184},{143,7},{128,24},{175,39},{160,... | collective-permute-start | bytes 1572872 | tf_op jit(solution)/shard_map/ppermute | solution.py:194
  16.7 2.3 %copy-start = (bf16[1024,2176]{1,0:T(8,128)(2,1)S(1)}, bf16[1024,2176]{1,0:T(8,128)(2,1)}, u32[]{:S(2)}) copy-start(bf16[1024,2176]{1,0:T(8,128)(2,1)} %fock_ref.1) | copy-start | bytes 13369348
  18.9 1.2 %copy-start.1 = (bf16[1024,512]{1,0:T(8,128)(2,1)S(1)}, bf16[1024,512]{1,0:T(8,128)(2,1)}, u32[]{:S(2)}) copy-start(bf16[1024,512]{1,0:T(8,128)(2,1)} %get-tuple-element.9.slab_ref.refs_0_) | copy-start | bytes 3145732
  20.2 0.7 copy-start.2
  33.0 6.6 %collective-permute-start.8 = (bf16[1024,512]{1,0:T(8,128)(2,1)S(1)}, bf16[1024,512]{1,0:T(8,128)(2,1)S(1)}, u32[]{:S(2)}, u32[]{:S(2)}) collective-permute-start(bf16[1024,512]{1,0:T(8,128)(2,1)S(1)} %copy-done.1), channel_id=1, source_target_pairs={{0,64},{64,0},{1,65},{65,1},{2,66},{66,2},{3,67},{67,3},{4,68},{68... | collective-permute-start | bytes 3145736 | tf_op jit(solution)/shard_map/ppermute | solution.py:178
  38.8 2.7 %collective-permute-start.7 = (bf16[1024,512]{1,0:T(8,128)(2,1)S(1)}, bf16[1024,512]{1,0:T(8,128)(2,1)S(1)}, u32[]{:S(2)}, u32[]{:S(2)}) collective-permute-start(bf16[1024,512]{1,0:T(8,128)(2,1)S(1)} %shard_map.72.refs_0_), channel_id=1, source_target_pairs={{0,64},{64,0},{1,65},{65,1},{2,66},{66,2},{3,67},{67,3},{4,68},{68... | collective-permute-start | bytes 3145736 | tf_op jit(solution)/shard_map/ppermute | solution.py:219

commit v8 on v4

--- a/solution.py
+++ b/solution.py
@@ -120,23 +120,32 @@
             terms_ref[c, pl.ds(k * half, half), :] = dot(t[...], far_ref[c]).astype(BF16)
 
 
-def gather_kernel(t0_ref, t1_ref, both_ref, near0_ref, near1_ref, far_ref, out_ref):
+def gather_kernel(t0_ref, t1_ref, both_ref, near0_ref, near1_ref, far_ref, *refs):
+    *out_refs, held = refs
     half = t0_ref.shape[0]
-    core, xh = lax.axis_index("core"), lax.axis_index("xh")
-    other = (1 - xh) * 4
+    core, xh, xl, y = (lax.axis_index(name) for name in ("core", "xh", "xl", "y"))
     for c in range(2):
-        out_ref[other + core * 2 + c] = far_ref[c]
+        held[core * 2 + c] = far_ref[c]
         for k, t in enumerate((t0_ref, t1_ref)):
-            out_ref[other + (1 - core) * 2 + c, pl.ds(k * half, half), :] = dot(t[...], both_ref[c]).astype(BF16)
-    for s in range(4):
-        for k, ref in enumerate((near0_ref, near1_ref)):
-            out_ref[xh * 4 + s, pl.ds(k * half, half), :] = ref[s]
-
-
-def first_sum_kernel(in_ref, out_ref):
-    total = in_ref[0].astype(F32)
-    for s in range(1, in_ref.shape[0]):
-        total += in_ref[s].astype(F32)
+            held[(1 - core) * 2 + c, pl.ds(k * half, half), :] = dot(t[...], both_ref[c]).astype(BF16)
+    count = len(out_refs) // 2
+    for near_here in (True, False):
+
+        @pl.when((xh == xl) == near_here)
+        def _():
+            for s in range(count):
+                to = lax.rem(y + s, count)
+                near, far = (out_refs[s], out_refs[count + s])[:: 1 if near_here else -1]
+                for k, ref in enumerate((near0_ref, near1_ref)):
+                    near[pl.ds(k * half, half), :] = ref[to]
+                far[...] = held[to]
+
+
+def first_sum_kernel(*refs):
+    *in_refs, out_ref = refs
+    total = in_refs[0][...].astype(F32)
+    for ref in in_refs[1:]:
+        total += ref[...].astype(F32)
     out_ref[...] = total.T.astype(BF16)
 
 
@@ -227,15 +236,20 @@
         flops=4 * rows * half * columns,
         moved=8 * rows * half,
     )(flipped0, flipped1, far)
-    terms = call(
+    piece = like((columns, half), BF16)
+    pieces = list(call(
         gather_kernel,
-        like((groups // deep, columns, half), BF16),
+        [piece] * (2 * wide),
         [VMEM] * 6,
+        [pltpu.VMEM((wide, columns, half), BF16)],
         flops=4 * rows * half * columns,
         moved=8 * rows * columns,
-    )(flipped0, flipped1, both, terms0, terms1, far_terms)
-    terms = lax.all_to_all(terms, ("xl", "y"), 0, 0, tiled=True)
-    part = call(first_sum_kernel, like((half, columns), BF16), [VMEM])(terms)
+    )(flipped0, flipped1, both, terms0, terms1, far_terms))
+    for step in range(1, 2 * wide):
+        across, along = divmod(step, wide)
+        pairs = [(x * wide + y, (x ^ across) * wide + (y + along) % wide) for x in range(2) for y in range(wide)]
+        pieces[step] = lax.ppermute(pieces[step], ("xl", "y"), pairs)
+    part = call(first_sum_kernel, like((half, columns), BF16), [VMEM] * (2 * wide), limit=12 * MIB)(*pieces)
     part = part.reshape(deep, half // deep, columns)
     part = lax.all_to_all(part, "z", 0, 0, tiled=True)
     factor = 1.0 / math.sqrt(rows * groups)

time: 98.3 us -> 104 us (1.058)
  blocking collectives: 50.6 us -> 13.3 us
  starting transfers between devices: 13 us -> 40.5 us
  waiting for transfers between devices: 14 us -> 29.2 us
    all_to_all x1 -> x0, blocking collectives: 36 us -> none  [on_device(): terms = lax.all_to_all(terms, ('xl', 'y'), 0, 0, tiled=True)]
    ppermute x0 -> x7, starting transfers between devices: none -> 27.5 us  [on_device(): pieces[step] = lax.ppermute(pieces[step], ('xl', 'y'), pairs)]
    ppermute x0 -> x7, waiting for transfers between devices: none -> 15.2 us  [on_device(): pieces[step] = lax.ppermute(pieces[step], ('xl', 'y'), pairs)]
    all_to_all x1, blocking collectives: 14.5 us -> 13.3 us  [on_device(): part = lax.all_to_all(part, 'z', 0, 0, tiled=True)]
  transfers between devices with their start and end apart: 8 -> 15, of which waited for: 3 -> 6; matrix products, arithmetic and copies ran while one was open for 0% -> 0% of each run, Pallas kernels for 9% -> 8%
where the time goes in v8:
time: 104 us; the launch traced here: 103 us
  starting transfers between devices  40.5 us (39%)
  waiting for transfers between devices  29.2 us (28%)
  Pallas kernels  13.6 us (13%)
  blocking collectives  13.3 us (13%)
  local copies, waits for them, and re-layouts  6.07 us (6%)
    ppermute x7, starting transfers between devices, on_device(): pieces[step] = lax.ppermute(pieces[step], ('xl', 'y'), pairs)  27.5 us
    ppermute x7, waiting for transfers between devices, on_device(): pieces[step] = lax.ppermute(pieces[step], ('xl', 'y'), pairs)  15.2 us
    all_to_all x1, blocking collectives, on_device(): part = lax.all_to_all(part, 'z', 0, 0, tiled=True)  13.3 us
    ppermute x1, waiting for transfers between devices, on_device(): low1 = lax.ppermute(up1, ROWS, within)  8.19 us
    unnamed x12, local copies, waits for them, and re-layouts  6.07 us
    ppermute x1, starting transfers between devices, on_device(): high0 = lax.ppermute(h0, ROWS, ring(groups, groups - 1))  5.74 us
    pallas_call x2, Pallas kernels, near(): call(functools.partial(near_kernel, size, h), (like((rows, width), BF16),...  4.91 us
    ppermute x1, starting transfers between devices, on_device(): high1 = lax.ppermute(down1, ROWS, [(b, a) for a, b in within])  4.2 us
  transfers between devices with their start and end apart: 15, of which 6 were waited for; matrix products, arithmetic and copies ran while one was open for 0% of the time, Pallas kernels for 8%

profile of v8, /device:TPU:10, one launch (start us, length us, event | category | flops | bytes accessed | tf_op | source)
XLA Modules:
  0.0 103.4 jit_solution(15807729067473283074)
XLA Ops:
  0.6 3.3 %shard_map.68 = (bf16[1024,256]{1,0:T(8,128)(2,1)}, bf16[1024,256]{1,0:T(8,128)(2,1)}, bf16[2,1024,256]{2,1,0:T(8,128)(2,1)}) custom-call(s32[4,8]{1,0:T(4,128)} %bitcast.6, bf16[1024,512]{1,0:T(8,128)(2,1)} %slab_hbm.1), custom_call_target="tpu_custom_call" | custom-call | tf_op jit(solution)/shard_map/pallas_call | solution.py:184
  3.9 0.1 collective-permute-start.1
  4.0 0.7 collective-permute-start
  4.7 2.2 %collective-permute-start.6 = (bf16[2,1024,256]{2,1,0:T(8,128)(2,1)}, bf16[2,1024,256]{2,1,0:T(8,128)(2,1)S(1)}, u32[]{:S(2)}, u32[]{:S(2)}) collective-permute-start(bf16[2,1024,256]{2,1,0:T(8,128)(2,1)} %get-tuple-element.28), channel_id=1, source_target_pairs={{0,128},{128,0},{1,129},{129,1},{2,130},{130,2},{3,131},{131,3},{4... | collective-permute-start | bytes 3145736 | tf_op jit(solution)/shard_map/ppermute | solution.py:202
  6.9 5.7 %collective-permute-start.5 = (bf16[1024,256]{1,0:T(8,128)(2,1)}, bf16[1024,256]{1,0:T(8,128)(2,1)S(1)}, u32[]{:S(2)}, u32[]{:S(2)}) collective-permute-start(bf16[1024,256]{1,0:T(8,128)(2,1)} %get-tuple-element.24.h0_ref.rest_0_), channel_id=1, source_target_pairs={{0,63},{1,0},{2,1},{3,2},{4,3},{5,4},{6,5},{7,6},{8,7},{9,8},{10,9... | collective-permute-start | bytes 1572872 | tf_op jit(solution)/shard_map/ppermute | solution.py:199
  12.7 1.0 copy-done
  13.8 0.1 collective-permute-start.2
  13.9 4.2 %collective-permute-start.3 = (bf16[1024,256]{1,0:T(8,128)(2,1)S(1)}, bf16[1024,256]{1,0:T(8,128)(2,1)S(1)}, u32[]{:S(2)}, u32[]{:S(2)}) collective-permute-start(bf16[1024,256]{1,0:T(8,128)(2,1)S(1)} %get-tuple-element.30), channel_id=1, source_target_pairs={{1,0},{2,1},{3,2},{4,3},{5,4},{6,5},{7,6},{8,7},{9,8},{10,9},{11,1... | collective-permute-start | bytes 1572872 | tf_op jit(solution)/shard_map/ppermute | solution.py:216
  18.1 1.0 %copy-done.1 = bf16[1024,256]{1,0:T(8,128)(2,1)S(1)} copy-done((bf16[1024,256]{1,0:T(8,128)(2,1)S(1)}, bf16[1024,256]{1,0:T(8,128)(2,1)}, u32[]{:S(2)}) %copy-start.1) | copy-done | bytes 524312
  19.1 1.0 %copy-done.2 = bf16[1024,256]{1,0:T(8,128)(2,1)S(1)} copy-done((bf16[1024,256]{1,0:T(8,128)(2,1)S(1)}, bf16[1024,256]{1,0:T(8,128)(2,1)}, u32[]{:S(2)}) %copy-start.2) | copy-done | bytes 524312
  20.2 2.3 %copy-done.3 = bf16[1024,2176]{1,0:T(8,128)(2,1)S(1)} copy-done((bf16[1024,2176]{1,0:T(8,128)(2,1)S(1)}, bf16[1024,2176]{1,0:T(8,128)(2,1)}, u32[]{:S(2)}) %copy-start.3) | copy-done | bytes 4456472
  22.4 0.7 copy-done.5
  23.1 2.8 %shard_map.69 = (bf16[1024,2176]{1,0:T(8,128)(2,1)S(1)}, f32[1024,256]{1,0:T(8,128)S(1)}, f32[1024,256]{1,0:T(8,128)S(1)}) custom-call(s32[8,17]{1,0:T(8,128)S(1)} %copy-done.5, bf16[1024,2176]{1,0:T(8,128)(2,1)S(1)} %copy-done.3, bf16[1024,256]{1,0:T(8,128)(2,1)S(1)} %copy-done.2, bf16[1024,256]{1,0:T(8,128)(2,1)S(1)} %copy-done.1), custom_call_target="tpu_custom_call" | custom-call | flops 1073741824 | bytes 8912896 | tf_op jit(solution)/shard_map/pallas_call | solution.py:204
  26.0 3.8 %collective-permute-done.4.low_ref = bf16[1024,256]{1,0:T(8,128)(2,1)S(1)} collective-permute-done((bf16[1024,256]{1,0:T(8,128)(2,1)}, bf16[1024,256]{1,0:T(8,128)(2,1)S(1)}, u32[]{:S(2)}, u32[]{:S(2)}) %collective-permute-start.4) | collective-permute-done | bytes 524320 | tf_op jit(solution)/shard_map/ppermute | solution.py:198
  29.8 2.0 %shard_map.72 = (bf16[1024,256]{1,0:T(8,128)(2,1)S(1)}, bf16[256,1024]{1,0:T(8,128)(2,1)S(1)}, bf16[4,256,256]{2,1,0:T(8,128)(2,1)S(1)}) custom-call(s32[4,8]{1,0:T(4,128)S(1)} %bitcast.4, bf16[1024,2176]{1,0:T(8,128)(2,1)S(1)} %get-tuple-element.26.held_ref, f32[1024,256]{1,0:T(8,128)S(1)} %get-tuple-element.31.mid_ref, ...), custom_call_target="tpu_custom_call" | custom-call | flops 1140850688 | bytes 4194304 | tf_op jit(solution)/shard_map/pallas_call | solution.py:220
  31.8 8.2 %collective-permute-done.2.low_ref = bf16[1024,256]{1,0:T(8,128)(2,1)S(1)} collective-permute-done((bf16[1024,256]{1,0:T(8,128)(2,1)S(1)}, bf16[1024,256]{1,0:T(8,128)(2,1)S(1)}, u32[]{:S(2)}, u32[]{:S(2)}) %collective-permute-start.2) | collective-permute-done | bytes 524320 | tf_op jit(solution)/shard_map/ppermute | solution.py:215
  40.0 2.9 %shard_map.73 = (bf16[1024,512]{1,0:T(8,128)(2,1)}, bf16[256,1024]{1,0:T(8,128)(2,1)S(1)}, bf16[4,256,256]{2,1,0:T(8,128)(2,1)S(1)}) custom-call(s32[4,8]{1,0:T(4,128)S(1)} %bitcast.5, bf16[1024,2176]{1,0:T(8,128)(2,1)S(1)} %get-tuple-element.26.held_ref, f32[1024,256]{1,0:T(8,128)S(1)} %get-tuple-element.27.mid_ref, ...), custom_call_target="tpu_custom_call" | custom-call | flops 1140850688 | bytes 4194304 | tf_op jit(solution)/shard_map/pallas_call | solution.py:220
  42.9 0.7 shard_map.75.far_ref
  43.6 1.9 %collective-permute-done.7.both_ref = bf16[2,1024,256]{2,1,0:T(8,128)(2,1)S(1)} collective-permute-done((bf16[2,1024,256]{2,1,0:T(8,128)(2,1)S(1)}, bf16[2,1024,256]{2,1,0:T(8,128)(2,1)S(1)}, u32[]{:S(2)}, u32[]{:S(2)}) %collective-permute-start.7) | collective-permute-done | bytes 1048608 | tf_op jit(solution)/shard_map/ppermute | solution.py:231
  45.6 0.9 shard_map.76
  46.4 1.7 %collective-permute-start.8 = (bf16[512,256]{1,0:T(8,128)(2,1)S(1)}, bf16[512,256]{1,0:T(8,128)(2,1)S(1)}, u32[]{:S(2)}, u32[]{:S(2)}) collective-permute-start(bf16[512,256]{1,0:T(8,128)(2,1)S(1)} %get-tuple-element.39), channel_id=1, source_target_pairs={{0,8},{8,16},{16,24},{24,0},{32,40},{40,48},{48,56},{56,32},{1,9},... | collective-permute-start | bytes 786440 | tf_op jit(solution)/shard_map/ppermute | solution.py:251
  48.1 8.7 %collective-permute-start.9 = (bf16[512,256]{1,0:T(8,128)(2,1)S(1)}, bf16[512,256]{1,0:T(8,128)(2,1)S(1)}, u32[]{:S(2)}, u32[]{:S(2)}) collective-permute-start(bf16[512,256]{1,0:T(8,128)(2,1)S(1)} %get-tuple-element.40), channel_id=1, source_target_pairs={{0,16},{8,24},{16,0},{24,8},{32,48},{40,56},{48,32},{56,40},{1,17}... | collective-permute-start | bytes 786440 | tf_op jit(solution)/shard_map/ppermute | solution.py:251
  56.8 0.5 collective-permute-start.11
  57.3 3.0 %collective-permute-start.12 = (bf16[512,256]{1,0:T(8,128)(2,1)S(1)}, bf16[512,256]{1,0:T(8,128)(2,1)S(1)}, u32[]{:S(2)}, u32[]{:S(2)}) collective-permute-start(bf16[512,256]{1,0:T(8,128)(2,1)S(1)} %get-tuple-element.43), channel_id=1, source_target_pairs={{0,40},{8,48},{16,56},{24,32},{32,8},{40,16},{48,24},{56,0},{1,41}... | collective-permute-start | bytes 786440 | tf_op jit(solution)/shard_map/ppermute | solution.py:251
  60.3 1.5 %collective-permute-done.8.refs_1_ = bf16[512,256]{1,0:T(8,128)(2,1)S(1)} collective-permute-done((bf16[512,256]{1,0:T(8,128)(2,1)S(1)}, bf16[512,256]{1,0:T(8,128)(2,1)S(1)}, u32[]{:S(2)}, u32[]{:S(2)}) %collective-permute-start.8) | collective-permute-done | bytes 262176 | tf_op jit(solution)/shard_map/ppermute | solution.py:251
  61.8 12.0 %collective-permute-start.13 = (bf16[512,256]{1,0:T(8,128)(2,1)S(1)}, bf16[512,256]{1,0:T(8,128)(2,1)S(1)}, u32[]{:S(2)}, u32[]{:S(2)}) collective-permute-start(bf16[512,256]{1,0:T(8,128)(2,1)S(1)} %get-tuple-element.44), channel_id=1, source_target_pairs={{0,48},{8,56},{16,32},{24,40},{32,16},{40,24},{48,0},{56,8},{1,49}... | collective-permute-start | bytes 786440 | tf_op jit(solution)/shard_map/ppermute | solution.py:251
  73.9 1.6 %collective-permute-start.14 = (bf16[512,256]{1,0:T(8,128)(2,1)S(1)}, bf16[512,256]{1,0:T(8,128)(2,1)S(1)}, u32[]{:S(2)}, u32[]{:S(2)}) collective-permute-start(bf16[512,256]{1,0:T(8,128)(2,1)S(1)} %get-tuple-element.45), channel_id=1, source_target_pairs={{0,56},{8,32},{16,40},{24,48},{32,24},{40,0},{48,8},{56,16},{1,57}... | collective-permute-start | bytes 786440 | tf_op jit(solution)/shard_map/ppermute | solution.py:251
  75.5 5.1 %collective-permute-done.13.refs_6_ = bf16[512,256]{1,0:T(8,128)(2,1)S(1)} collective-permute-done((bf16[512,256]{1,0:T(8,128)(2,1)S(1)}, bf16[512,256]{1,0:T(8,128)(2,1)S(1)}, u32[]{:S(2)}, u32[]{:S(2)}) %collective-permute-start.13) | collective-permute-done | bytes 262176 | tf_op jit(solution)/shard_map/ppermute | solution.py:251
  80.6 8.5 %collective-permute-done.14.refs_7_ = bf16[512,256]{1,0:T(8,128)(2,1)S(1)} collective-permute-done((bf16[512,256]{1,0:T(8,128)(2,1)S(1)}, bf16[512,256]{1,0:T(8,128)(2,1)S(1)}, u32[]{:S(2)}, u32[]{:S(2)}) %collective-permute-start.14) | collective-permute-done | bytes 262176 | tf_op jit(solution)/shard_map/ppermute | solution.py:251
  89.2 0.3 shard_map.77
  89.5 13.3 %all_to_all.5.in_ref = bf16[8,32,512]{2,1,0:T(8,128)(2,1)S(1)} all-to-all(bf16[8,32,512]{2,1,0:T(8,128)(2,1)S(1)} %bitcast.3), channel_id=1, replica_groups=mesh['xh'=2,'core'=2,'xl'=2,'y'=4,'z'=8] {'z'}, dimensions={0} | all-to-all | bytes 524288 | tf_op jit(solution)/shard_map/all_to_all | solution.py:254
  102.8 0.7 shard_map.78
  (22 shorter events, 0.1 us)
Async XLA Ops:
  3.9 25.9 %copy-start.4 = (s32[8,4]{0,1:T(4,128)S(1)}, s32[8,4]{0,1:T(4,128)}, u32[]{:S(2)}) copy-start(s32[8,4]{0,1:T(4,128)} %param.9) | copy-start | bytes 388
  3.9 8.8 %collective-permute-start.1 = (bf16[2,1024,256]{2,1,0:T(8,128)(2,1)}, bf16[2,1024,256]{2,1,0:T(8,128)(2,1)S(1)}, u32[]{:S(2)}, u32[]{:S(2)}) collective-permute-start(bf16[2,1024,256]{2,1,0:T(8,128)(2,1)} %get-tuple-element.28), channel_id=1, source_target_pairs={{0,64},{64,0},{1,65},{65,1},{2,66},{66,2},{3,67},{67,3},{4,68},{68... | collective-permute-start | bytes 3145736 | tf_op jit(solution)/shard_map/ppermute | solution.py:203
  4.0 8.7 %collective-permute-start = (bf16[1024,256]{1,0:T(8,128)(2,1)}, bf16[1024,256]{1,0:T(8,128)(2,1)S(1)}, u32[]{:S(2)}, u32[]{:S(2)}) collective-permute-start(bf16[1024,256]{1,0:T(8,128)(2,1)} %get-tuple-element.25.h1_ref.own_ref.rest_1_), channel_id=1, source_target_pairs={{0,32},{31,63},{32,0},{63,31},{64,96},{95,127},{96,64},{127,95},{1... | collective-permute-start | bytes 1572872 | tf_op jit(solution)/shard_map/ppermute | solution.py:201
  4.7 38.2 %collective-permute-start.6 = (bf16[2,1024,256]{2,1,0:T(8,128)(2,1)}, bf16[2,1024,256]{2,1,0:T(8,128)(2,1)S(1)}, u32[]{:S(2)}, u32[]{:S(2)}) collective-permute-start(bf16[2,1024,256]{2,1,0:T(8,128)(2,1)} %get-tuple-element.28), channel_id=1, source_target_pairs={{0,128},{128,0},{1,129},{129,1},{2,130},{130,2},{3,131},{131,3},{4... | collective-permute-start | bytes 3145736 | tf_op jit(solution)/shard_map/ppermute | solution.py:202
  6.9 19.0 %collective-permute-start.5 = (bf16[1024,256]{1,0:T(8,128)(2,1)}, bf16[1024,256]{1,0:T(8,128)(2,1)S(1)}, u32[]{:S(2)}, u32[]{:S(2)}) collective-permute-start(bf16[1024,256]{1,0:T(8,128)(2,1)} %get-tuple-element.24.h0_ref.rest_0_), channel_id=1, source_target_pairs={{0,63},{1,0},{2,1},{3,2},{4,3},{5,4},{6,5},{7,6},{8,7},{9,8},{10,9... | collective-permute-start | bytes 1572872 | tf_op jit(solution)/shard_map/ppermute | solution.py:199
  12.7 17.1 %collective-permute-start.4 = (bf16[1024,256]{1,0:T(8,128)(2,1)}, bf16[1024,256]{1,0:T(8,128)(2,1)S(1)}, u32[]{:S(2)}, u32[]{:S(2)}) collective-permute-start(bf16[1024,256]{1,0:T(8,128)(2,1)} %get-tuple-element.24.h0_ref.rest_0_), channel_id=1, source_target_pairs={{0,1},{1,2},{2,3},{3,4},{4,5},{5,6},{6,7},{7,8},{8,9},{9,10},{10,1... | collective-permute-start | bytes 1572872 | tf_op jit(solution)/shard_map/ppermute | solution.py:198
  12.7 1.0 %copy-start = (bf16[1024,256]{1,0:T(8,128)(2,1)S(1)}, bf16[1024,256]{1,0:T(8,128)(2,1)}, u32[]{:S(2)}) copy-start(bf16[1024,256]{1,0:T(8,128)(2,1)} %get-tuple-element.25.h1_ref.own_ref.rest_1_) | copy-start | bytes 1572868
  13.8 26.2 %collective-permute-start.2 = (bf16[1024,256]{1,0:T(8,128)(2,1)S(1)}, bf16[1024,256]{1,0:T(8,128)(2,1)S(1)}, u32[]{:S(2)}, u32[]{:S(2)}) collective-permute-start(bf16[1024,256]{1,0:T(8,128)(2,1)S(1)} %get-tuple-element.29), channel_id=1, source_target_pairs={{0,1},{1,2},{2,3},{3,4},{4,5},{5,6},{6,7},{7,8},{8,9},{9,10},{10,1... | collective-permute-start | bytes 1572872 | tf_op jit(solution)/shard_map/ppermute | solution.py:215
  13.9 26.1 %collective-permute-start.3 = (bf16[1024,256]{1,0:T(8,128)(2,1)S(1)}, bf16[1024,256]{1,0:T(8,128)(2,1)S(1)}, u32[]{:S(2)}, u32[]{:S(2)}) collective-permute-start(bf16[1024,256]{1,0:T(8,128)(2,1)S(1)} %get-tuple-element.30), channel_id=1, source_target_pairs={{1,0},{2,1},{3,2},{4,3},{5,4},{6,5},{7,6},{8,7},{9,8},{10,9},{11,1... | collective-permute-start | bytes 1572872 | tf_op jit(solution)/shard_map/ppermute | solution.py:216
  18.1 1.0 %copy-start.1 = (bf16[1024,256]{1,0:T(8,128)(2,1)S(1)}, bf16[1024,256]{1,0:T(8,128)(2,1)}, u32[]{:S(2)}) copy-start(bf16[1024,256]{1,0:T(8,128)(2,1)} %get-tuple-element.25.h1_ref.own_ref.rest_1_) | copy-start | bytes 1572868
  19.1 1.0 %copy-start.2 = (bf16[1024,256]{1,0:T(8,128)(2,1)S(1)}, bf16[1024,256]{1,0:T(8,128)(2,1)}, u32[]{:S(2)}) copy-start(bf16[1024,256]{1,0:T(8,128)(2,1)} %get-tuple-element.24.h0_ref.rest_0_) | copy-start | bytes 1572868
  20.2 2.3 %copy-start.3 = (bf16[1024,2176]{1,0:T(8,128)(2,1)S(1)}, bf16[1024,2176]{1,0:T(8,128)(2,1)}, u32[]{:S(2)}) copy-start(bf16[1024,2176]{1,0:T(8,128)(2,1)} %fock_ref.1) | copy-start | bytes 13369348
  22.4 0.7 copy-start.5
  42.9 2.7 %collective-permute-start.7 = (bf16[2,1024,256]{2,1,0:T(8,128)(2,1)S(1)}, bf16[2,1024,256]{2,1,0:T(8,128)(2,1)S(1)}, u32[]{:S(2)}, u32[]{:S(2)}) collective-permute-start(bf16[2,1024,256]{2,1,0:T(8,128)(2,1)S(1)} %shard_map.74.far_ref), channel_id=1, source_target_pairs={{0,64},{64,0},{1,65},{65,1},{2,66},{66,2},{3,67},{67,3},{4,68},{68... | collective-permute-start | bytes 3145736 | tf_op jit(solution)/shard_map/ppermute | solution.py:231
  46.4 15.4 %collective-permute-start.8 = (bf16[512,256]{1,0:T(8,128)(2,1)S(1)}, bf16[512,256]{1,0:T(8,128)(2,1)S(1)}, u32[]{:S(2)}, u32[]{:S(2)}) collective-permute-start(bf16[512,256]{1,0:T(8,128)(2,1)S(1)} %get-tuple-element.39), channel_id=1, source_target_pairs={{0,8},{8,16},{16,24},{24,0},{32,40},{40,48},{48,56},{56,32},{1,9},... | collective-permute-start | bytes 786440 | tf_op jit(solution)/shard_map/ppermute | solution.py:251
  48.1 25.8 %collective-permute-start.9 = (bf16[512,256]{1,0:T(8,128)(2,1)S(1)}, bf16[512,256]{1,0:T(8,128)(2,1)S(1)}, u32[]{:S(2)}, u32[]{:S(2)}) collective-permute-start(bf16[512,256]{1,0:T(8,128)(2,1)S(1)} %get-tuple-element.40), channel_id=1, source_target_pairs={{0,16},{8,24},{16,0},{24,8},{32,48},{40,56},{48,32},{56,40},{1,17}... | collective-permute-start | bytes 786440 | tf_op jit(solution)/shard_map/ppermute | solution.py:251
  56.8 18.7 %collective-permute-start.10 = (bf16[512,256]{1,0:T(8,128)(2,1)S(1)}, bf16[512,256]{1,0:T(8,128)(2,1)S(1)}, u32[]{:S(2)}, u32[]{:S(2)}) collective-permute-start(bf16[512,256]{1,0:T(8,128)(2,1)S(1)} %get-tuple-element.41), channel_id=1, source_target_pairs={{0,24},{8,0},{16,8},{24,16},{32,56},{40,32},{48,40},{56,48},{1,25}... | collective-permute-start | bytes 786440 | tf_op jit(solution)/shard_map/ppermute | solution.py:251
  56.8 18.7 %collective-permute-start.11 = (bf16[512,256]{1,0:T(8,128)(2,1)S(1)}, bf16[512,256]{1,0:T(8,128)(2,1)S(1)}, u32[]{:S(2)}, u32[]{:S(2)}) collective-permute-start(bf16[512,256]{1,0:T(8,128)(2,1)S(1)} %get-tuple-element.42), channel_id=1, source_target_pairs={{0,32},{8,40},{16,48},{24,56},{32,0},{40,8},{48,16},{56,24},{1,33}... | collective-permute-start | bytes 786440 | tf_op jit(solution)/shard_map/ppermute | solution.py:251
  57.3 18.2 %collective-permute-start.12 = (bf16[512,256]{1,0:T(8,128)(2,1)S(1)}, bf16[512,256]{1,0:T(8,128)(2,1)S(1)}, u32[]{:S(2)}, u32[]{:S(2)}) collective-permute-start(bf16[512,256]{1,0:T(8,128)(2,1)S(1)} %get-tuple-element.43), channel_id=1, source_target_pairs={{0,40},{8,48},{16,56},{24,32},{32,8},{40,16},{48,24},{56,0},{1,41}... | collective-permute-start | bytes 786440 | tf_op jit(solution)/shard_map/ppermute | solution.py:251
  61.8 18.8 %collective-permute-start.13 = (bf16[512,256]{1,0:T(8,128)(2,1)S(1)}, bf16[512,256]{1,0:T(8,128)(2,1)S(1)}, u32[]{:S(2)}, u32[]{:S(2)}) collective-permute-start(bf16[512,256]{1,0:T(8,128)(2,1)S(1)} %get-tuple-element.44), channel_id=1, source_target_pairs={{0,48},{8,56},{16,32},{24,40},{32,16},{40,24},{48,0},{56,8},{1,49}... | collective-permute-start | bytes 786440 | tf_op jit(solution)/shard_map/ppermute | solution.py:251
  73.9 15.3 %collective-permute-start.14 = (bf16[512,256]{1,0:T(8,128)(2,1)S(1)}, bf16[512,256]{1,0:T(8,128)(2,1)S(1)}, u32[]{:S(2)}, u32[]{:S(2)}) collective-permute-start(bf16[512,256]{1,0:T(8,128)(2,1)S(1)} %get-tuple-element.45), channel_id=1, source_target_pairs={{0,56},{8,32},{16,40},{24,48},{32,24},{40,0},{48,8},{56,16},{1,57}... | collective-permute-start | bytes 786440 | tf_op jit(solution)/shard_map/ppermute | solution.py:251

commit v9 on v4

--- a/solution.py
+++ b/solution.py
@@ -87,11 +87,12 @@
     own_refs, near_ref, rest = rest[:2], rest[2], rest[3:]
     start = 0
     if h == 1:
-        first_ref, rest = rest[0], rest[1:]
+        first_ref, earlier_ref, rest = rest[0], rest[1], rest[2:]
         start = first_ref.shape[1]
     out_ref, outt_ref, terms_ref = rest
     if h == 1:
         out_ref[:, :start] = first_ref[...]
+        terms_ref[:, :start, :] = earlier_ref[...]
     blocks = rmask_ref.shape[1]
     slots = held_ref.shape[1] // size
     panels = mid_ref.shape[1] // size
@@ -107,10 +108,10 @@
             tile = jnp.where(keep, tile, jnp.zeros_like(tile)).astype(BF16)
             out_ref[rows, pl.ds(start + j * size, size)] = tile
             outt_ref[cols, rows] = tile.T
-    core = lax.axis_index("core")
+    core, deep = lax.axis_index("core"), pl.ds(start, outt_ref.shape[0])
     for k in range(2):
-        terms_ref[core * 2 + k] = dot(outt_ref[...], own_refs[k][...]).astype(BF16)
-        terms_ref[(1 - core) * 2 + k] = dot(outt_ref[...], near_ref[k]).astype(BF16)
+        terms_ref[core * 2 + k, deep, :] = dot(outt_ref[...], own_refs[k][...]).astype(BF16)
+        terms_ref[(1 - core) * 2 + k, deep, :] = dot(outt_ref[...], near_ref[k]).astype(BF16)
 
 
 def far_kernel(t0_ref, t1_ref, far_ref, terms_ref):
@@ -120,24 +121,26 @@
             terms_ref[c, pl.ds(k * half, half), :] = dot(t[...], far_ref[c]).astype(BF16)
 
 
-def gather_kernel(t0_ref, t1_ref, both_ref, near0_ref, near1_ref, far_ref, out_ref):
+def gather_kernel(t0_ref, t1_ref, both_ref, far_ref, out_ref):
     half = t0_ref.shape[0]
-    core, xh = lax.axis_index("core"), lax.axis_index("xh")
-    other = (1 - xh) * 4
+    core = lax.axis_index("core")
     for c in range(2):
-        out_ref[other + core * 2 + c] = far_ref[c]
+        out_ref[core * 2 + c] = far_ref[c]
         for k, t in enumerate((t0_ref, t1_ref)):
-            out_ref[other + (1 - core) * 2 + c, pl.ds(k * half, half), :] = dot(t[...], both_ref[c]).astype(BF16)
-    for s in range(4):
-        for k, ref in enumerate((near0_ref, near1_ref)):
-            out_ref[xh * 4 + s, pl.ds(k * half, half), :] = ref[s]
-
-
-def first_sum_kernel(in_ref, out_ref):
-    total = in_ref[0].astype(F32)
-    for s in range(1, in_ref.shape[0]):
-        total += in_ref[s].astype(F32)
-    out_ref[...] = total.T.astype(BF16)
+            out_ref[(1 - core) * 2 + c, pl.ds(k * half, half), :] = dot(t[...], both_ref[c]).astype(BF16)
+
+
+def first_sum_kernel(near_ref, far_ref, out_ref):
+    count, deep, _ = out_ref.shape
+    inner = count // 2
+    xh = lax.axis_index("xh")
+    for f, ref in enumerate((near_ref, far_ref)):
+        total = ref[0].astype(F32)
+        for s in range(1, ref.shape[0]):
+            total += ref[s].astype(F32)
+        turned = total.T.astype(BF16)
+        for z in range(inner):
+            out_ref[(xh ^ f) * inner + z] = turned[z * deep : (z + 1) * deep]
 
 
 def last_sum_kernel(factor, in_ref, out_ref):
@@ -210,14 +213,15 @@
         width = half if h == 0 else columns
         return call(
             functools.partial(near_kernel, size, h),
-            (like((rows, width), BF16), like((half, rows), BF16), like((4, half, half), BF16)),
+            (like((rows, width), BF16), like((half, rows), BF16), like((wide, width, half), BF16)),
             [SMEM] + [VMEM] * (7 + len(first)),
             flops=2 * rows * half * (2 * columns + (slots - blocks) * size),
             moved=8 * rows * columns,
         )(result_mask.T, held, mid, low, high, h0, h1, near_panels, *first)
 
     product0, flipped0, terms0 = near(0, mid0, low0, high0)
-    product, flipped1, terms1 = near(1, mid1, low1, high1, product0)
+    product, flipped1, terms1 = near(1, mid1, low1, high1, product0, terms0)
+    near_got = lax.all_to_all(terms1, "y", 0, 0, tiled=True)
     far = after(far, terms1)
     both = lax.ppermute(far, "core", swap)
     far_terms = call(
@@ -229,15 +233,14 @@
     )(flipped0, flipped1, far)
     terms = call(
         gather_kernel,
-        like((groups // deep, columns, half), BF16),
-        [VMEM] * 6,
+        like((wide, columns, half), BF16),
+        [VMEM] * 4,
         flops=4 * rows * half * columns,
         moved=8 * rows * columns,
-    )(flipped0, flipped1, both, terms0, terms1, far_terms)
-    terms = lax.all_to_all(terms, ("xl", "y"), 0, 0, tiled=True)
-    part = call(first_sum_kernel, like((half, columns), BF16), [VMEM])(terms)
-    part = part.reshape(deep, half // deep, columns)
-    part = lax.all_to_all(part, "z", 0, 0, tiled=True)
+    )(flipped0, flipped1, both, far_terms)
+    far_got = lax.all_to_all(terms, "y", 0, 0, tiled=True)
+    part = call(first_sum_kernel, like((2 * deep, half // deep, columns), BF16), [VMEM] * 2)(near_got, far_got)
+    part = lax.all_to_all(part, ("xl", "z"), 0, 0, tiled=True)
     factor = 1.0 / math.sqrt(rows * groups)
     projected = call(
         functools.partial(last_sum_kernel, factor), like((half // deep, columns), F32), [VMEM]

time: 98.3 us -> 107 us (1.089)
  the two profiles are of different devices: /device:TPU:10 before, /device:TPU:34 now
where the time goes in v9:
time: 107 us; the launch traced here: 106 us
  blocking collectives  40.5 us (38%)
  waiting for transfers between devices  22.7 us (21%)
  starting transfers between devices  21 us (20%)
  Pallas kernels  15.1 us (14%)
  local copies, waits for them, and re-layouts  6.07 us (6%)
    all_to_all x1, blocking collectives, on_device(): part = lax.all_to_all(part, ('xl', 'z'), 0, 0, tiled=True)  22.9 us
    all_to_all x1, blocking collectives, on_device(): far_got = lax.all_to_all(terms, 'y', 0, 0, tiled=True)  17.7 us
    all_to_all x1, waiting for transfers between devices, on_device(): near_got = lax.all_to_all(terms1, 'y', 0, 0, tiled=True)  13.3 us
    ppermute x1, starting transfers between devices, on_device(): high1 = lax.ppermute(down1, ROWS, [(b, a) for a, b in within])  10.5 us
    ppermute x1, waiting for transfers between devices, on_device(): low1 = lax.ppermute(up1, ROWS, within)  8.17 us
    unnamed x12, local copies, waits for them, and re-layouts  6.07 us
    pallas_call x2, Pallas kernels, near(): call(functools.partial(near_kernel, size, h), (like((rows, width), BF16),...  5.3 us
    all_to_all x1, starting transfers between devices, on_device(): near_got = lax.all_to_all(terms1, 'y', 0, 0, tiled=True)  3.53 us
  transfers between devices with their start and end apart: 9, of which 3 were waited for; matrix products, arithmetic and copies ran while one was open for 0% of the time, Pallas kernels for 10%

profile of v9, /device:TPU:34, one launch (start us, length us, event | category | flops | bytes accessed | tf_op | source)
XLA Modules:
  0.0 106.2 jit_solution(13430416116000238382)
XLA Ops:
  0.6 3.2 %shard_map.68 = (bf16[1024,256]{1,0:T(8,128)(2,1)}, bf16[1024,256]{1,0:T(8,128)(2,1)}, bf16[2,1024,256]{2,1,0:T(8,128)(2,1)}) custom-call(s32[4,8]{1,0:T(4,128)} %bitcast.4, bf16[1024,512]{1,0:T(8,128)(2,1)} %slab_hbm.1), custom_call_target="tpu_custom_call" | custom-call | tf_op jit(solution)/shard_map/pallas_call | solution.py:178
  3.9 0.0 copy-start.4
  3.9 0.1 collective-permute-start.1
  4.0 0.7 collective-permute-start
  4.7 2.2 %collective-permute-start.6 = (bf16[2,1024,256]{2,1,0:T(8,128)(2,1)}, bf16[2,1024,256]{2,1,0:T(8,128)(2,1)S(1)}, u32[]{:S(2)}, u32[]{:S(2)}) collective-permute-start(bf16[2,1024,256]{2,1,0:T(8,128)(2,1)} %get-tuple-element.20), channel_id=1, source_target_pairs={{0,128},{128,0},{1,129},{129,1},{2,130},{130,2},{3,131},{131,3},{4... | collective-permute-start | bytes 3145736 | tf_op jit(solution)/shard_map/ppermute | solution.py:196
  6.9 2.2 %collective-permute-start.5 = (bf16[1024,256]{1,0:T(8,128)(2,1)}, bf16[1024,256]{1,0:T(8,128)(2,1)S(1)}, u32[]{:S(2)}, u32[]{:S(2)}) collective-permute-start(bf16[1024,256]{1,0:T(8,128)(2,1)} %get-tuple-element.16.h0_ref.rest_0_), channel_id=1, source_target_pairs={{0,63},{1,0},{2,1},{3,2},{4,3},{5,4},{6,5},{7,6},{8,7},{9,8},{10,9... | collective-permute-start | bytes 1572872 | tf_op jit(solution)/shard_map/ppermute | solution.py:193
  9.1 0.0 collective-permute-start.4
  9.1 0.0 collective-permute-done.refs_0_
  9.1 1.0 copy-done
  10.1 0.1 shard_map.71
  10.2 1.9 %collective-permute-start.2 = (bf16[1024,256]{1,0:T(8,128)(2,1)S(1)}, bf16[1024,256]{1,0:T(8,128)(2,1)S(1)}, u32[]{:S(2)}, u32[]{:S(2)}) collective-permute-start(bf16[1024,256]{1,0:T(8,128)(2,1)S(1)} %get-tuple-element.21), channel_id=1, source_target_pairs={{0,1},{1,2},{2,3},{3,4},{4,5},{5,6},{6,7},{7,8},{8,9},{9,10},{10,1... | collective-permute-start | bytes 1572872 | tf_op jit(solution)/shard_map/ppermute | solution.py:209
  12.1 10.5 %collective-permute-start.3 = (bf16[1024,256]{1,0:T(8,128)(2,1)S(1)}, bf16[1024,256]{1,0:T(8,128)(2,1)S(1)}, u32[]{:S(2)}, u32[]{:S(2)}) collective-permute-start(bf16[1024,256]{1,0:T(8,128)(2,1)S(1)} %get-tuple-element.22), channel_id=1, source_target_pairs={{1,0},{2,1},{3,2},{4,3},{5,4},{6,5},{7,6},{8,7},{9,8},{10,9},{11,1... | collective-permute-start | bytes 1572872 | tf_op jit(solution)/shard_map/ppermute | solution.py:210
  22.6 1.0 copy-done.1
  23.6 1.0 copy-done.2
  24.6 2.3 %copy-done.3 = bf16[1024,2176]{1,0:T(8,128)(2,1)S(1)} copy-done((bf16[1024,2176]{1,0:T(8,128)(2,1)S(1)}, bf16[1024,2176]{1,0:T(8,128)(2,1)}, u32[]{:S(2)}) %copy-start.3) | copy-done | bytes 4456472
  26.9 0.7 copy-done.5
  27.6 2.8 %shard_map.69 = (bf16[1024,2176]{1,0:T(8,128)(2,1)S(1)}, f32[1024,256]{1,0:T(8,128)S(1)}, f32[1024,256]{1,0:T(8,128)S(1)}) custom-call(s32[8,17]{1,0:T(8,128)S(1)} %copy-done.5, bf16[1024,2176]{1,0:T(8,128)(2,1)S(1)} %copy-done.3, bf16[1024,256]{1,0:T(8,128)(2,1)S(1)} %copy-done.2, bf16[1024,256]{1,0:T(8,128)(2,1)S(1)} %copy-done.1), custom_call_target="tpu_custom_call" | custom-call | flops 1073741824 | bytes 8912896 | tf_op jit(solution)/shard_map/pallas_call | solution.py:198
  30.4 0.0 collective-permute-done.5.high_ref
  30.4 1.2 %collective-permute-done.4.low_ref = bf16[1024,256]{1,0:T(8,128)(2,1)S(1)} collective-permute-done((bf16[1024,256]{1,0:T(8,128)(2,1)}, bf16[1024,256]{1,0:T(8,128)(2,1)S(1)}, u32[]{:S(2)}, u32[]{:S(2)}) %collective-permute-start.4) | collective-permute-done | bytes 524320 | tf_op jit(solution)/shard_map/ppermute | solution.py:192
  31.6 2.0 %shard_map.72 = (bf16[1024,256]{1,0:T(8,128)(2,1)S(1)}, bf16[256,1024]{1,0:T(8,128)(2,1)S(1)}, bf16[4,256,256]{2,1,0:T(8,128)(2,1)S(1)}) custom-call(s32[4,8]{1,0:T(4,128)S(1)} %bitcast.2, bf16[1024,2176]{1,0:T(8,128)(2,1)S(1)} %get-tuple-element.18.held_ref, f32[1024,256]{1,0:T(8,128)S(1)} %get-tuple-element.23.mid_ref, ...), custom_call_target="tpu_custom_call" | custom-call | flops 1140850688 | bytes 4194304 | tf_op jit(solution)/shard_map/pallas_call | solution.py:214
  33.6 8.2 %collective-permute-done.2.low_ref = bf16[1024,256]{1,0:T(8,128)(2,1)S(1)} collective-permute-done((bf16[1024,256]{1,0:T(8,128)(2,1)S(1)}, bf16[1024,256]{1,0:T(8,128)(2,1)S(1)}, u32[]{:S(2)}, u32[]{:S(2)}) %collective-permute-start.2) | collective-permute-done | bytes 524320 | tf_op jit(solution)/shard_map/ppermute | solution.py:209
  41.8 3.3 %shard_map.73 = (bf16[1024,512]{1,0:T(8,128)(2,1)}, bf16[256,1024]{1,0:T(8,128)(2,1)S(1)}, bf16[4,512,256]{2,1,0:T(8,128)(2,1)}) custom-call(s32[4,8]{1,0:T(4,128)S(1)} %bitcast.3, bf16[1024,2176]{1,0:T(8,128)(2,1)S(1)} %get-tuple-element.18.held_ref, f32[1024,256]{1,0:T(8,128)S(1)} %get-tuple-element.19.mid_ref, ...), custom_call_target="tpu_custom_call" | custom-call | flops 1140850688 | bytes 4194304 | tf_op jit(solution)/shard_map/pallas_call | solution.py:214
  45.1 0.0 collective-permute-done.6.refs_0_
  45.1 3.5 %all-to-all-start = ((bf16[4,512,256]{2,1,0:T(8,128)(2,1)}), bf16[4,512,256]{2,1,0:T(8,128)(2,1)S(1)}, u32[]{:S(2)}, u32[]{:S(2)}) async-start(bf16[4,512,256]{2,1,0:T(8,128)(2,1)} %get-tuple-element.27.refs_1_), calls=%async_computation | async-start | bytes 2097152 | tf_op jit(solution)/shard_map/all_to_all | solution.py:224
  48.7 0.7 shard_map.75.far_ref
  49.4 0.0 collective-permute-done.7.both_ref
  49.4 1.9 %shard_map.76 = bf16[4,512,256]{2,1,0:T(8,128)(2,1)S(1)} custom-call(bf16[256,1024]{1,0:T(8,128)(2,1)S(1)} %get-tuple-element.28.t0_ref, bf16[256,1024]{1,0:T(8,128)(2,1)S(1)} %get-tuple-element.29.t1_ref, bf16[2,1024,256]{2,1,0:T(8,128)(2,1)} %collective-permute-done.7.both_ref, bf16[2,512,256]{2,1,0:T(8,128)(2,1)S(1)} %shard_map.75.far_ref), custom_call_target="tpu_custom_call" | custom-call | flops 536870912 | bytes 4194304 | tf_op jit(solution)/shard_map/pallas_call | solution.py:234
  51.3 13.3 %all-to-all-done.near_ref = bf16[4,512,256]{2,1,0:T(8,128)(2,1)S(1)} async-done(((bf16[4,512,256]{2,1,0:T(8,128)(2,1)}), bf16[4,512,256]{2,1,0:T(8,128)(2,1)S(1)}, u32[]{:S(2)}, u32[]{:S(2)}) %all-to-all-start) | async-done | bytes 1048608 | tf_op jit(solution)/shard_map/all_to_all | solution.py:224
  64.7 17.7 %all_to_all.15.far_ref = bf16[4,512,256]{2,1,0:T(8,128)(2,1)S(1)} all-to-all(bf16[4,512,256]{2,1,0:T(8,128)(2,1)S(1)} %shard_map.76), channel_id=1, replica_groups=mesh['xh'=2,'core'=2,'xl'=2,'y'=4,'z'=8] {'y'}, dimensions={0} | all-to-all | bytes 2097152 | tf_op jit(solution)/shard_map/all_to_all | solution.py:241
  82.3 0.4 shard_map.77
  82.7 22.9 %all_to_all.16.in_ref = bf16[16,32,512]{2,1,0:T(8,128)(2,1)S(1)} all-to-all(bf16[16,32,512]{2,1,0:T(8,128)(2,1)S(1)} %shard_map.77), channel_id=1, replica_groups=mesh['xh'=2,'core'=2,'xl'=2,'y'=4,'z'=8] {'xl','z'}, dimensions={0} | all-to-all | bytes 1048576 | tf_op jit(solution)/shard_map/all_to_all | solution.py:243
  105.5 0.7 shard_map.78
  (11 shorter events, 0.0 us)
Async XLA Ops:
  3.9 27.7 %copy-start.4 = (s32[8,4]{0,1:T(4,128)S(1)}, s32[8,4]{0,1:T(4,128)}, u32[]{:S(2)}) copy-start(s32[8,4]{0,1:T(4,128)} %param.9) | copy-start | bytes 388
  3.9 5.2 %collective-permute-start.1 = (bf16[2,1024,256]{2,1,0:T(8,128)(2,1)}, bf16[2,1024,256]{2,1,0:T(8,128)(2,1)S(1)}, u32[]{:S(2)}, u32[]{:S(2)}) collective-permute-start(bf16[2,1024,256]{2,1,0:T(8,128)(2,1)} %get-tuple-element.20), channel_id=1, source_target_pairs={{0,64},{64,0},{1,65},{65,1},{2,66},{66,2},{3,67},{67,3},{4,68},{68... | collective-permute-start | bytes 3145736 | tf_op jit(solution)/shard_map/ppermute | solution.py:197
  4.0 5.1 %collective-permute-start = (bf16[1024,256]{1,0:T(8,128)(2,1)}, bf16[1024,256]{1,0:T(8,128)(2,1)S(1)}, u32[]{:S(2)}, u32[]{:S(2)}) collective-permute-start(bf16[1024,256]{1,0:T(8,128)(2,1)} %get-tuple-element.17.h1_ref.own_ref.rest_1_), channel_id=1, source_target_pairs={{0,32},{31,63},{32,0},{63,31},{64,96},{95,127},{96,64},{127,95},{1... | collective-permute-start | bytes 1572872 | tf_op jit(solution)/shard_map/ppermute | solution.py:195
  4.7 40.4 %collective-permute-start.6 = (bf16[2,1024,256]{2,1,0:T(8,128)(2,1)}, bf16[2,1024,256]{2,1,0:T(8,128)(2,1)S(1)}, u32[]{:S(2)}, u32[]{:S(2)}) collective-permute-start(bf16[2,1024,256]{2,1,0:T(8,128)(2,1)} %get-tuple-element.20), channel_id=1, source_target_pairs={{0,128},{128,0},{1,129},{129,1},{2,130},{130,2},{3,131},{131,3},{4... | collective-permute-start | bytes 3145736 | tf_op jit(solution)/shard_map/ppermute | solution.py:196
  6.9 23.5 %collective-permute-start.5 = (bf16[1024,256]{1,0:T(8,128)(2,1)}, bf16[1024,256]{1,0:T(8,128)(2,1)S(1)}, u32[]{:S(2)}, u32[]{:S(2)}) collective-permute-start(bf16[1024,256]{1,0:T(8,128)(2,1)} %get-tuple-element.16.h0_ref.rest_0_), channel_id=1, source_target_pairs={{0,63},{1,0},{2,1},{3,2},{4,3},{5,4},{6,5},{7,6},{8,7},{9,8},{10,9... | collective-permute-start | bytes 1572872 | tf_op jit(solution)/shard_map/ppermute | solution.py:193
  9.1 22.6 %collective-permute-start.4 = (bf16[1024,256]{1,0:T(8,128)(2,1)}, bf16[1024,256]{1,0:T(8,128)(2,1)S(1)}, u32[]{:S(2)}, u32[]{:S(2)}) collective-permute-start(bf16[1024,256]{1,0:T(8,128)(2,1)} %get-tuple-element.16.h0_ref.rest_0_), channel_id=1, source_target_pairs={{0,1},{1,2},{2,3},{3,4},{4,5},{5,6},{6,7},{7,8},{8,9},{9,10},{10,1... | collective-permute-start | bytes 1572872 | tf_op jit(solution)/shard_map/ppermute | solution.py:192
  9.1 1.0 copy-start
  10.2 31.6 %collective-permute-start.2 = (bf16[1024,256]{1,0:T(8,128)(2,1)S(1)}, bf16[1024,256]{1,0:T(8,128)(2,1)S(1)}, u32[]{:S(2)}, u32[]{:S(2)}) collective-permute-start(bf16[1024,256]{1,0:T(8,128)(2,1)S(1)} %get-tuple-element.21), channel_id=1, source_target_pairs={{0,1},{1,2},{2,3},{3,4},{4,5},{5,6},{6,7},{7,8},{8,9},{9,10},{10,1... | collective-permute-start | bytes 1572872 | tf_op jit(solution)/shard_map/ppermute | solution.py:209
  12.1 29.8 %collective-permute-start.3 = (bf16[1024,256]{1,0:T(8,128)(2,1)S(1)}, bf16[1024,256]{1,0:T(8,128)(2,1)S(1)}, u32[]{:S(2)}, u32[]{:S(2)}) collective-permute-start(bf16[1024,256]{1,0:T(8,128)(2,1)S(1)} %get-tuple-element.22), channel_id=1, source_target_pairs={{1,0},{2,1},{3,2},{4,3},{5,4},{6,5},{7,6},{8,7},{9,8},{10,9},{11,1... | collective-permute-start | bytes 1572872 | tf_op jit(solution)/shard_map/ppermute | solution.py:210
  22.6 1.0 copy-start.1
  23.6 1.0 copy-start.2
  24.6 2.3 %copy-start.3 = (bf16[1024,2176]{1,0:T(8,128)(2,1)S(1)}, bf16[1024,2176]{1,0:T(8,128)(2,1)}, u32[]{:S(2)}) copy-start(bf16[1024,2176]{1,0:T(8,128)(2,1)} %fock_ref.1) | copy-start | bytes 13369348
  26.9 0.7 copy-start.5
  45.1 4.3 %collective-permute-start.7 = (bf16[2,1024,256]{2,1,0:T(8,128)(2,1)S(1)}, bf16[2,1024,256]{2,1,0:T(8,128)(2,1)}, u32[]{:S(2)}, u32[]{:S(2)}) collective-permute-start(bf16[2,1024,256]{2,1,0:T(8,128)(2,1)S(1)} %shard_map.74.far_ref), channel_id=1, source_target_pairs={{0,64},{64,0},{1,65},{65,1},{2,66},{66,2},{3,67},{67,3},{4,68},{68... | collective-permute-start | bytes 3145736 | tf_op jit(solution)/shard_map/ppermute | solution.py:226
  45.1 19.5 %all-to-all-start = ((bf16[4,512,256]{2,1,0:T(8,128)(2,1)}), bf16[4,512,256]{2,1,0:T(8,128)(2,1)S(1)}, u32[]{:S(2)}, u32[]{:S(2)}) async-start(bf16[4,512,256]{2,1,0:T(8,128)(2,1)} %get-tuple-element.27.refs_1_), calls=%async_computation | async-start | bytes 2097152 | tf_op jit(solution)/shard_map/all_to_all | solution.py:224

commit v10 on v4

--- a/solution.py
+++ b/solution.py
@@ -117,7 +117,7 @@
     half = t0_ref.shape[0]
     for c in range(2):
         for k, t in enumerate((t0_ref, t1_ref)):
-            terms_ref[c, pl.ds(k * half, half), :] = dot(t[...], far_ref[c]).astype(BF16)
+            terms_ref[c, :, pl.ds(k * half, half)] = dot(t[...], far_ref[c]).astype(BF16)
 
 
 def gather_kernel(t0_ref, t1_ref, both_ref, near0_ref, near1_ref, far_ref, out_ref):
@@ -127,17 +127,19 @@
     for c in range(2):
         out_ref[other + core * 2 + c] = far_ref[c]
         for k, t in enumerate((t0_ref, t1_ref)):
-            out_ref[other + (1 - core) * 2 + c, pl.ds(k * half, half), :] = dot(t[...], both_ref[c]).astype(BF16)
+            out_ref[other + (1 - core) * 2 + c, :, pl.ds(k * half, half)] = dot(t[...], both_ref[c]).astype(BF16)
     for s in range(4):
         for k, ref in enumerate((near0_ref, near1_ref)):
-            out_ref[xh * 4 + s, pl.ds(k * half, half), :] = ref[s]
+            out_ref[xh * 4 + s, :, pl.ds(k * half, half)] = ref[s]
 
 
 def first_sum_kernel(in_ref, out_ref):
     total = in_ref[0].astype(F32)
     for s in range(1, in_ref.shape[0]):
         total += in_ref[s].astype(F32)
-    out_ref[...] = total.T.astype(BF16)
+    half = total.shape[0]
+    for k in range(2):
+        out_ref[:, pl.ds(k * half, half)] = total[:, k * half : (k + 1) * half].T.astype(BF16)
 
 
 def last_sum_kernel(factor, in_ref, out_ref):
@@ -222,14 +224,14 @@
     both = lax.ppermute(far, "core", swap)
     far_terms = call(
         far_kernel,
-        like((2, columns, half), BF16),
+        like((2, half, columns), BF16),
         [VMEM] * 3,
         flops=4 * rows * half * columns,
         moved=8 * rows * half,
     )(flipped0, flipped1, far)
     terms = call(
         gather_kernel,
-        like((groups // deep, columns, half), BF16),
+        like((groups // deep, half, columns), BF16),
         [VMEM] * 6,
         flops=4 * rows * half * columns,
         moved=8 * rows * columns,

time: 98.3 us -> 98.3 us (level)
  no operation moved by 1% of the time
where the time goes in v10:
time: 98.3 us; the launch traced here: 97.9 us
  blocking collectives  50.6 us (51%)
  waiting for transfers between devices  14 us (14%)
  Pallas kernels  13.5 us (14%)
  starting transfers between devices  13 us (13%)
  local copies, waits for them, and re-layouts  6.07 us (6%)
    all_to_all x1, blocking collectives, on_device(): terms = lax.all_to_all(terms, ('xl', 'y'), 0, 0, tiled=True)  36 us
    all_to_all x1, blocking collectives, on_device(): part = lax.all_to_all(part, 'z', 0, 0, tiled=True)  14.5 us
    ppermute x1, waiting for transfers between devices, on_device(): low1 = lax.ppermute(up1, ROWS, within)  8.19 us
    unnamed x12, local copies, waits for them, and re-layouts  6.07 us
    ppermute x1, starting transfers between devices, on_device(): high0 = lax.ppermute(h0, ROWS, ring(groups, groups - 1))  5.74 us
    pallas_call x2, Pallas kernels, near(): call(functools.partial(near_kernel, size, h), (like((rows, width), BF16),...  4.92 us
    ppermute x1, starting transfers between devices, on_device(): high1 = lax.ppermute(down1, ROWS, [(b, a) for a, b in within])  4.2 us
    ppermute x1, waiting for transfers between devices, on_device(): low0 = lax.ppermute(h0, ROWS, ring(groups, 1))  3.84 us
  transfers between devices with their start and end apart: 8, of which 3 were waited for; matrix products, arithmetic and copies ran while one was open for 0% of the time, Pallas kernels for 9%

profile of v10, /device:TPU:10, one launch (start us, length us, event | category | flops | bytes accessed | tf_op | source)
XLA Modules:
  0.0 97.9 jit_solution(16973458953653426149)
XLA Ops:
  0.6 3.2 %shard_map.68 = (bf16[1024,256]{1,0:T(8,128)(2,1)}, bf16[1024,256]{1,0:T(8,128)(2,1)}, bf16[2,1024,256]{2,1,0:T(8,128)(2,1)}) custom-call(s32[4,8]{1,0:T(4,128)} %bitcast.6, bf16[1024,512]{1,0:T(8,128)(2,1)} %slab_hbm.1), custom_call_target="tpu_custom_call" | custom-call | tf_op jit(solution)/shard_map/pallas_call | solution.py:177
  3.9 0.0 copy-start.4
  3.9 0.1 collective-permute-start.1
  4.0 0.7 collective-permute-start
  4.7 2.2 %collective-permute-start.6 = (bf16[2,1024,256]{2,1,0:T(8,128)(2,1)}, bf16[2,1024,256]{2,1,0:T(8,128)(2,1)S(1)}, u32[]{:S(2)}, u32[]{:S(2)}) collective-permute-start(bf16[2,1024,256]{2,1,0:T(8,128)(2,1)} %get-tuple-element.20), channel_id=1, source_target_pairs={{0,128},{128,0},{1,129},{129,1},{2,130},{130,2},{3,131},{131,3},{4... | collective-permute-start | bytes 3145736 | tf_op jit(solution)/shard_map/ppermute | solution.py:195
  6.9 5.7 %collective-permute-start.5 = (bf16[1024,256]{1,0:T(8,128)(2,1)}, bf16[1024,256]{1,0:T(8,128)(2,1)S(1)}, u32[]{:S(2)}, u32[]{:S(2)}) collective-permute-start(bf16[1024,256]{1,0:T(8,128)(2,1)} %get-tuple-element.16.h0_ref.rest_0_), channel_id=1, source_target_pairs={{0,63},{1,0},{2,1},{3,2},{4,3},{5,4},{6,5},{7,6},{8,7},{9,8},{10,9... | collective-permute-start | bytes 1572872 | tf_op jit(solution)/shard_map/ppermute | solution.py:192
  12.7 0.0 collective-permute-start.4
  12.7 0.0 collective-permute-done.refs_0_
  12.7 0.0 collective-permute-done.1.refs_1_.rest_2_
  12.7 1.0 %copy-done = bf16[1024,256]{1,0:T(8,128)(2,1)S(1)} copy-done((bf16[1024,256]{1,0:T(8,128)(2,1)S(1)}, bf16[1024,256]{1,0:T(8,128)(2,1)}, u32[]{:S(2)}) %copy-start) | copy-done | bytes 524312
  13.7 0.1 shard_map.71
  13.8 0.1 collective-permute-start.2
  13.9 4.2 %collective-permute-start.3 = (bf16[1024,256]{1,0:T(8,128)(2,1)S(1)}, bf16[1024,256]{1,0:T(8,128)(2,1)S(1)}, u32[]{:S(2)}, u32[]{:S(2)}) collective-permute-start(bf16[1024,256]{1,0:T(8,128)(2,1)S(1)} %get-tuple-element.22), channel_id=1, source_target_pairs={{1,0},{2,1},{3,2},{4,3},{5,4},{6,5},{7,6},{8,7},{9,8},{10,9},{11,1... | collective-permute-start | bytes 1572872 | tf_op jit(solution)/shard_map/ppermute | solution.py:209
  18.1 1.0 %copy-done.1 = bf16[1024,256]{1,0:T(8,128)(2,1)S(1)} copy-done((bf16[1024,256]{1,0:T(8,128)(2,1)S(1)}, bf16[1024,256]{1,0:T(8,128)(2,1)}, u32[]{:S(2)}) %copy-start.1) | copy-done | bytes 524312
  19.1 1.0 %copy-done.2 = bf16[1024,256]{1,0:T(8,128)(2,1)S(1)} copy-done((bf16[1024,256]{1,0:T(8,128)(2,1)S(1)}, bf16[1024,256]{1,0:T(8,128)(2,1)}, u32[]{:S(2)}) %copy-start.2) | copy-done | bytes 524312
  20.2 2.3 %copy-done.3 = bf16[1024,2176]{1,0:T(8,128)(2,1)S(1)} copy-done((bf16[1024,2176]{1,0:T(8,128)(2,1)S(1)}, bf16[1024,2176]{1,0:T(8,128)(2,1)}, u32[]{:S(2)}) %copy-start.3) | copy-done | bytes 4456472
  22.4 0.7 copy-done.5
  23.1 2.8 %shard_map.69 = (bf16[1024,2176]{1,0:T(8,128)(2,1)S(1)}, f32[1024,256]{1,0:T(8,128)S(1)}, f32[1024,256]{1,0:T(8,128)S(1)}) custom-call(s32[8,17]{1,0:T(8,128)S(1)} %copy-done.5, bf16[1024,2176]{1,0:T(8,128)(2,1)S(1)} %copy-done.3, bf16[1024,256]{1,0:T(8,128)(2,1)S(1)} %copy-done.2, bf16[1024,256]{1,0:T(8,128)(2,1)S(1)} %copy-done.1), custom_call_target="tpu_custom_call" | custom-call | flops 1073741824 | bytes 8912896 | tf_op jit(solution)/shard_map/pallas_call | solution.py:197
  25.9 0.0 collective-permute-done.5.high_ref
  25.9 3.8 %collective-permute-done.4.low_ref = bf16[1024,256]{1,0:T(8,128)(2,1)S(1)} collective-permute-done((bf16[1024,256]{1,0:T(8,128)(2,1)}, bf16[1024,256]{1,0:T(8,128)(2,1)S(1)}, u32[]{:S(2)}, u32[]{:S(2)}) %collective-permute-start.4) | collective-permute-done | bytes 524320 | tf_op jit(solution)/shard_map/ppermute | solution.py:191
  29.8 2.0 %shard_map.72 = (bf16[1024,256]{1,0:T(8,128)(2,1)S(1)}, bf16[256,1024]{1,0:T(8,128)(2,1)S(1)}, bf16[4,256,256]{2,1,0:T(8,128)(2,1)S(1)}) custom-call(s32[4,8]{1,0:T(4,128)S(1)} %bitcast.4, bf16[1024,2176]{1,0:T(8,128)(2,1)S(1)} %get-tuple-element.18.held_ref, f32[1024,256]{1,0:T(8,128)S(1)} %get-tuple-element.23.mid_ref, ...), custom_call_target="tpu_custom_call" | custom-call | flops 1140850688 | bytes 4194304 | tf_op jit(solution)/shard_map/pallas_call | solution.py:213
  31.8 8.2 %collective-permute-done.2.low_ref = bf16[1024,256]{1,0:T(8,128)(2,1)S(1)} collective-permute-done((bf16[1024,256]{1,0:T(8,128)(2,1)S(1)}, bf16[1024,256]{1,0:T(8,128)(2,1)S(1)}, u32[]{:S(2)}, u32[]{:S(2)}) %collective-permute-start.2) | collective-permute-done | bytes 524320 | tf_op jit(solution)/shard_map/ppermute | solution.py:208
  40.0 0.0 collective-permute-done.3.high_ref
  40.0 2.9 %shard_map.73 = (bf16[1024,512]{1,0:T(8,128)(2,1)}, bf16[256,1024]{1,0:T(8,128)(2,1)S(1)}, bf16[4,256,256]{2,1,0:T(8,128)(2,1)S(1)}) custom-call(s32[4,8]{1,0:T(4,128)S(1)} %bitcast.5, bf16[1024,2176]{1,0:T(8,128)(2,1)S(1)} %get-tuple-element.18.held_ref, f32[1024,256]{1,0:T(8,128)S(1)} %get-tuple-element.19.mid_ref, ...), custom_call_target="tpu_custom_call" | custom-call | flops 1140850688 | bytes 4194304 | tf_op jit(solution)/shard_map/pallas_call | solution.py:213
  42.9 0.0 collective-permute-done.6.refs_0_
  42.9 0.7 shard_map.75.far_ref
  43.6 1.9 %collective-permute-done.7.both_ref = bf16[2,1024,256]{2,1,0:T(8,128)(2,1)S(1)} collective-permute-done((bf16[2,1024,256]{2,1,0:T(8,128)(2,1)S(1)}, bf16[2,1024,256]{2,1,0:T(8,128)(2,1)S(1)}, u32[]{:S(2)}, u32[]{:S(2)}) %collective-permute-start.7) | collective-permute-done | bytes 1048608 | tf_op jit(solution)/shard_map/ppermute | solution.py:224
  45.6 0.7 shard_map.76
  46.3 36.0 %all_to_all.10.in_ref = bf16[8,256,512]{2,1,0:T(8,128)(2,1)S(1)} all-to-all(bf16[8,256,512]{2,1,0:T(8,128)(2,1)S(1)} %shard_map.76), channel_id=1, replica_groups=mesh['xh'=2,'core'=2,'xl'=2,'y'=4,'z'=8] {'xl','y'}, dimensions={0} | all-to-all | bytes 4194304 | tf_op jit(solution)/shard_map/all_to_all | solution.py:239
  82.3 0.3 shard_map.77
  82.7 14.5 %all_to_all.11.in_ref = bf16[8,32,512]{2,1,0:T(8,128)(2,1)S(1)} all-to-all(bf16[8,32,512]{2,1,0:T(8,128)(2,1)S(1)} %bitcast.3), channel_id=1, replica_groups=mesh['xh'=2,'core'=2,'xl'=2,'y'=4,'z'=8] {'z'}, dimensions={0} | all-to-all | bytes 524288 | tf_op jit(solution)/shard_map/all_to_all | solution.py:242
  97.2 0.7 shard_map.78
  (9 shorter events, 0.0 us)
Async XLA Ops:
  3.9 25.9 %copy-start.4 = (s32[8,4]{0,1:T(4,128)S(1)}, s32[8,4]{0,1:T(4,128)}, u32[]{:S(2)}) copy-start(s32[8,4]{0,1:T(4,128)} %param.9) | copy-start | bytes 388
  3.9 8.8 %collective-permute-start.1 = (bf16[2,1024,256]{2,1,0:T(8,128)(2,1)}, bf16[2,1024,256]{2,1,0:T(8,128)(2,1)S(1)}, u32[]{:S(2)}, u32[]{:S(2)}) collective-permute-start(bf16[2,1024,256]{2,1,0:T(8,128)(2,1)} %get-tuple-element.20), channel_id=1, source_target_pairs={{0,64},{64,0},{1,65},{65,1},{2,66},{66,2},{3,67},{67,3},{4,68},{68... | collective-permute-start | bytes 3145736 | tf_op jit(solution)/shard_map/ppermute | solution.py:196
  4.0 8.7 %collective-permute-start = (bf16[1024,256]{1,0:T(8,128)(2,1)}, bf16[1024,256]{1,0:T(8,128)(2,1)S(1)}, u32[]{:S(2)}, u32[]{:S(2)}) collective-permute-start(bf16[1024,256]{1,0:T(8,128)(2,1)} %get-tuple-element.17.h1_ref.own_ref.rest_1_), channel_id=1, source_target_pairs={{0,32},{31,63},{32,0},{63,31},{64,96},{95,127},{96,64},{127,95},{1... | collective-permute-start | bytes 1572872 | tf_op jit(solution)/shard_map/ppermute | solution.py:194
  4.7 38.2 %collective-permute-start.6 = (bf16[2,1024,256]{2,1,0:T(8,128)(2,1)}, bf16[2,1024,256]{2,1,0:T(8,128)(2,1)S(1)}, u32[]{:S(2)}, u32[]{:S(2)}) collective-permute-start(bf16[2,1024,256]{2,1,0:T(8,128)(2,1)} %get-tuple-element.20), channel_id=1, source_target_pairs={{0,128},{128,0},{1,129},{129,1},{2,130},{130,2},{3,131},{131,3},{4... | collective-permute-start | bytes 3145736 | tf_op jit(solution)/shard_map/ppermute | solution.py:195
  6.9 19.0 %collective-permute-start.5 = (bf16[1024,256]{1,0:T(8,128)(2,1)}, bf16[1024,256]{1,0:T(8,128)(2,1)S(1)}, u32[]{:S(2)}, u32[]{:S(2)}) collective-permute-start(bf16[1024,256]{1,0:T(8,128)(2,1)} %get-tuple-element.16.h0_ref.rest_0_), channel_id=1, source_target_pairs={{0,63},{1,0},{2,1},{3,2},{4,3},{5,4},{6,5},{7,6},{8,7},{9,8},{10,9... | collective-permute-start | bytes 1572872 | tf_op jit(solution)/shard_map/ppermute | solution.py:192
  12.7 17.1 %collective-permute-start.4 = (bf16[1024,256]{1,0:T(8,128)(2,1)}, bf16[1024,256]{1,0:T(8,128)(2,1)S(1)}, u32[]{:S(2)}, u32[]{:S(2)}) collective-permute-start(bf16[1024,256]{1,0:T(8,128)(2,1)} %get-tuple-element.16.h0_ref.rest_0_), channel_id=1, source_target_pairs={{0,1},{1,2},{2,3},{3,4},{4,5},{5,6},{6,7},{7,8},{8,9},{9,10},{10,1... | collective-permute-start | bytes 1572872 | tf_op jit(solution)/shard_map/ppermute | solution.py:191
  12.7 1.0 %copy-start = (bf16[1024,256]{1,0:T(8,128)(2,1)S(1)}, bf16[1024,256]{1,0:T(8,128)(2,1)}, u32[]{:S(2)}) copy-start(bf16[1024,256]{1,0:T(8,128)(2,1)} %get-tuple-element.17.h1_ref.own_ref.rest_1_) | copy-start | bytes 1572868
  13.8 26.2 %collective-permute-start.2 = (bf16[1024,256]{1,0:T(8,128)(2,1)S(1)}, bf16[1024,256]{1,0:T(8,128)(2,1)S(1)}, u32[]{:S(2)}, u32[]{:S(2)}) collective-permute-start(bf16[1024,256]{1,0:T(8,128)(2,1)S(1)} %get-tuple-element.21), channel_id=1, source_target_pairs={{0,1},{1,2},{2,3},{3,4},{4,5},{5,6},{6,7},{7,8},{8,9},{9,10},{10,1... | collective-permute-start | bytes 1572872 | tf_op jit(solution)/shard_map/ppermute | solution.py:208
  13.9 26.1 %collective-permute-start.3 = (bf16[1024,256]{1,0:T(8,128)(2,1)S(1)}, bf16[1024,256]{1,0:T(8,128)(2,1)S(1)}, u32[]{:S(2)}, u32[]{:S(2)}) collective-permute-start(bf16[1024,256]{1,0:T(8,128)(2,1)S(1)} %get-tuple-element.22), channel_id=1, source_target_pairs={{1,0},{2,1},{3,2},{4,3},{5,4},{6,5},{7,6},{8,7},{9,8},{10,9},{11,1... | collective-permute-start | bytes 1572872 | tf_op jit(solution)/shard_map/ppermute | solution.py:209
  18.1 1.0 %copy-start.1 = (bf16[1024,256]{1,0:T(8,128)(2,1)S(1)}, bf16[1024,256]{1,0:T(8,128)(2,1)}, u32[]{:S(2)}) copy-start(bf16[1024,256]{1,0:T(8,128)(2,1)} %get-tuple-element.17.h1_ref.own_ref.rest_1_) | copy-start | bytes 1572868
  19.1 1.0 %copy-start.2 = (bf16[1024,256]{1,0:T(8,128)(2,1)S(1)}, bf16[1024,256]{1,0:T(8,128)(2,1)}, u32[]{:S(2)}) copy-start(bf16[1024,256]{1,0:T(8,128)(2,1)} %get-tuple-element.16.h0_ref.rest_0_) | copy-start | bytes 1572868
  20.2 2.3 %copy-start.3 = (bf16[1024,2176]{1,0:T(8,128)(2,1)S(1)}, bf16[1024,2176]{1,0:T(8,128)(2,1)}, u32[]{:S(2)}) copy-start(bf16[1024,2176]{1,0:T(8,128)(2,1)} %fock_ref.1) | copy-start | bytes 13369348
  22.4 0.7 copy-start.5
  42.9 2.7 %collective-permute-start.7 = (bf16[2,1024,256]{2,1,0:T(8,128)(2,1)S(1)}, bf16[2,1024,256]{2,1,0:T(8,128)(2,1)S(1)}, u32[]{:S(2)}, u32[]{:S(2)}) collective-permute-start(bf16[2,1024,256]{2,1,0:T(8,128)(2,1)S(1)} %shard_map.74.far_ref), channel_id=1, source_target_pairs={{0,64},{64,0},{1,65},{65,1},{2,66},{66,2},{3,67},{67,3},{4,68},{68... | collective-permute-start | bytes 3145736 | tf_op jit(solution)/shard_map/ppermute | solution.py:224

commit v11 on v9

--- a/solution.py
+++ b/solution.py
@@ -121,24 +121,27 @@
             terms_ref[c, pl.ds(k * half, half), :] = dot(t[...], far_ref[c]).astype(BF16)
 
 
-def gather_kernel(t0_ref, t1_ref, both_ref, far_ref, out_ref):
+def gather_kernel(t0_ref, t1_ref, both_ref, near_ref, far_ref, out_ref):
     half = t0_ref.shape[0]
     core = lax.axis_index("core")
+    late = pl.ds(half, half)
     for c in range(2):
-        out_ref[core * 2 + c] = far_ref[c]
+        out_ref[core * 2 + c, :, late] = far_ref[c]
         for k, t in enumerate((t0_ref, t1_ref)):
-            out_ref[(1 - core) * 2 + c, pl.ds(k * half, half), :] = dot(t[...], both_ref[c]).astype(BF16)
-
-
-def first_sum_kernel(near_ref, far_ref, out_ref):
+            out_ref[(1 - core) * 2 + c, pl.ds(k * half, half), late] = dot(t[...], both_ref[c]).astype(BF16)
+    out_ref[:, :, :half] = near_ref[...]
+
+
+def first_sum_kernel(in_ref, out_ref):
     count, deep, _ = out_ref.shape
     inner = count // 2
     xh = lax.axis_index("xh")
-    for f, ref in enumerate((near_ref, far_ref)):
-        total = ref[0].astype(F32)
-        for s in range(1, ref.shape[0]):
-            total += ref[s].astype(F32)
-        turned = total.T.astype(BF16)
+    total = in_ref[0].astype(F32)
+    for s in range(1, in_ref.shape[0]):
+        total += in_ref[s].astype(F32)
+    half = total.shape[1] // 2
+    for f in range(2):
+        turned = total[:, f * half : (f + 1) * half].T.astype(BF16)
         for z in range(inner):
             out_ref[(xh ^ f) * inner + z] = turned[z * deep : (z + 1) * deep]
 
@@ -221,7 +224,6 @@
 
     product0, flipped0, terms0 = near(0, mid0, low0, high0)
     product, flipped1, terms1 = near(1, mid1, low1, high1, product0, terms0)
-    near_got = lax.all_to_all(terms1, "y", 0, 0, tiled=True)
     far = after(far, terms1)
     both = lax.ppermute(far, "core", swap)
     far_terms = call(
@@ -233,13 +235,13 @@
     )(flipped0, flipped1, far)
     terms = call(
         gather_kernel,
-        like((wide, columns, half), BF16),
-        [VMEM] * 4,
+        like((wide, columns, columns), BF16),
+        [VMEM] * 5,
         flops=4 * rows * half * columns,
         moved=8 * rows * columns,
-    )(flipped0, flipped1, both, far_terms)
-    far_got = lax.all_to_all(terms, "y", 0, 0, tiled=True)
-    part = call(first_sum_kernel, like((2 * deep, half // deep, columns), BF16), [VMEM] * 2)(near_got, far_got)
+    )(flipped0, flipped1, both, terms1, far_terms)
+    terms = lax.all_to_all(terms, "y", 0, 0, tiled=True)
+    part = call(first_sum_kernel, like((2 * deep, half // deep, columns), BF16), [VMEM])(terms)
     part = lax.all_to_all(part, ("xl", "z"), 0, 0, tiled=True)
     factor = 1.0 / math.sqrt(rows * groups)
     projected = call(

time: 107 us -> 103 us (0.963)
  blocking collectives: 40.5 us -> 53 us
  waiting for transfers between devices: 22.7 us -> 11.3 us
  starting transfers between devices: 21 us -> 17.5 us
  Pallas kernels: 15.1 us -> 13.6 us
    all_to_all x1 -> x0, waiting for transfers between devices: 13.3 us -> none  [on_device(): near_got = lax.all_to_all(terms1, 'y', 0, 0, tiled=True)]
    all_to_all x1, blocking collectives: 17.7 us -> 29.4 us  [on_device(): terms = lax.all_to_all(terms, 'y', 0, 0, tiled=True)]
    all_to_all x1 -> x0, starting transfers between devices: 3.53 us -> none  [on_device(): near_got = lax.all_to_all(terms1, 'y', 0, 0, tiled=True)]
    ppermute x1, waiting for transfers between devices: 0.01 us -> 1.94 us  [on_device(): both = lax.ppermute(far, 'core', swap)]
    pallas_call x1, Pallas kernels: 1.93 us -> 0.74 us  [on_device(): call(gather_kernel, like((wide, columns, columns), BF16), [VMEM] * 5, flo...]
  transfers between devices with their start and end apart: 9 -> 8, of which waited for: 3 -> 3; matrix products, arithmetic and copies ran while one was open for 0% -> 0% of each run, Pallas kernels for 10% -> 8%
where the time goes in v11:
time: 103 us; the launch traced here: 102 us
  blocking collectives  53 us (51%)
  starting transfers between devices  17.5 us (17%)
  Pallas kernels  13.6 us (13%)
  waiting for transfers between devices  11.3 us (11%)
  local copies, waits for them, and re-layouts  6.07 us (6%)
    all_to_all x1, blocking collectives, on_device(): terms = lax.all_to_all(terms, 'y', 0, 0, tiled=True)  29.4 us
    all_to_all x1, blocking collectives, on_device(): part = lax.all_to_all(part, ('xl', 'z'), 0, 0, tiled=True)  23.6 us
    ppermute x1, starting transfers between devices, on_device(): high1 = lax.ppermute(down1, ROWS, [(b, a) for a, b in within])  10.5 us
    ppermute x1, waiting for transfers between devices, on_device(): low1 = lax.ppermute(up1, ROWS, within)  8.19 us
    unnamed x12, local copies, waits for them, and re-layouts  6.07 us
    pallas_call x2, Pallas kernels, near(): call(functools.partial(near_kernel, size, h), (like((rows, width), BF16),...  4.94 us
    pallas_call x1, Pallas kernels, on_device(): call(functools.partial(mask_kernel, size), (piece, piece, like((2, rows,...  3.25 us
    pallas_call x1, Pallas kernels, on_device(): call(functools.partial(middle_kernel, size), (like((rows, slots * size),...  2.81 us
  transfers between devices with their start and end apart: 8, of which 3 were waited for; matrix products, arithmetic and copies ran while one was open for 0% of the time, Pallas kernels for 8%

profile of v11, /device:TPU:34, one launch (start us, length us, event | category | flops | bytes accessed | tf_op | source)
XLA Modules:
  0.0 102.2 jit_solution(2948636631452903031)
XLA Ops:
  0.6 3.2 %shard_map.68 = (bf16[1024,256]{1,0:T(8,128)(2,1)}, bf16[1024,256]{1,0:T(8,128)(2,1)}, bf16[2,1024,256]{2,1,0:T(8,128)(2,1)}) custom-call(s32[4,8]{1,0:T(4,128)} %bitcast.4, bf16[1024,512]{1,0:T(8,128)(2,1)} %slab_hbm.1), custom_call_target="tpu_custom_call" | custom-call | tf_op jit(solution)/shard_map/pallas_call | solution.py:181
  3.9 0.0 copy-start.4
  3.9 0.1 collective-permute-start.1
  4.0 0.7 collective-permute-start
  4.7 2.2 %collective-permute-start.6 = (bf16[2,1024,256]{2,1,0:T(8,128)(2,1)}, bf16[2,1024,256]{2,1,0:T(8,128)(2,1)S(1)}, u32[]{:S(2)}, u32[]{:S(2)}) collective-permute-start(bf16[2,1024,256]{2,1,0:T(8,128)(2,1)} %get-tuple-element.20), channel_id=1, source_target_pairs={{0,128},{128,0},{1,129},{129,1},{2,130},{130,2},{3,131},{131,3},{4... | collective-permute-start | bytes 3145736 | tf_op jit(solution)/shard_map/ppermute | solution.py:199
  6.9 2.2 %collective-permute-start.5 = (bf16[1024,256]{1,0:T(8,128)(2,1)}, bf16[1024,256]{1,0:T(8,128)(2,1)S(1)}, u32[]{:S(2)}, u32[]{:S(2)}) collective-permute-start(bf16[1024,256]{1,0:T(8,128)(2,1)} %get-tuple-element.16.h0_ref.rest_0_), channel_id=1, source_target_pairs={{0,63},{1,0},{2,1},{3,2},{4,3},{5,4},{6,5},{7,6},{8,7},{9,8},{10,9... | collective-permute-start | bytes 1572872 | tf_op jit(solution)/shard_map/ppermute | solution.py:196
  9.1 0.0 collective-permute-start.4
  9.1 0.0 collective-permute-done.refs_0_
  9.1 0.0 collective-permute-done.1.refs_1_.rest_2_
  9.1 1.0 %copy-done = bf16[1024,256]{1,0:T(8,128)(2,1)S(1)} copy-done((bf16[1024,256]{1,0:T(8,128)(2,1)S(1)}, bf16[1024,256]{1,0:T(8,128)(2,1)}, u32[]{:S(2)}) %copy-start) | copy-done | bytes 524312
  10.1 0.1 shard_map.71
  10.2 1.9 %collective-permute-start.2 = (bf16[1024,256]{1,0:T(8,128)(2,1)S(1)}, bf16[1024,256]{1,0:T(8,128)(2,1)S(1)}, u32[]{:S(2)}, u32[]{:S(2)}) collective-permute-start(bf16[1024,256]{1,0:T(8,128)(2,1)S(1)} %get-tuple-element.21), channel_id=1, source_target_pairs={{0,1},{1,2},{2,3},{3,4},{4,5},{5,6},{6,7},{7,8},{8,9},{9,10},{10,1... | collective-permute-start | bytes 1572872 | tf_op jit(solution)/shard_map/ppermute | solution.py:212
  12.1 10.5 %collective-permute-start.3 = (bf16[1024,256]{1,0:T(8,128)(2,1)S(1)}, bf16[1024,256]{1,0:T(8,128)(2,1)S(1)}, u32[]{:S(2)}, u32[]{:S(2)}) collective-permute-start(bf16[1024,256]{1,0:T(8,128)(2,1)S(1)} %get-tuple-element.22), channel_id=1, source_target_pairs={{1,0},{2,1},{3,2},{4,3},{5,4},{6,5},{7,6},{8,7},{9,8},{10,9},{11,1... | collective-permute-start | bytes 1572872 | tf_op jit(solution)/shard_map/ppermute | solution.py:213
  22.6 1.0 %copy-done.1 = bf16[1024,256]{1,0:T(8,128)(2,1)S(1)} copy-done((bf16[1024,256]{1,0:T(8,128)(2,1)S(1)}, bf16[1024,256]{1,0:T(8,128)(2,1)}, u32[]{:S(2)}) %copy-start.1) | copy-done | bytes 524312
  23.6 1.0 %copy-done.2 = bf16[1024,256]{1,0:T(8,128)(2,1)S(1)} copy-done((bf16[1024,256]{1,0:T(8,128)(2,1)S(1)}, bf16[1024,256]{1,0:T(8,128)(2,1)}, u32[]{:S(2)}) %copy-start.2) | copy-done | bytes 524312
  24.6 2.3 %copy-done.3 = bf16[1024,2176]{1,0:T(8,128)(2,1)S(1)} copy-done((bf16[1024,2176]{1,0:T(8,128)(2,1)S(1)}, bf16[1024,2176]{1,0:T(8,128)(2,1)}, u32[]{:S(2)}) %copy-start.3) | copy-done | bytes 4456472
  26.9 0.7 copy-done.5
  27.6 2.8 %shard_map.69 = (bf16[1024,2176]{1,0:T(8,128)(2,1)S(1)}, f32[1024,256]{1,0:T(8,128)S(1)}, f32[1024,256]{1,0:T(8,128)S(1)}) custom-call(s32[8,17]{1,0:T(8,128)S(1)} %copy-done.5, bf16[1024,2176]{1,0:T(8,128)(2,1)S(1)} %copy-done.3, bf16[1024,256]{1,0:T(8,128)(2,1)S(1)} %copy-done.2, bf16[1024,256]{1,0:T(8,128)(2,1)S(1)} %copy-done.1), custom_call_target="tpu_custom_call" | custom-call | flops 1073741824 | bytes 8912896 | tf_op jit(solution)/shard_map/pallas_call | solution.py:201
  30.4 0.0 collective-permute-done.5.high_ref
  30.4 1.2 %collective-permute-done.4.low_ref = bf16[1024,256]{1,0:T(8,128)(2,1)S(1)} collective-permute-done((bf16[1024,256]{1,0:T(8,128)(2,1)}, bf16[1024,256]{1,0:T(8,128)(2,1)S(1)}, u32[]{:S(2)}, u32[]{:S(2)}) %collective-permute-start.4) | collective-permute-done | bytes 524320 | tf_op jit(solution)/shard_map/ppermute | solution.py:195
  31.6 2.0 %shard_map.72 = (bf16[1024,256]{1,0:T(8,128)(2,1)S(1)}, bf16[256,1024]{1,0:T(8,128)(2,1)S(1)}, bf16[4,256,256]{2,1,0:T(8,128)(2,1)S(1)}) custom-call(s32[4,8]{1,0:T(4,128)S(1)} %bitcast.2, bf16[1024,2176]{1,0:T(8,128)(2,1)S(1)} %get-tuple-element.18.held_ref, f32[1024,256]{1,0:T(8,128)S(1)} %get-tuple-element.23.mid_ref, ...), custom_call_target="tpu_custom_call" | custom-call | flops 1140850688 | bytes 4194304 | tf_op jit(solution)/shard_map/pallas_call | solution.py:217
  33.6 8.2 %collective-permute-done.2.low_ref = bf16[1024,256]{1,0:T(8,128)(2,1)S(1)} collective-permute-done((bf16[1024,256]{1,0:T(8,128)(2,1)S(1)}, bf16[1024,256]{1,0:T(8,128)(2,1)S(1)}, u32[]{:S(2)}, u32[]{:S(2)}) %collective-permute-start.2) | collective-permute-done | bytes 524320 | tf_op jit(solution)/shard_map/ppermute | solution.py:212
  41.8 0.0 collective-permute-done.3.high_ref
  41.8 3.0 %shard_map.73 = (bf16[1024,512]{1,0:T(8,128)(2,1)}, bf16[256,1024]{1,0:T(8,128)(2,1)S(1)}, bf16[4,512,256]{2,1,0:T(8,128)(2,1)S(1)}) custom-call(s32[4,8]{1,0:T(4,128)S(1)} %bitcast.3, bf16[1024,2176]{1,0:T(8,128)(2,1)S(1)} %get-tuple-element.18.held_ref, f32[1024,256]{1,0:T(8,128)S(1)} %get-tuple-element.19.mid_ref, ...), custom_call_target="tpu_custom_call" | custom-call | flops 1140850688 | bytes 4194304 | tf_op jit(solution)/shard_map/pallas_call | solution.py:217
  44.8 0.0 collective-permute-done.6.refs_0_
  44.8 0.7 shard_map.75.far_ref
  45.5 1.9 %collective-permute-done.7.both_ref = bf16[2,1024,256]{2,1,0:T(8,128)(2,1)S(1)} collective-permute-done((bf16[2,1024,256]{2,1,0:T(8,128)(2,1)S(1)}, bf16[2,1024,256]{2,1,0:T(8,128)(2,1)S(1)}, u32[]{:S(2)}, u32[]{:S(2)}) %collective-permute-start.7) | collective-permute-done | bytes 1048608 | tf_op jit(solution)/shard_map/ppermute | solution.py:228
  47.4 0.7 shard_map.76
  48.2 29.4 %all_to_all.10.in_ref = bf16[4,512,512]{2,1,0:T(8,128)(2,1)S(1)} all-to-all(bf16[4,512,512]{2,1,0:T(8,128)(2,1)S(1)} %shard_map.76), channel_id=1, replica_groups=mesh['xh'=2,'core'=2,'xl'=2,'y'=4,'z'=8] {'y'}, dimensions={0} | all-to-all | bytes 4194304 | tf_op jit(solution)/shard_map/all_to_all | solution.py:243
  77.6 0.4 shard_map.77
  77.9 23.6 %all_to_all.11.in_ref = bf16[16,32,512]{2,1,0:T(8,128)(2,1)S(1)} all-to-all(bf16[16,32,512]{2,1,0:T(8,128)(2,1)S(1)} %shard_map.77), channel_id=1, replica_groups=mesh['xh'=2,'core'=2,'xl'=2,'y'=4,'z'=8] {'xl','z'}, dimensions={0} | all-to-all | bytes 1048576 | tf_op jit(solution)/shard_map/all_to_all | solution.py:245
  101.5 0.7 shard_map.78
  (9 shorter events, 0.0 us)
Async XLA Ops:
  3.9 27.7 %copy-start.4 = (s32[8,4]{0,1:T(4,128)S(1)}, s32[8,4]{0,1:T(4,128)}, u32[]{:S(2)}) copy-start(s32[8,4]{0,1:T(4,128)} %param.9) | copy-start | bytes 388
  3.9 5.2 %collective-permute-start.1 = (bf16[2,1024,256]{2,1,0:T(8,128)(2,1)}, bf16[2,1024,256]{2,1,0:T(8,128)(2,1)S(1)}, u32[]{:S(2)}, u32[]{:S(2)}) collective-permute-start(bf16[2,1024,256]{2,1,0:T(8,128)(2,1)} %get-tuple-element.20), channel_id=1, source_target_pairs={{0,64},{64,0},{1,65},{65,1},{2,66},{66,2},{3,67},{67,3},{4,68},{68... | collective-permute-start | bytes 3145736 | tf_op jit(solution)/shard_map/ppermute | solution.py:200
  4.0 5.1 %collective-permute-start = (bf16[1024,256]{1,0:T(8,128)(2,1)}, bf16[1024,256]{1,0:T(8,128)(2,1)S(1)}, u32[]{:S(2)}, u32[]{:S(2)}) collective-permute-start(bf16[1024,256]{1,0:T(8,128)(2,1)} %get-tuple-element.17.h1_ref.own_ref.rest_1_), channel_id=1, source_target_pairs={{0,32},{31,63},{32,0},{63,31},{64,96},{95,127},{96,64},{127,95},{1... | collective-permute-start | bytes 1572872 | tf_op jit(solution)/shard_map/ppermute | solution.py:198
  4.7 40.1 %collective-permute-start.6 = (bf16[2,1024,256]{2,1,0:T(8,128)(2,1)}, bf16[2,1024,256]{2,1,0:T(8,128)(2,1)S(1)}, u32[]{:S(2)}, u32[]{:S(2)}) collective-permute-start(bf16[2,1024,256]{2,1,0:T(8,128)(2,1)} %get-tuple-element.20), channel_id=1, source_target_pairs={{0,128},{128,0},{1,129},{129,1},{2,130},{130,2},{3,131},{131,3},{4... | collective-permute-start | bytes 3145736 | tf_op jit(solution)/shard_map/ppermute | solution.py:199
  6.9 23.5 %collective-permute-start.5 = (bf16[1024,256]{1,0:T(8,128)(2,1)}, bf16[1024,256]{1,0:T(8,128)(2,1)S(1)}, u32[]{:S(2)}, u32[]{:S(2)}) collective-permute-start(bf16[1024,256]{1,0:T(8,128)(2,1)} %get-tuple-element.16.h0_ref.rest_0_), channel_id=1, source_target_pairs={{0,63},{1,0},{2,1},{3,2},{4,3},{5,4},{6,5},{7,6},{8,7},{9,8},{10,9... | collective-permute-start | bytes 1572872 | tf_op jit(solution)/shard_map/ppermute | solution.py:196
  9.1 22.6 %collective-permute-start.4 = (bf16[1024,256]{1,0:T(8,128)(2,1)}, bf16[1024,256]{1,0:T(8,128)(2,1)S(1)}, u32[]{:S(2)}, u32[]{:S(2)}) collective-permute-start(bf16[1024,256]{1,0:T(8,128)(2,1)} %get-tuple-element.16.h0_ref.rest_0_), channel_id=1, source_target_pairs={{0,1},{1,2},{2,3},{3,4},{4,5},{5,6},{6,7},{7,8},{8,9},{9,10},{10,1... | collective-permute-start | bytes 1572872 | tf_op jit(solution)/shard_map/ppermute | solution.py:195
  9.1 1.0 %copy-start = (bf16[1024,256]{1,0:T(8,128)(2,1)S(1)}, bf16[1024,256]{1,0:T(8,128)(2,1)}, u32[]{:S(2)}) copy-start(bf16[1024,256]{1,0:T(8,128)(2,1)} %get-tuple-element.17.h1_ref.own_ref.rest_1_) | copy-start | bytes 1572868
  10.2 31.6 %collective-permute-start.2 = (bf16[1024,256]{1,0:T(8,128)(2,1)S(1)}, bf16[1024,256]{1,0:T(8,128)(2,1)S(1)}, u32[]{:S(2)}, u32[]{:S(2)}) collective-permute-start(bf16[1024,256]{1,0:T(8,128)(2,1)S(1)} %get-tuple-element.21), channel_id=1, source_target_pairs={{0,1},{1,2},{2,3},{3,4},{4,5},{5,6},{6,7},{7,8},{8,9},{9,10},{10,1... | collective-permute-start | bytes 1572872 | tf_op jit(solution)/shard_map/ppermute | solution.py:212
  12.1 29.8 %collective-permute-start.3 = (bf16[1024,256]{1,0:T(8,128)(2,1)S(1)}, bf16[1024,256]{1,0:T(8,128)(2,1)S(1)}, u32[]{:S(2)}, u32[]{:S(2)}) collective-permute-start(bf16[1024,256]{1,0:T(8,128)(2,1)S(1)} %get-tuple-element.22), channel_id=1, source_target_pairs={{1,0},{2,1},{3,2},{4,3},{5,4},{6,5},{7,6},{8,7},{9,8},{10,9},{11,1... | collective-permute-start | bytes 1572872 | tf_op jit(solution)/shard_map/ppermute | solution.py:213
  22.6 1.0 %copy-start.1 = (bf16[1024,256]{1,0:T(8,128)(2,1)S(1)}, bf16[1024,256]{1,0:T(8,128)(2,1)}, u32[]{:S(2)}) copy-start(bf16[1024,256]{1,0:T(8,128)(2,1)} %get-tuple-element.17.h1_ref.own_ref.rest_1_) | copy-start | bytes 1572868
  23.6 1.0 %copy-start.2 = (bf16[1024,256]{1,0:T(8,128)(2,1)S(1)}, bf16[1024,256]{1,0:T(8,128)(2,1)}, u32[]{:S(2)}) copy-start(bf16[1024,256]{1,0:T(8,128)(2,1)} %get-tuple-element.16.h0_ref.rest_0_) | copy-start | bytes 1572868
  24.6 2.3 %copy-start.3 = (bf16[1024,2176]{1,0:T(8,128)(2,1)S(1)}, bf16[1024,2176]{1,0:T(8,128)(2,1)}, u32[]{:S(2)}) copy-start(bf16[1024,2176]{1,0:T(8,128)(2,1)} %fock_ref.1) | copy-start | bytes 13369348
  26.9 0.7 copy-start.5
  44.8 2.7 %collective-permute-start.7 = (bf16[2,1024,256]{2,1,0:T(8,128)(2,1)S(1)}, bf16[2,1024,256]{2,1,0:T(8,128)(2,1)S(1)}, u32[]{:S(2)}, u32[]{:S(2)}) collective-permute-start(bf16[2,1024,256]{2,1,0:T(8,128)(2,1)S(1)} %shard_map.74.far_ref), channel_id=1, source_target_pairs={{0,64},{64,0},{1,65},{65,1},{2,66},{66,2},{3,67},{67,3},{4,68},{68... | collective-permute-start | bytes 3145736 | tf_op jit(solution)/shard_map/ppermute | solution.py:228

commit v12 on v4

--- a/solution.py
+++ b/solution.py
@@ -33,13 +33,16 @@
     return jnp.dot(a, b, preferred_element_type=F32)
 
 
-def mask_kernel(size, mask_ref, slab_hbm, h0_hbm, h1_hbm, both_hbm, loaded, kept, in_sems, out_sems):
+def mask_kernel(size, mask_hbm, slab_hbm, h0_hbm, h1_hbm, both_hbm, mask_ref, loaded, kept, mask_sem, in_sems, out_sems):
     panels, blocks = mask_ref.shape
+    mask_load = pltpu.make_async_copy(mask_hbm, mask_ref, mask_sem)
+    mask_load.start()
     half = panels // 2
     at = [pl.ds(i * size, size) for i in range(blocks)]
     loads = [pltpu.make_async_copy(slab_hbm.at[at[i]], loaded.at[at[i]], in_sems.at[i]) for i in range(blocks)]
     for load in loads:
         load.start()
+    mask_load.wait()
     stores = []
     for i, load in enumerate(loads):
         load.wait()
@@ -175,10 +178,12 @@
     h0, h1, panels = call(
         functools.partial(mask_kernel, size),
         (piece, piece, like((2, rows, half), BF16)),
-        [SMEM, HBM],
+        [HBM, HBM],
         [
+            pltpu.SMEM(orbital_mask.shape[::-1], jnp.int32),
             pltpu.VMEM((rows, columns), BF16),
             pltpu.VMEM((2, rows, half), BF16),
+            pltpu.SemaphoreType.DMA,
             pltpu.SemaphoreType.DMA((blocks,)),
             pltpu.SemaphoreType.DMA((blocks, 4)),
         ],

time: 98.3 us -> 97.6 us (level)
  no operation moved by 1% of the time
where the time goes in v12:
time: 97.6 us; the launch traced here: 97.2 us
  blocking collectives  50.6 us (52%)
  waiting for transfers between devices  14 us (14%)
  starting transfers between devices  13 us (13%)
  Pallas kernels  12.8 us (13%)
  local copies, waits for them, and re-layouts  6.07 us (6%)
    all_to_all x1, blocking collectives, on_device(): terms = lax.all_to_all(terms, ('xl', 'y'), 0, 0, tiled=True)  36.1 us
    all_to_all x1, blocking collectives, on_device(): part = lax.all_to_all(part, 'z', 0, 0, tiled=True)  14.5 us
    ppermute x1, waiting for transfers between devices, on_device(): low1 = lax.ppermute(up1, ROWS, within)  8.19 us
    unnamed x12, local copies, waits for them, and re-layouts  6.07 us
    ppermute x1, starting transfers between devices, on_device(): high0 = lax.ppermute(h0, ROWS, ring(groups, groups - 1))  5.74 us
    pallas_call x2, Pallas kernels, near(): call(functools.partial(near_kernel, size, h), (like((rows, width), BF16),...  4.91 us
    ppermute x1, starting transfers between devices, on_device(): high1 = lax.ppermute(down1, ROWS, [(b, a) for a, b in within])  4.2 us
    ppermute x1, waiting for transfers between devices, on_device(): low0 = lax.ppermute(h0, ROWS, ring(groups, 1))  3.84 us
  transfers between devices with their start and end apart: 8, of which 3 were waited for; matrix products, arithmetic and copies ran while one was open for 0% of the time, Pallas kernels for 9%

profile of v12, /device:TPU:10, one launch (start us, length us, event | category | flops | bytes accessed | tf_op | source)
XLA Modules:
  0.0 97.2 jit_solution(9368615830627875106)
XLA Ops:
  0.6 2.6 %shard_map.68 = (bf16[1024,256]{1,0:T(8,128)(2,1)}, bf16[1024,256]{1,0:T(8,128)(2,1)}, bf16[2,1024,256]{2,1,0:T(8,128)(2,1)}) custom-call(s32[4,8]{1,0:T(4,128)} %bitcast.6, bf16[1024,512]{1,0:T(8,128)(2,1)} %slab_hbm.1), custom_call_target="tpu_custom_call" | custom-call | tf_op jit(solution)/shard_map/pallas_call | solution.py:178
  3.2 0.0 copy-start.4
  3.2 0.1 collective-permute-start.1
  3.3 0.7 collective-permute-start
  4.0 2.2 %collective-permute-start.6 = (bf16[2,1024,256]{2,1,0:T(8,128)(2,1)}, bf16[2,1024,256]{2,1,0:T(8,128)(2,1)S(1)}, u32[]{:S(2)}, u32[]{:S(2)}) collective-permute-start(bf16[2,1024,256]{2,1,0:T(8,128)(2,1)} %get-tuple-element.20), channel_id=1, source_target_pairs={{0,128},{128,0},{1,129},{129,1},{2,130},{130,2},{3,131},{131,3},{4... | collective-permute-start | bytes 3145736 | tf_op jit(solution)/shard_map/ppermute | solution.py:198
  6.2 5.7 %collective-permute-start.5 = (bf16[1024,256]{1,0:T(8,128)(2,1)}, bf16[1024,256]{1,0:T(8,128)(2,1)S(1)}, u32[]{:S(2)}, u32[]{:S(2)}) collective-permute-start(bf16[1024,256]{1,0:T(8,128)(2,1)} %get-tuple-element.16.h0_ref.rest_0_), channel_id=1, source_target_pairs={{0,63},{1,0},{2,1},{3,2},{4,3},{5,4},{6,5},{7,6},{8,7},{9,8},{10,9... | collective-permute-start | bytes 1572872 | tf_op jit(solution)/shard_map/ppermute | solution.py:195
  12.0 0.0 collective-permute-start.4
  12.0 0.0 collective-permute-done.refs_0_
  12.0 0.0 collective-permute-done.1.refs_1_.rest_2_
  12.0 1.0 %copy-done = bf16[1024,256]{1,0:T(8,128)(2,1)S(1)} copy-done((bf16[1024,256]{1,0:T(8,128)(2,1)S(1)}, bf16[1024,256]{1,0:T(8,128)(2,1)}, u32[]{:S(2)}) %copy-start) | copy-done | bytes 524312
  13.0 0.1 shard_map.71
  13.1 0.1 collective-permute-start.2
  13.2 4.2 %collective-permute-start.3 = (bf16[1024,256]{1,0:T(8,128)(2,1)S(1)}, bf16[1024,256]{1,0:T(8,128)(2,1)S(1)}, u32[]{:S(2)}, u32[]{:S(2)}) collective-permute-start(bf16[1024,256]{1,0:T(8,128)(2,1)S(1)} %get-tuple-element.22), channel_id=1, source_target_pairs={{1,0},{2,1},{3,2},{4,3},{5,4},{6,5},{7,6},{8,7},{9,8},{10,9},{11,1... | collective-permute-start | bytes 1572872 | tf_op jit(solution)/shard_map/ppermute | solution.py:212
  17.4 1.0 %copy-done.1 = bf16[1024,256]{1,0:T(8,128)(2,1)S(1)} copy-done((bf16[1024,256]{1,0:T(8,128)(2,1)S(1)}, bf16[1024,256]{1,0:T(8,128)(2,1)}, u32[]{:S(2)}) %copy-start.1) | copy-done | bytes 524312
  18.4 1.0 %copy-done.2 = bf16[1024,256]{1,0:T(8,128)(2,1)S(1)} copy-done((bf16[1024,256]{1,0:T(8,128)(2,1)S(1)}, bf16[1024,256]{1,0:T(8,128)(2,1)}, u32[]{:S(2)}) %copy-start.2) | copy-done | bytes 524312
  19.5 2.3 %copy-done.3 = bf16[1024,2176]{1,0:T(8,128)(2,1)S(1)} copy-done((bf16[1024,2176]{1,0:T(8,128)(2,1)S(1)}, bf16[1024,2176]{1,0:T(8,128)(2,1)}, u32[]{:S(2)}) %copy-start.3) | copy-done | bytes 4456472
  21.8 0.7 copy-done.5
  22.4 2.8 %shard_map.69 = (bf16[1024,2176]{1,0:T(8,128)(2,1)S(1)}, f32[1024,256]{1,0:T(8,128)S(1)}, f32[1024,256]{1,0:T(8,128)S(1)}) custom-call(s32[8,17]{1,0:T(8,128)S(1)} %copy-done.5, bf16[1024,2176]{1,0:T(8,128)(2,1)S(1)} %copy-done.3, bf16[1024,256]{1,0:T(8,128)(2,1)S(1)} %copy-done.2, bf16[1024,256]{1,0:T(8,128)(2,1)S(1)} %copy-done.1), custom_call_target="tpu_custom_call" | custom-call | flops 1073741824 | bytes 8912896 | tf_op jit(solution)/shard_map/pallas_call | solution.py:200
  25.2 0.0 collective-permute-done.5.high_ref
  25.3 3.8 %collective-permute-done.4.low_ref = bf16[1024,256]{1,0:T(8,128)(2,1)S(1)} collective-permute-done((bf16[1024,256]{1,0:T(8,128)(2,1)}, bf16[1024,256]{1,0:T(8,128)(2,1)S(1)}, u32[]{:S(2)}, u32[]{:S(2)}) %collective-permute-start.4) | collective-permute-done | bytes 524320 | tf_op jit(solution)/shard_map/ppermute | solution.py:194
  29.1 2.0 %shard_map.72 = (bf16[1024,256]{1,0:T(8,128)(2,1)S(1)}, bf16[256,1024]{1,0:T(8,128)(2,1)S(1)}, bf16[4,256,256]{2,1,0:T(8,128)(2,1)S(1)}) custom-call(s32[4,8]{1,0:T(4,128)S(1)} %bitcast.4, bf16[1024,2176]{1,0:T(8,128)(2,1)S(1)} %get-tuple-element.18.held_ref, f32[1024,256]{1,0:T(8,128)S(1)} %get-tuple-element.23.mid_ref, ...), custom_call_target="tpu_custom_call" | custom-call | flops 1140850688 | bytes 4194304 | tf_op jit(solution)/shard_map/pallas_call | solution.py:216
  31.1 8.2 %collective-permute-done.2.low_ref = bf16[1024,256]{1,0:T(8,128)(2,1)S(1)} collective-permute-done((bf16[1024,256]{1,0:T(8,128)(2,1)S(1)}, bf16[1024,256]{1,0:T(8,128)(2,1)S(1)}, u32[]{:S(2)}, u32[]{:S(2)}) %collective-permute-start.2) | collective-permute-done | bytes 524320 | tf_op jit(solution)/shard_map/ppermute | solution.py:211
  39.3 0.0 collective-permute-done.3.high_ref
  39.3 2.9 %shard_map.73 = (bf16[1024,512]{1,0:T(8,128)(2,1)}, bf16[256,1024]{1,0:T(8,128)(2,1)S(1)}, bf16[4,256,256]{2,1,0:T(8,128)(2,1)S(1)}) custom-call(s32[4,8]{1,0:T(4,128)S(1)} %bitcast.5, bf16[1024,2176]{1,0:T(8,128)(2,1)S(1)} %get-tuple-element.18.held_ref, f32[1024,256]{1,0:T(8,128)S(1)} %get-tuple-element.19.mid_ref, ...), custom_call_target="tpu_custom_call" | custom-call | flops 1140850688 | bytes 4194304 | tf_op jit(solution)/shard_map/pallas_call | solution.py:216
  42.2 0.0 collective-permute-start.7
  42.2 0.7 shard_map.75.far_ref
  42.9 1.9 %collective-permute-done.7.both_ref = bf16[2,1024,256]{2,1,0:T(8,128)(2,1)S(1)} collective-permute-done((bf16[2,1024,256]{2,1,0:T(8,128)(2,1)S(1)}, bf16[2,1024,256]{2,1,0:T(8,128)(2,1)S(1)}, u32[]{:S(2)}, u32[]{:S(2)}) %collective-permute-start.7) | collective-permute-done | bytes 1048608 | tf_op jit(solution)/shard_map/ppermute | solution.py:227
  44.9 0.7 shard_map.76
  45.6 36.1 %all_to_all.10.in_ref = bf16[8,512,256]{2,1,0:T(8,128)(2,1)S(1)} all-to-all(bf16[8,512,256]{2,1,0:T(8,128)(2,1)S(1)} %shard_map.76), channel_id=1, replica_groups=mesh['xh'=2,'core'=2,'xl'=2,'y'=4,'z'=8] {'xl','y'}, dimensions={0} | all-to-all | bytes 4194304 | tf_op jit(solution)/shard_map/all_to_all | solution.py:242
  81.7 0.3 shard_map.77
  82.0 14.5 %all_to_all.11.in_ref = bf16[8,32,512]{2,1,0:T(8,128)(2,1)S(1)} all-to-all(bf16[8,32,512]{2,1,0:T(8,128)(2,1)S(1)} %bitcast.3), channel_id=1, replica_groups=mesh['xh'=2,'core'=2,'xl'=2,'y'=4,'z'=8] {'z'}, dimensions={0} | all-to-all | bytes 524288 | tf_op jit(solution)/shard_map/all_to_all | solution.py:245
  96.5 0.7 shard_map.78
  (9 shorter events, 0.0 us)
Async XLA Ops:
  3.2 25.9 %copy-start.4 = (s32[8,4]{0,1:T(4,128)S(1)}, s32[8,4]{0,1:T(4,128)}, u32[]{:S(2)}) copy-start(s32[8,4]{0,1:T(4,128)} %param.9) | copy-start | bytes 388
  3.2 8.8 %collective-permute-start.1 = (bf16[2,1024,256]{2,1,0:T(8,128)(2,1)}, bf16[2,1024,256]{2,1,0:T(8,128)(2,1)S(1)}, u32[]{:S(2)}, u32[]{:S(2)}) collective-permute-start(bf16[2,1024,256]{2,1,0:T(8,128)(2,1)} %get-tuple-element.20), channel_id=1, source_target_pairs={{0,64},{64,0},{1,65},{65,1},{2,66},{66,2},{3,67},{67,3},{4,68},{68... | collective-permute-start | bytes 3145736 | tf_op jit(solution)/shard_map/ppermute | solution.py:199
  3.3 8.7 %collective-permute-start = (bf16[1024,256]{1,0:T(8,128)(2,1)}, bf16[1024,256]{1,0:T(8,128)(2,1)S(1)}, u32[]{:S(2)}, u32[]{:S(2)}) collective-permute-start(bf16[1024,256]{1,0:T(8,128)(2,1)} %get-tuple-element.17.h1_ref.own_ref.rest_1_), channel_id=1, source_target_pairs={{0,32},{31,63},{32,0},{63,31},{64,96},{95,127},{96,64},{127,95},{1... | collective-permute-start | bytes 1572872 | tf_op jit(solution)/shard_map/ppermute | solution.py:197
  4.0 38.2 %collective-permute-start.6 = (bf16[2,1024,256]{2,1,0:T(8,128)(2,1)}, bf16[2,1024,256]{2,1,0:T(8,128)(2,1)S(1)}, u32[]{:S(2)}, u32[]{:S(2)}) collective-permute-start(bf16[2,1024,256]{2,1,0:T(8,128)(2,1)} %get-tuple-element.20), channel_id=1, source_target_pairs={{0,128},{128,0},{1,129},{129,1},{2,130},{130,2},{3,131},{131,3},{4... | collective-permute-start | bytes 3145736 | tf_op jit(solution)/shard_map/ppermute | solution.py:198
  6.2 19.0 %collective-permute-start.5 = (bf16[1024,256]{1,0:T(8,128)(2,1)}, bf16[1024,256]{1,0:T(8,128)(2,1)S(1)}, u32[]{:S(2)}, u32[]{:S(2)}) collective-permute-start(bf16[1024,256]{1,0:T(8,128)(2,1)} %get-tuple-element.16.h0_ref.rest_0_), channel_id=1, source_target_pairs={{0,63},{1,0},{2,1},{3,2},{4,3},{5,4},{6,5},{7,6},{8,7},{9,8},{10,9... | collective-permute-start | bytes 1572872 | tf_op jit(solution)/shard_map/ppermute | solution.py:195
  12.0 17.1 %collective-permute-start.4 = (bf16[1024,256]{1,0:T(8,128)(2,1)}, bf16[1024,256]{1,0:T(8,128)(2,1)S(1)}, u32[]{:S(2)}, u32[]{:S(2)}) collective-permute-start(bf16[1024,256]{1,0:T(8,128)(2,1)} %get-tuple-element.16.h0_ref.rest_0_), channel_id=1, source_target_pairs={{0,1},{1,2},{2,3},{3,4},{4,5},{5,6},{6,7},{7,8},{8,9},{9,10},{10,1... | collective-permute-start | bytes 1572872 | tf_op jit(solution)/shard_map/ppermute | solution.py:194
  12.0 1.0 %copy-start = (bf16[1024,256]{1,0:T(8,128)(2,1)S(1)}, bf16[1024,256]{1,0:T(8,128)(2,1)}, u32[]{:S(2)}) copy-start(bf16[1024,256]{1,0:T(8,128)(2,1)} %get-tuple-element.17.h1_ref.own_ref.rest_1_) | copy-start | bytes 1572868
  13.1 26.2 %collective-permute-start.2 = (bf16[1024,256]{1,0:T(8,128)(2,1)S(1)}, bf16[1024,256]{1,0:T(8,128)(2,1)S(1)}, u32[]{:S(2)}, u32[]{:S(2)}) collective-permute-start(bf16[1024,256]{1,0:T(8,128)(2,1)S(1)} %get-tuple-element.21), channel_id=1, source_target_pairs={{0,1},{1,2},{2,3},{3,4},{4,5},{5,6},{6,7},{7,8},{8,9},{9,10},{10,1... | collective-permute-start | bytes 1572872 | tf_op jit(solution)/shard_map/ppermute | solution.py:211
  13.2 26.1 %collective-permute-start.3 = (bf16[1024,256]{1,0:T(8,128)(2,1)S(1)}, bf16[1024,256]{1,0:T(8,128)(2,1)S(1)}, u32[]{:S(2)}, u32[]{:S(2)}) collective-permute-start(bf16[1024,256]{1,0:T(8,128)(2,1)S(1)} %get-tuple-element.22), channel_id=1, source_target_pairs={{1,0},{2,1},{3,2},{4,3},{5,4},{6,5},{7,6},{8,7},{9,8},{10,9},{11,1... | collective-permute-start | bytes 1572872 | tf_op jit(solution)/shard_map/ppermute | solution.py:212
  17.4 1.0 %copy-start.1 = (bf16[1024,256]{1,0:T(8,128)(2,1)S(1)}, bf16[1024,256]{1,0:T(8,128)(2,1)}, u32[]{:S(2)}) copy-start(bf16[1024,256]{1,0:T(8,128)(2,1)} %get-tuple-element.17.h1_ref.own_ref.rest_1_) | copy-start | bytes 1572868
  18.4 1.0 %copy-start.2 = (bf16[1024,256]{1,0:T(8,128)(2,1)S(1)}, bf16[1024,256]{1,0:T(8,128)(2,1)}, u32[]{:S(2)}) copy-start(bf16[1024,256]{1,0:T(8,128)(2,1)} %get-tuple-element.16.h0_ref.rest_0_) | copy-start | bytes 1572868
  19.5 2.3 %copy-start.3 = (bf16[1024,2176]{1,0:T(8,128)(2,1)S(1)}, bf16[1024,2176]{1,0:T(8,128)(2,1)}, u32[]{:S(2)}) copy-start(bf16[1024,2176]{1,0:T(8,128)(2,1)} %fock_ref.1) | copy-start | bytes 13369348
  21.8 0.7 copy-start.5
  42.2 2.7 %collective-permute-start.7 = (bf16[2,1024,256]{2,1,0:T(8,128)(2,1)S(1)}, bf16[2,1024,256]{2,1,0:T(8,128)(2,1)S(1)}, u32[]{:S(2)}, u32[]{:S(2)}) collective-permute-start(bf16[2,1024,256]{2,1,0:T(8,128)(2,1)S(1)} %shard_map.74.far_ref), channel_id=1, source_target_pairs={{0,64},{64,0},{1,65},{65,1},{2,66},{66,2},{3,67},{67,3},{4,68},{68... | collective-permute-start | bytes 3145736 | tf_op jit(solution)/shard_map/ppermute | solution.py:227

commit v13 on v12

--- a/solution.py
+++ b/solution.py
@@ -193,7 +193,8 @@
     swap = ring(2, 1)
     low0 = lax.ppermute(h0, ROWS, ring(groups, 1))
     high0 = lax.ppermute(h0, ROWS, ring(groups, groups - 1))
-    ends = [(i, (i + plane) % groups) for i in range(groups) if i % plane in (0, plane - 1)]
+    far_ends = (0, plane - 1)
+    ends = [(i, (i + plane) % groups if i % plane in far_ends else i) for i in range(groups)]
     crossed = lax.ppermute(h1, ROWS, ends)
     far = lax.ppermute(panels, "xh", swap)
     near_panels = lax.ppermute(panels, "core", swap)

time: 97.6 us -> 97.7 us (level)
    ppermute x1, starting transfers between devices: 0.69 us -> 1.7 us  [on_device(): crossed = lax.ppermute(h1, ROWS, ends)]
where the time goes in v13:
time: 97.7 us; the launch traced here: 97.2 us
  blocking collectives  49.7 us (51%)
  waiting for transfers between devices  14 us (14%)
  starting transfers between devices  13.9 us (14%)
  Pallas kernels  12.8 us (13%)
  local copies, waits for them, and re-layouts  6.07 us (6%)
    all_to_all x1, blocking collectives, on_device(): terms = lax.all_to_all(terms, ('xl', 'y'), 0, 0, tiled=True)  35.1 us
    all_to_all x1, blocking collectives, on_device(): part = lax.all_to_all(part, 'z', 0, 0, tiled=True)  14.5 us
    ppermute x1, waiting for transfers between devices, on_device(): low1 = lax.ppermute(up1, ROWS, within)  8.19 us
    unnamed x12, local copies, waits for them, and re-layouts  6.07 us
    ppermute x1, starting transfers between devices, on_device(): high0 = lax.ppermute(h0, ROWS, ring(groups, groups - 1))  5.74 us
    pallas_call x2, Pallas kernels, near(): call(functools.partial(near_kernel, size, h), (like((rows, width), BF16),...  4.91 us
    ppermute x1, starting transfers between devices, on_device(): high1 = lax.ppermute(down1, ROWS, [(b, a) for a, b in within])  4.2 us
    ppermute x1, waiting for transfers between devices, on_device(): low0 = lax.ppermute(h0, ROWS, ring(groups, 1))  3.83 us
  transfers between devices with their start and end apart: 8, of which 3 were waited for; matrix products, arithmetic and copies ran while one was open for 0% of the time, Pallas kernels for 9%

profile of v13, /device:TPU:10, one launch (start us, length us, event | category | flops | bytes accessed | tf_op | source)
XLA Modules:
  0.0 97.2 jit_solution(2649495834114668848)
XLA Ops:
  0.6 2.6 %shard_map.68 = (bf16[1024,256]{1,0:T(8,128)(2,1)}, bf16[1024,256]{1,0:T(8,128)(2,1)}, bf16[2,1024,256]{2,1,0:T(8,128)(2,1)}) custom-call(s32[4,8]{1,0:T(4,128)} %bitcast.6, bf16[1024,512]{1,0:T(8,128)(2,1)} %slab_hbm.1), custom_call_target="tpu_custom_call" | custom-call | tf_op jit(solution)/shard_map/pallas_call | solution.py:178
  3.2 0.0 copy-start.4
  3.2 0.1 collective-permute-start.1
  3.3 1.7 %collective-permute-start = (bf16[1024,256]{1,0:T(8,128)(2,1)}, bf16[1024,256]{1,0:T(8,128)(2,1)S(1)}, u32[]{:S(2)}, u32[]{:S(2)}) collective-permute-start(bf16[1024,256]{1,0:T(8,128)(2,1)} %get-tuple-element.17.h1_ref.own_ref.rest_1_), channel_id=1, source_target_pairs={{0,32},{1,1},{2,2},{3,3},{4,4},{5,5},{6,6},{7,7},{8,8},{9,9},{10,1... | collective-permute-start | bytes 1572872 | tf_op jit(solution)/shard_map/ppermute | solution.py:198
  5.0 2.1 %collective-permute-start.6 = (bf16[2,1024,256]{2,1,0:T(8,128)(2,1)}, bf16[2,1024,256]{2,1,0:T(8,128)(2,1)S(1)}, u32[]{:S(2)}, u32[]{:S(2)}) collective-permute-start(bf16[2,1024,256]{2,1,0:T(8,128)(2,1)} %get-tuple-element.20), channel_id=1, source_target_pairs={{0,128},{128,0},{1,129},{129,1},{2,130},{130,2},{3,131},{131,3},{4... | collective-permute-start | bytes 3145736 | tf_op jit(solution)/shard_map/ppermute | solution.py:199
  7.1 5.7 %collective-permute-start.5 = (bf16[1024,256]{1,0:T(8,128)(2,1)}, bf16[1024,256]{1,0:T(8,128)(2,1)S(1)}, u32[]{:S(2)}, u32[]{:S(2)}) collective-permute-start(bf16[1024,256]{1,0:T(8,128)(2,1)} %get-tuple-element.16.h0_ref.rest_0_), channel_id=1, source_target_pairs={{0,63},{1,0},{2,1},{3,2},{4,3},{5,4},{6,5},{7,6},{8,7},{9,8},{10,9... | collective-permute-start | bytes 1572872 | tf_op jit(solution)/shard_map/ppermute | solution.py:195
  12.9 0.0 collective-permute-start.4
  12.9 0.0 collective-permute-done.refs_0_
  12.9 0.0 collective-permute-done.1.refs_1_.rest_2_
  12.9 1.0 %copy-done = bf16[1024,256]{1,0:T(8,128)(2,1)S(1)} copy-done((bf16[1024,256]{1,0:T(8,128)(2,1)S(1)}, bf16[1024,256]{1,0:T(8,128)(2,1)}, u32[]{:S(2)}) %copy-start) | copy-done | bytes 524312
  13.9 0.1 shard_map.71
  14.0 0.1 collective-permute-start.2
  14.1 4.2 %collective-permute-start.3 = (bf16[1024,256]{1,0:T(8,128)(2,1)S(1)}, bf16[1024,256]{1,0:T(8,128)(2,1)S(1)}, u32[]{:S(2)}, u32[]{:S(2)}) collective-permute-start(bf16[1024,256]{1,0:T(8,128)(2,1)S(1)} %get-tuple-element.22), channel_id=1, source_target_pairs={{1,0},{2,1},{3,2},{4,3},{5,4},{6,5},{7,6},{8,7},{9,8},{10,9},{11,1... | collective-permute-start | bytes 1572872 | tf_op jit(solution)/shard_map/ppermute | solution.py:213
  18.3 1.0 %copy-done.1 = bf16[1024,256]{1,0:T(8,128)(2,1)S(1)} copy-done((bf16[1024,256]{1,0:T(8,128)(2,1)S(1)}, bf16[1024,256]{1,0:T(8,128)(2,1)}, u32[]{:S(2)}) %copy-start.1) | copy-done | bytes 524312
  19.4 1.0 %copy-done.2 = bf16[1024,256]{1,0:T(8,128)(2,1)S(1)} copy-done((bf16[1024,256]{1,0:T(8,128)(2,1)S(1)}, bf16[1024,256]{1,0:T(8,128)(2,1)}, u32[]{:S(2)}) %copy-start.2) | copy-done | bytes 524312
  20.4 2.3 %copy-done.3 = bf16[1024,2176]{1,0:T(8,128)(2,1)S(1)} copy-done((bf16[1024,2176]{1,0:T(8,128)(2,1)S(1)}, bf16[1024,2176]{1,0:T(8,128)(2,1)}, u32[]{:S(2)}) %copy-start.3) | copy-done | bytes 4456472
  22.7 0.7 copy-done.5
  23.4 2.8 %shard_map.69 = (bf16[1024,2176]{1,0:T(8,128)(2,1)S(1)}, f32[1024,256]{1,0:T(8,128)S(1)}, f32[1024,256]{1,0:T(8,128)S(1)}) custom-call(s32[8,17]{1,0:T(8,128)S(1)} %copy-done.5, bf16[1024,2176]{1,0:T(8,128)(2,1)S(1)} %copy-done.3, bf16[1024,256]{1,0:T(8,128)(2,1)S(1)} %copy-done.2, bf16[1024,256]{1,0:T(8,128)(2,1)S(1)} %copy-done.1), custom_call_target="tpu_custom_call" | custom-call | flops 1073741824 | bytes 8912896 | tf_op jit(solution)/shard_map/pallas_call | solution.py:201
  26.2 0.0 collective-permute-done.5.high_ref
  26.2 3.8 %collective-permute-done.4.low_ref = bf16[1024,256]{1,0:T(8,128)(2,1)S(1)} collective-permute-done((bf16[1024,256]{1,0:T(8,128)(2,1)}, bf16[1024,256]{1,0:T(8,128)(2,1)S(1)}, u32[]{:S(2)}, u32[]{:S(2)}) %collective-permute-start.4) | collective-permute-done | bytes 524320 | tf_op jit(solution)/shard_map/ppermute | solution.py:194
  30.0 2.0 %shard_map.72 = (bf16[1024,256]{1,0:T(8,128)(2,1)S(1)}, bf16[256,1024]{1,0:T(8,128)(2,1)S(1)}, bf16[4,256,256]{2,1,0:T(8,128)(2,1)S(1)}) custom-call(s32[4,8]{1,0:T(4,128)S(1)} %bitcast.4, bf16[1024,2176]{1,0:T(8,128)(2,1)S(1)} %get-tuple-element.18.held_ref, f32[1024,256]{1,0:T(8,128)S(1)} %get-tuple-element.23.mid_ref, ...), custom_call_target="tpu_custom_call" | custom-call | flops 1140850688 | bytes 4194304 | tf_op jit(solution)/shard_map/pallas_call | solution.py:217
  32.0 8.2 %collective-permute-done.2.low_ref = bf16[1024,256]{1,0:T(8,128)(2,1)S(1)} collective-permute-done((bf16[1024,256]{1,0:T(8,128)(2,1)S(1)}, bf16[1024,256]{1,0:T(8,128)(2,1)S(1)}, u32[]{:S(2)}, u32[]{:S(2)}) %collective-permute-start.2) | collective-permute-done | bytes 524320 | tf_op jit(solution)/shard_map/ppermute | solution.py:212
  40.2 2.9 %shard_map.73 = (bf16[1024,512]{1,0:T(8,128)(2,1)}, bf16[256,1024]{1,0:T(8,128)(2,1)S(1)}, bf16[4,256,256]{2,1,0:T(8,128)(2,1)S(1)}) custom-call(s32[4,8]{1,0:T(4,128)S(1)} %bitcast.5, bf16[1024,2176]{1,0:T(8,128)(2,1)S(1)} %get-tuple-element.18.held_ref, f32[1024,256]{1,0:T(8,128)S(1)} %get-tuple-element.19.mid_ref, ...), custom_call_target="tpu_custom_call" | custom-call | flops 1140850688 | bytes 4194304 | tf_op jit(solution)/shard_map/pallas_call | solution.py:217
  43.1 0.0 collective-permute-done.6.refs_0_
  43.1 0.0 collective-permute-start.7
  43.1 0.7 shard_map.75.far_ref
  43.8 1.9 %collective-permute-done.7.both_ref = bf16[2,1024,256]{2,1,0:T(8,128)(2,1)S(1)} collective-permute-done((bf16[2,1024,256]{2,1,0:T(8,128)(2,1)S(1)}, bf16[2,1024,256]{2,1,0:T(8,128)(2,1)S(1)}, u32[]{:S(2)}, u32[]{:S(2)}) %collective-permute-start.7) | collective-permute-done | bytes 1048608 | tf_op jit(solution)/shard_map/ppermute | solution.py:228
  45.8 0.7 shard_map.76
  46.5 35.1 %all_to_all.10.in_ref = bf16[8,512,256]{2,1,0:T(8,128)(2,1)S(1)} all-to-all(bf16[8,512,256]{2,1,0:T(8,128)(2,1)S(1)} %shard_map.76), channel_id=1, replica_groups=mesh['xh'=2,'core'=2,'xl'=2,'y'=4,'z'=8] {'xl','y'}, dimensions={0} | all-to-all | bytes 4194304 | tf_op jit(solution)/shard_map/all_to_all | solution.py:243
  81.7 0.3 shard_map.77
  82.0 14.5 %all_to_all.11.in_ref = bf16[8,32,512]{2,1,0:T(8,128)(2,1)S(1)} all-to-all(bf16[8,32,512]{2,1,0:T(8,128)(2,1)S(1)} %bitcast.3), channel_id=1, replica_groups=mesh['xh'=2,'core'=2,'xl'=2,'y'=4,'z'=8] {'z'}, dimensions={0} | all-to-all | bytes 524288 | tf_op jit(solution)/shard_map/all_to_all | solution.py:246
  96.5 0.7 shard_map.78
  (9 shorter events, 0.0 us)
Async XLA Ops:
  3.2 26.8 %copy-start.4 = (s32[8,4]{0,1:T(4,128)S(1)}, s32[8,4]{0,1:T(4,128)}, u32[]{:S(2)}) copy-start(s32[8,4]{0,1:T(4,128)} %param.9) | copy-start | bytes 388
  3.2 9.7 %collective-permute-start.1 = (bf16[2,1024,256]{2,1,0:T(8,128)(2,1)}, bf16[2,1024,256]{2,1,0:T(8,128)(2,1)S(1)}, u32[]{:S(2)}, u32[]{:S(2)}) collective-permute-start(bf16[2,1024,256]{2,1,0:T(8,128)(2,1)} %get-tuple-element.20), channel_id=1, source_target_pairs={{0,64},{64,0},{1,65},{65,1},{2,66},{66,2},{3,67},{67,3},{4,68},{68... | collective-permute-start | bytes 3145736 | tf_op jit(solution)/shard_map/ppermute | solution.py:200
  3.3 9.6 %collective-permute-start = (bf16[1024,256]{1,0:T(8,128)(2,1)}, bf16[1024,256]{1,0:T(8,128)(2,1)S(1)}, u32[]{:S(2)}, u32[]{:S(2)}) collective-permute-start(bf16[1024,256]{1,0:T(8,128)(2,1)} %get-tuple-element.17.h1_ref.own_ref.rest_1_), channel_id=1, source_target_pairs={{0,32},{1,1},{2,2},{3,3},{4,4},{5,5},{6,6},{7,7},{8,8},{9,9},{10,1... | collective-permute-start | bytes 1572872 | tf_op jit(solution)/shard_map/ppermute | solution.py:198
  5.0 38.1 %collective-permute-start.6 = (bf16[2,1024,256]{2,1,0:T(8,128)(2,1)}, bf16[2,1024,256]{2,1,0:T(8,128)(2,1)S(1)}, u32[]{:S(2)}, u32[]{:S(2)}) collective-permute-start(bf16[2,1024,256]{2,1,0:T(8,128)(2,1)} %get-tuple-element.20), channel_id=1, source_target_pairs={{0,128},{128,0},{1,129},{129,1},{2,130},{130,2},{3,131},{131,3},{4... | collective-permute-start | bytes 3145736 | tf_op jit(solution)/shard_map/ppermute | solution.py:199
  7.1 19.0 %collective-permute-start.5 = (bf16[1024,256]{1,0:T(8,128)(2,1)}, bf16[1024,256]{1,0:T(8,128)(2,1)S(1)}, u32[]{:S(2)}, u32[]{:S(2)}) collective-permute-start(bf16[1024,256]{1,0:T(8,128)(2,1)} %get-tuple-element.16.h0_ref.rest_0_), channel_id=1, source_target_pairs={{0,63},{1,0},{2,1},{3,2},{4,3},{5,4},{6,5},{7,6},{8,7},{9,8},{10,9... | collective-permute-start | bytes 1572872 | tf_op jit(solution)/shard_map/ppermute | solution.py:195
  12.9 17.1 %collective-permute-start.4 = (bf16[1024,256]{1,0:T(8,128)(2,1)}, bf16[1024,256]{1,0:T(8,128)(2,1)S(1)}, u32[]{:S(2)}, u32[]{:S(2)}) collective-permute-start(bf16[1024,256]{1,0:T(8,128)(2,1)} %get-tuple-element.16.h0_ref.rest_0_), channel_id=1, source_target_pairs={{0,1},{1,2},{2,3},{3,4},{4,5},{5,6},{6,7},{7,8},{8,9},{9,10},{10,1... | collective-permute-start | bytes 1572872 | tf_op jit(solution)/shard_map/ppermute | solution.py:194
  12.9 1.0 %copy-start = (bf16[1024,256]{1,0:T(8,128)(2,1)S(1)}, bf16[1024,256]{1,0:T(8,128)(2,1)}, u32[]{:S(2)}) copy-start(bf16[1024,256]{1,0:T(8,128)(2,1)} %get-tuple-element.17.h1_ref.own_ref.rest_1_) | copy-start | bytes 1572868
  14.0 26.2 %collective-permute-start.2 = (bf16[1024,256]{1,0:T(8,128)(2,1)S(1)}, bf16[1024,256]{1,0:T(8,128)(2,1)S(1)}, u32[]{:S(2)}, u32[]{:S(2)}) collective-permute-start(bf16[1024,256]{1,0:T(8,128)(2,1)S(1)} %get-tuple-element.21), channel_id=1, source_target_pairs={{0,1},{1,2},{2,3},{3,4},{4,5},{5,6},{6,7},{7,8},{8,9},{9,10},{10,1... | collective-permute-start | bytes 1572872 | tf_op jit(solution)/shard_map/ppermute | solution.py:212
  14.1 26.1 %collective-permute-start.3 = (bf16[1024,256]{1,0:T(8,128)(2,1)S(1)}, bf16[1024,256]{1,0:T(8,128)(2,1)S(1)}, u32[]{:S(2)}, u32[]{:S(2)}) collective-permute-start(bf16[1024,256]{1,0:T(8,128)(2,1)S(1)} %get-tuple-element.22), channel_id=1, source_target_pairs={{1,0},{2,1},{3,2},{4,3},{5,4},{6,5},{7,6},{8,7},{9,8},{10,9},{11,1... | collective-permute-start | bytes 1572872 | tf_op jit(solution)/shard_map/ppermute | solution.py:213
  18.3 1.0 %copy-start.1 = (bf16[1024,256]{1,0:T(8,128)(2,1)S(1)}, bf16[1024,256]{1,0:T(8,128)(2,1)}, u32[]{:S(2)}) copy-start(bf16[1024,256]{1,0:T(8,128)(2,1)} %get-tuple-element.17.h1_ref.own_ref.rest_1_) | copy-start | bytes 1572868
  19.4 1.0 %copy-start.2 = (bf16[1024,256]{1,0:T(8,128)(2,1)S(1)}, bf16[1024,256]{1,0:T(8,128)(2,1)}, u32[]{:S(2)}) copy-start(bf16[1024,256]{1,0:T(8,128)(2,1)} %get-tuple-element.16.h0_ref.rest_0_) | copy-start | bytes 1572868
  20.4 2.3 %copy-start.3 = (bf16[1024,2176]{1,0:T(8,128)(2,1)S(1)}, bf16[1024,2176]{1,0:T(8,128)(2,1)}, u32[]{:S(2)}) copy-start(bf16[1024,2176]{1,0:T(8,128)(2,1)} %fock_ref.1) | copy-start | bytes 13369348
  22.7 0.7 copy-start.5
  43.1 2.7 %collective-permute-start.7 = (bf16[2,1024,256]{2,1,0:T(8,128)(2,1)S(1)}, bf16[2,1024,256]{2,1,0:T(8,128)(2,1)S(1)}, u32[]{:S(2)}, u32[]{:S(2)}) collective-permute-start(bf16[2,1024,256]{2,1,0:T(8,128)(2,1)S(1)} %shard_map.74.far_ref), channel_id=1, source_target_pairs={{0,64},{64,0},{1,65},{65,1},{2,66},{66,2},{3,67},{67,3},{4,68},{68... | collective-permute-start | bytes 3145736 | tf_op jit(solution)/shard_map/ppermute | solution.py:228

commit v14 on v12

--- a/solution.py
+++ b/solution.py
@@ -38,8 +38,10 @@
     mask_load = pltpu.make_async_copy(mask_hbm, mask_ref, mask_sem)
     mask_load.start()
     half = panels // 2
-    at = [pl.ds(i * size, size) for i in range(blocks)]
-    loads = [pltpu.make_async_copy(slab_hbm.at[at[i]], loaded.at[at[i]], in_sems.at[i]) for i in range(blocks)]
+    pieces = in_sems.shape[0]
+    span = blocks // pieces
+    at = [pl.ds(i * span * size, span * size) for i in range(pieces)]
+    loads = [pltpu.make_async_copy(slab_hbm.at[at[i]], loaded.at[at[i]], in_sems.at[i]) for i in range(pieces)]
     for load in loads:
         load.start()
     mask_load.wait()
@@ -47,9 +49,11 @@
     for i, load in enumerate(loads):
         load.wait()
         for j in range(panels):
-            tile = loaded[at[i], pl.ds(j * size, size)]
-            tile = jnp.where(mask_ref[j, i] != 0, tile, jnp.zeros_like(tile))
-            kept[j // half, at[i], pl.ds((j % half) * size, size)] = tile
+            for b in range(i * span, (i + 1) * span):
+                rows = pl.ds(b * size, size)
+                tile = loaded[rows, pl.ds(j * size, size)]
+                tile = jnp.where(mask_ref[j, b] != 0, tile, jnp.zeros_like(tile))
+                kept[j // half, rows, pl.ds((j % half) * size, size)] = tile
         for h, ref in enumerate((h0_hbm, h1_hbm)):
             stores.append(pltpu.make_async_copy(kept.at[h, at[i]], ref.at[at[i]], out_sems.at[i, 2 * h]))
             stores.append(pltpu.make_async_copy(kept.at[h, at[i]], both_hbm.at[h, at[i]], out_sems.at[i, 2 * h + 1]))
@@ -184,8 +188,8 @@
             pltpu.VMEM((rows, columns), BF16),
             pltpu.VMEM((2, rows, half), BF16),
             pltpu.SemaphoreType.DMA,
-            pltpu.SemaphoreType.DMA((blocks,)),
-            pltpu.SemaphoreType.DMA((blocks, 4)),
+            pltpu.SemaphoreType.DMA((blocks // 2,)),
+            pltpu.SemaphoreType.DMA((blocks // 2, 4)),
         ],
         limit=60 * MIB,
         place=HBM,

time: 97.6 us -> 97.6 us (level)
  no operation moved by 1% of the time
where the time goes in v14:
time: 97.6 us; the launch traced here: 97.1 us
  blocking collectives  50.6 us (52%)
  waiting for transfers between devices  14 us (14%)
  starting transfers between devices  13 us (13%)
  Pallas kernels  12.7 us (13%)
  local copies, waits for them, and re-layouts  6.07 us (6%)
    all_to_all x1, blocking collectives, on_device(): terms = lax.all_to_all(terms, ('xl', 'y'), 0, 0, tiled=True)  36.1 us
    all_to_all x1, blocking collectives, on_device(): part = lax.all_to_all(part, 'z', 0, 0, tiled=True)  14.5 us
    ppermute x1, waiting for transfers between devices, on_device(): low1 = lax.ppermute(up1, ROWS, within)  8.19 us
    unnamed x12, local copies, waits for them, and re-layouts  6.07 us
    ppermute x1, starting transfers between devices, on_device(): high0 = lax.ppermute(h0, ROWS, ring(groups, groups - 1))  5.74 us
    pallas_call x2, Pallas kernels, near(): call(functools.partial(near_kernel, size, h), (like((rows, width), BF16),...  4.91 us
    ppermute x1, starting transfers between devices, on_device(): high1 = lax.ppermute(down1, ROWS, [(b, a) for a, b in within])  4.2 us
    ppermute x1, waiting for transfers between devices, on_device(): low0 = lax.ppermute(h0, ROWS, ring(groups, 1))  3.83 us
  transfers between devices with their start and end apart: 8, of which 3 were waited for; matrix products, arithmetic and copies ran while one was open for 0% of the time, Pallas kernels for 9%

profile of v14, /device:TPU:10, one launch (start us, length us, event | category | flops | bytes accessed | tf_op | source)
XLA Modules:
  0.0 97.1 jit_solution(11688302033036965544)
XLA Ops:
  0.6 2.5 %shard_map.68 = (bf16[1024,256]{1,0:T(8,128)(2,1)}, bf16[1024,256]{1,0:T(8,128)(2,1)}, bf16[2,1024,256]{2,1,0:T(8,128)(2,1)}) custom-call(s32[4,8]{1,0:T(4,128)} %bitcast.6, bf16[1024,512]{1,0:T(8,128)(2,1)} %slab_hbm.1), custom_call_target="tpu_custom_call" | custom-call | tf_op jit(solution)/shard_map/pallas_call | solution.py:182
  3.1 0.0 copy-start.4
  3.1 0.1 collective-permute-start.1
  3.2 0.7 collective-permute-start
  3.9 2.2 %collective-permute-start.6 = (bf16[2,1024,256]{2,1,0:T(8,128)(2,1)}, bf16[2,1024,256]{2,1,0:T(8,128)(2,1)S(1)}, u32[]{:S(2)}, u32[]{:S(2)}) collective-permute-start(bf16[2,1024,256]{2,1,0:T(8,128)(2,1)} %get-tuple-element.20), channel_id=1, source_target_pairs={{0,128},{128,0},{1,129},{129,1},{2,130},{130,2},{3,131},{131,3},{4... | collective-permute-start | bytes 3145736 | tf_op jit(solution)/shard_map/ppermute | solution.py:202
  6.2 5.7 %collective-permute-start.5 = (bf16[1024,256]{1,0:T(8,128)(2,1)}, bf16[1024,256]{1,0:T(8,128)(2,1)S(1)}, u32[]{:S(2)}, u32[]{:S(2)}) collective-permute-start(bf16[1024,256]{1,0:T(8,128)(2,1)} %get-tuple-element.16.h0_ref.rest_0_), channel_id=1, source_target_pairs={{0,63},{1,0},{2,1},{3,2},{4,3},{5,4},{6,5},{7,6},{8,7},{9,8},{10,9... | collective-permute-start | bytes 1572872 | tf_op jit(solution)/shard_map/ppermute | solution.py:199
  11.9 0.0 collective-permute-start.4
  11.9 0.0 collective-permute-done.refs_0_
  11.9 0.0 collective-permute-done.1.refs_1_.rest_2_
  11.9 1.0 %copy-done = bf16[1024,256]{1,0:T(8,128)(2,1)S(1)} copy-done((bf16[1024,256]{1,0:T(8,128)(2,1)S(1)}, bf16[1024,256]{1,0:T(8,128)(2,1)}, u32[]{:S(2)}) %copy-start) | copy-done | bytes 524312
  13.0 0.1 shard_map.71
  13.0 0.1 collective-permute-start.2
  13.1 4.2 %collective-permute-start.3 = (bf16[1024,256]{1,0:T(8,128)(2,1)S(1)}, bf16[1024,256]{1,0:T(8,128)(2,1)S(1)}, u32[]{:S(2)}, u32[]{:S(2)}) collective-permute-start(bf16[1024,256]{1,0:T(8,128)(2,1)S(1)} %get-tuple-element.22), channel_id=1, source_target_pairs={{1,0},{2,1},{3,2},{4,3},{5,4},{6,5},{7,6},{8,7},{9,8},{10,9},{11,1... | collective-permute-start | bytes 1572872 | tf_op jit(solution)/shard_map/ppermute | solution.py:216
  17.3 1.0 %copy-done.1 = bf16[1024,256]{1,0:T(8,128)(2,1)S(1)} copy-done((bf16[1024,256]{1,0:T(8,128)(2,1)S(1)}, bf16[1024,256]{1,0:T(8,128)(2,1)}, u32[]{:S(2)}) %copy-start.1) | copy-done | bytes 524312
  18.4 1.0 %copy-done.2 = bf16[1024,256]{1,0:T(8,128)(2,1)S(1)} copy-done((bf16[1024,256]{1,0:T(8,128)(2,1)S(1)}, bf16[1024,256]{1,0:T(8,128)(2,1)}, u32[]{:S(2)}) %copy-start.2) | copy-done | bytes 524312
  19.4 2.3 %copy-done.3 = bf16[1024,2176]{1,0:T(8,128)(2,1)S(1)} copy-done((bf16[1024,2176]{1,0:T(8,128)(2,1)S(1)}, bf16[1024,2176]{1,0:T(8,128)(2,1)}, u32[]{:S(2)}) %copy-start.3) | copy-done | bytes 4456472
  21.7 0.7 copy-done.5
  22.4 2.8 %shard_map.69 = (bf16[1024,2176]{1,0:T(8,128)(2,1)S(1)}, f32[1024,256]{1,0:T(8,128)S(1)}, f32[1024,256]{1,0:T(8,128)S(1)}) custom-call(s32[8,17]{1,0:T(8,128)S(1)} %copy-done.5, bf16[1024,2176]{1,0:T(8,128)(2,1)S(1)} %copy-done.3, bf16[1024,256]{1,0:T(8,128)(2,1)S(1)} %copy-done.2, bf16[1024,256]{1,0:T(8,128)(2,1)S(1)} %copy-done.1), custom_call_target="tpu_custom_call" | custom-call | flops 1073741824 | bytes 8912896 | tf_op jit(solution)/shard_map/pallas_call | solution.py:204
  25.2 0.0 collective-permute-done.5.high_ref
  25.2 3.8 %collective-permute-done.4.low_ref = bf16[1024,256]{1,0:T(8,128)(2,1)S(1)} collective-permute-done((bf16[1024,256]{1,0:T(8,128)(2,1)}, bf16[1024,256]{1,0:T(8,128)(2,1)S(1)}, u32[]{:S(2)}, u32[]{:S(2)}) %collective-permute-start.4) | collective-permute-done | bytes 524320 | tf_op jit(solution)/shard_map/ppermute | solution.py:198
  29.0 2.0 %shard_map.72 = (bf16[1024,256]{1,0:T(8,128)(2,1)S(1)}, bf16[256,1024]{1,0:T(8,128)(2,1)S(1)}, bf16[4,256,256]{2,1,0:T(8,128)(2,1)S(1)}) custom-call(s32[4,8]{1,0:T(4,128)S(1)} %bitcast.4, bf16[1024,2176]{1,0:T(8,128)(2,1)S(1)} %get-tuple-element.18.held_ref, f32[1024,256]{1,0:T(8,128)S(1)} %get-tuple-element.23.mid_ref, ...), custom_call_target="tpu_custom_call" | custom-call | flops 1140850688 | bytes 4194304 | tf_op jit(solution)/shard_map/pallas_call | solution.py:220
  31.0 8.2 %collective-permute-done.2.low_ref = bf16[1024,256]{1,0:T(8,128)(2,1)S(1)} collective-permute-done((bf16[1024,256]{1,0:T(8,128)(2,1)S(1)}, bf16[1024,256]{1,0:T(8,128)(2,1)S(1)}, u32[]{:S(2)}, u32[]{:S(2)}) %collective-permute-start.2) | collective-permute-done | bytes 524320 | tf_op jit(solution)/shard_map/ppermute | solution.py:215
  39.2 0.0 collective-permute-done.3.high_ref
  39.2 2.9 %shard_map.73 = (bf16[1024,512]{1,0:T(8,128)(2,1)}, bf16[256,1024]{1,0:T(8,128)(2,1)S(1)}, bf16[4,256,256]{2,1,0:T(8,128)(2,1)S(1)}) custom-call(s32[4,8]{1,0:T(4,128)S(1)} %bitcast.5, bf16[1024,2176]{1,0:T(8,128)(2,1)S(1)} %get-tuple-element.18.held_ref, f32[1024,256]{1,0:T(8,128)S(1)} %get-tuple-element.19.mid_ref, ...), custom_call_target="tpu_custom_call" | custom-call | flops 1140850688 | bytes 4194304 | tf_op jit(solution)/shard_map/pallas_call | solution.py:220
  42.1 0.0 collective-permute-start.7
  42.1 0.7 shard_map.75.far_ref
  42.9 1.9 %collective-permute-done.7.both_ref = bf16[2,1024,256]{2,1,0:T(8,128)(2,1)S(1)} collective-permute-done((bf16[2,1024,256]{2,1,0:T(8,128)(2,1)S(1)}, bf16[2,1024,256]{2,1,0:T(8,128)(2,1)S(1)}, u32[]{:S(2)}, u32[]{:S(2)}) %collective-permute-start.7) | collective-permute-done | bytes 1048608 | tf_op jit(solution)/shard_map/ppermute | solution.py:231
  44.8 0.7 shard_map.76
  45.5 36.1 %all_to_all.10.in_ref = bf16[8,512,256]{2,1,0:T(8,128)(2,1)S(1)} all-to-all(bf16[8,512,256]{2,1,0:T(8,128)(2,1)S(1)} %shard_map.76), channel_id=1, replica_groups=mesh['xh'=2,'core'=2,'xl'=2,'y'=4,'z'=8] {'xl','y'}, dimensions={0} | all-to-all | bytes 4194304 | tf_op jit(solution)/shard_map/all_to_all | solution.py:246
  81.6 0.3 shard_map.77
  81.9 14.5 %all_to_all.11.in_ref = bf16[8,32,512]{2,1,0:T(8,128)(2,1)S(1)} all-to-all(bf16[8,32,512]{2,1,0:T(8,128)(2,1)S(1)} %bitcast.3), channel_id=1, replica_groups=mesh['xh'=2,'core'=2,'xl'=2,'y'=4,'z'=8] {'z'}, dimensions={0} | all-to-all | bytes 524288 | tf_op jit(solution)/shard_map/all_to_all | solution.py:249
  96.5 0.7 shard_map.78
  (9 shorter events, 0.0 us)
Async XLA Ops:
  3.1 25.9 %copy-start.4 = (s32[8,4]{0,1:T(4,128)S(1)}, s32[8,4]{0,1:T(4,128)}, u32[]{:S(2)}) copy-start(s32[8,4]{0,1:T(4,128)} %param.9) | copy-start | bytes 388
  3.1 8.8 %collective-permute-start.1 = (bf16[2,1024,256]{2,1,0:T(8,128)(2,1)}, bf16[2,1024,256]{2,1,0:T(8,128)(2,1)S(1)}, u32[]{:S(2)}, u32[]{:S(2)}) collective-permute-start(bf16[2,1024,256]{2,1,0:T(8,128)(2,1)} %get-tuple-element.20), channel_id=1, source_target_pairs={{0,64},{64,0},{1,65},{65,1},{2,66},{66,2},{3,67},{67,3},{4,68},{68... | collective-permute-start | bytes 3145736 | tf_op jit(solution)/shard_map/ppermute | solution.py:203
  3.2 8.7 %collective-permute-start = (bf16[1024,256]{1,0:T(8,128)(2,1)}, bf16[1024,256]{1,0:T(8,128)(2,1)S(1)}, u32[]{:S(2)}, u32[]{:S(2)}) collective-permute-start(bf16[1024,256]{1,0:T(8,128)(2,1)} %get-tuple-element.17.h1_ref.own_ref.rest_1_), channel_id=1, source_target_pairs={{0,32},{31,63},{32,0},{63,31},{64,96},{95,127},{96,64},{127,95},{1... | collective-permute-start | bytes 1572872 | tf_op jit(solution)/shard_map/ppermute | solution.py:201
  3.9 38.2 %collective-permute-start.6 = (bf16[2,1024,256]{2,1,0:T(8,128)(2,1)}, bf16[2,1024,256]{2,1,0:T(8,128)(2,1)S(1)}, u32[]{:S(2)}, u32[]{:S(2)}) collective-permute-start(bf16[2,1024,256]{2,1,0:T(8,128)(2,1)} %get-tuple-element.20), channel_id=1, source_target_pairs={{0,128},{128,0},{1,129},{129,1},{2,130},{130,2},{3,131},{131,3},{4... | collective-permute-start | bytes 3145736 | tf_op jit(solution)/shard_map/ppermute | solution.py:202
  6.2 19.0 %collective-permute-start.5 = (bf16[1024,256]{1,0:T(8,128)(2,1)}, bf16[1024,256]{1,0:T(8,128)(2,1)S(1)}, u32[]{:S(2)}, u32[]{:S(2)}) collective-permute-start(bf16[1024,256]{1,0:T(8,128)(2,1)} %get-tuple-element.16.h0_ref.rest_0_), channel_id=1, source_target_pairs={{0,63},{1,0},{2,1},{3,2},{4,3},{5,4},{6,5},{7,6},{8,7},{9,8},{10,9... | collective-permute-start | bytes 1572872 | tf_op jit(solution)/shard_map/ppermute | solution.py:199
  11.9 17.1 %collective-permute-start.4 = (bf16[1024,256]{1,0:T(8,128)(2,1)}, bf16[1024,256]{1,0:T(8,128)(2,1)S(1)}, u32[]{:S(2)}, u32[]{:S(2)}) collective-permute-start(bf16[1024,256]{1,0:T(8,128)(2,1)} %get-tuple-element.16.h0_ref.rest_0_), channel_id=1, source_target_pairs={{0,1},{1,2},{2,3},{3,4},{4,5},{5,6},{6,7},{7,8},{8,9},{9,10},{10,1... | collective-permute-start | bytes 1572872 | tf_op jit(solution)/shard_map/ppermute | solution.py:198
  11.9 1.0 %copy-start = (bf16[1024,256]{1,0:T(8,128)(2,1)S(1)}, bf16[1024,256]{1,0:T(8,128)(2,1)}, u32[]{:S(2)}) copy-start(bf16[1024,256]{1,0:T(8,128)(2,1)} %get-tuple-element.17.h1_ref.own_ref.rest_1_) | copy-start | bytes 1572868
  13.0 26.2 %collective-permute-start.2 = (bf16[1024,256]{1,0:T(8,128)(2,1)S(1)}, bf16[1024,256]{1,0:T(8,128)(2,1)S(1)}, u32[]{:S(2)}, u32[]{:S(2)}) collective-permute-start(bf16[1024,256]{1,0:T(8,128)(2,1)S(1)} %get-tuple-element.21), channel_id=1, source_target_pairs={{0,1},{1,2},{2,3},{3,4},{4,5},{5,6},{6,7},{7,8},{8,9},{9,10},{10,1... | collective-permute-start | bytes 1572872 | tf_op jit(solution)/shard_map/ppermute | solution.py:215
  13.1 26.1 %collective-permute-start.3 = (bf16[1024,256]{1,0:T(8,128)(2,1)S(1)}, bf16[1024,256]{1,0:T(8,128)(2,1)S(1)}, u32[]{:S(2)}, u32[]{:S(2)}) collective-permute-start(bf16[1024,256]{1,0:T(8,128)(2,1)S(1)} %get-tuple-element.22), channel_id=1, source_target_pairs={{1,0},{2,1},{3,2},{4,3},{5,4},{6,5},{7,6},{8,7},{9,8},{10,9},{11,1... | collective-permute-start | bytes 1572872 | tf_op jit(solution)/shard_map/ppermute | solution.py:216
  17.3 1.0 %copy-start.1 = (bf16[1024,256]{1,0:T(8,128)(2,1)S(1)}, bf16[1024,256]{1,0:T(8,128)(2,1)}, u32[]{:S(2)}) copy-start(bf16[1024,256]{1,0:T(8,128)(2,1)} %get-tuple-element.17.h1_ref.own_ref.rest_1_) | copy-start | bytes 1572868
  18.4 1.0 %copy-start.2 = (bf16[1024,256]{1,0:T(8,128)(2,1)S(1)}, bf16[1024,256]{1,0:T(8,128)(2,1)}, u32[]{:S(2)}) copy-start(bf16[1024,256]{1,0:T(8,128)(2,1)} %get-tuple-element.16.h0_ref.rest_0_) | copy-start | bytes 1572868
  19.4 2.3 %copy-start.3 = (bf16[1024,2176]{1,0:T(8,128)(2,1)S(1)}, bf16[1024,2176]{1,0:T(8,128)(2,1)}, u32[]{:S(2)}) copy-start(bf16[1024,2176]{1,0:T(8,128)(2,1)} %fock_ref.1) | copy-start | bytes 13369348
  21.7 0.7 copy-start.5
  42.1 2.7 %collective-permute-start.7 = (bf16[2,1024,256]{2,1,0:T(8,128)(2,1)S(1)}, bf16[2,1024,256]{2,1,0:T(8,128)(2,1)S(1)}, u32[]{:S(2)}, u32[]{:S(2)}) collective-permute-start(bf16[2,1024,256]{2,1,0:T(8,128)(2,1)S(1)} %shard_map.74.far_ref), channel_id=1, source_target_pairs={{0,64},{64,0},{1,65},{65,1},{2,66},{66,2},{3,67},{67,3},{4,68},{68... | collective-permute-start | bytes 3145736 | tf_op jit(solution)/shard_map/ppermute | solution.py:231
